TPU v7x, 128 devices: a whole 4x4x4 slice. The times are simulated.
128 devices in a mesh: dom: 32 (over x, z, core), bal: 4 (over y).
Axes of the slice: x: 4, y: 4, z: 4, core: 2. Of those that a mesh axis runs over, the one named last changes fastest.
Arguments:
- right_side: float32 [1024, 64, 128], P(('dom', 'bal')), may hold values from -100 to 100
- a_tiles: bfloat16 [1024, 5, 128, 128], P(('dom', 'bal')), may hold values from -4 to 4
- a_cols: int32 [1024, 5], P(('dom', 'bal')), may hold values from 0 to 1023, as said below
- m_tiles: bfloat16 [13312, 128, 128], P(('dom', 'bal')), may hold values from -2 to 2
- m_rows: int32 [13312], P(('dom', 'bal')), may hold values from 0 to 1023, as said below
- m_cols: int32 [13312], P(('dom', 'bal')), may hold values from 0 to 1023, as said below
- m_count: int32 [128], P(('dom', 'bal')), may hold values from 24 to 104, as said below
Outputs:
- solution: float32 [1024, 64, 128], P(('dom', 'bal'))
- residual: float32 [1024, 64, 128], P(('dom', 'bal'))
- basis: float32 [1024, 64, 128], P(('dom', 'bal'))
- shadow: float32 [1024, 64, 128], P(('dom', 'bal'))
Inputs may be any that keep to these rules, and one draw needn't show every extreme that they name: a_cols[r, j] differs from r by at most 16, and every block row has a tile exactly 16 away. `m_rows`: the slots i * 104 to (i + 1) * 104 - 1 name block rows i * 8 to (i + 1) * 8 - 1, the rows of device i in the order of dom then bal. m_cols[s] differs from m_rows[s] by at most 32; on every device a live slot reaches exactly 32. The live slots of device i are its first m_count[i]; in every draw some device has all 104 live.
All inputs are finite; a program needn't handle non-finite values.
Results may differ from a plain program's by a relative error of at most 0.014.
Values may be sent and summed in bfloat16 or wider, within the bound.
No kernel may reach another device: no remote copies, remote signals or barrier semaphores. Data moves between devices by JAX's collectives and lax.ppermute only.
A program may use at most 64 MiB of HBM per device.

v0:
```python
import jax
import jax.numpy as jnp
from jax import lax
from jax.experimental import pallas as pl
from jax.experimental.pallas import tpu as pltpu
from jax.sharding import PartitionSpec as P

ITERS = 2
BR = 8
TILE = 128
K = 64
NT = (((1,), (1,)), ((), ()))
NN = (((1,), (0,)), ((), ()))
TN = (((0,), (0,)), ((), ()))
F32 = jnp.float32
BF16 = jnp.bfloat16
DOM, BAL = "dom", "bal"
UNROLL = 8


def hdot(a, b, dims=NN):
    return lax.dot_general(a, b, dims, precision=lax.Precision.HIGHEST, preferred_element_type=F32)


def bdot(a, b, dims):
    return lax.dot_general(a, b, dims, preferred_element_type=F32)


def swap(value, axis, size, distance):
    return lax.ppermute(value, axis, [(i, i ^ distance) for i in range(size)])


def swap_y(value, distance):
    return swap(value, BAL, lax.axis_size(BAL), distance)


def swap_core(value):
    return swap(value, DOM, lax.axis_size(DOM), 1)


def swap_next(value):
    size = lax.axis_size(DOM)
    route = []
    for i in range(1, size - 1, 2):
        route += [(i, i + 1), (i + 1, i)]
    return lax.ppermute(value, DOM, route)


def reduce_all(value):
    size = lax.axis_size(DOM)
    value = value + swap(value, DOM, size, 1)
    parts = [swap_y(value, k) for k in (1, 2, 3)]
    value = (value + parts[0]) + (parts[1] + parts[2])
    for unit in (2, 8):
        parts = [swap(value, DOM, size, k * unit) for k in (1, 2, 3)]
        value = (value + parts[0]) + (parts[1] + parts[2])
    return value


VM = pl.BlockSpec(memory_space=pltpu.VMEM)
SM = pl.BlockSpec(memory_space=pltpu.SMEM)


def call(body, name, specs, outs, scratch, args, flops=0, nbytes=0, final=False):
    args = [pltpu.with_memory_space_constraint(a, pltpu.VMEM) if s is VM else a for s, a in zip(specs, args)]
    return pl.pallas_call(
        body,
        name=name,
        in_specs=specs,
        out_specs=tuple(VM for _ in outs),
        out_shape=tuple(jax.ShapeDtypeStruct(s, d) if final else pltpu.VMEM(s, d) for s, d in outs),
        scratch_shapes=scratch,
        compiler_params=pltpu.CompilerParams(vmem_limit_bytes=14 * 2**20),
        cost_estimate=pl.CostEstimate(flops=flops, bytes_accessed=nbytes, transcendentals=0),
    )(*args)


def inverse_factors(mats, out_ref):
    nb = K // 8
    row = lax.broadcasted_iota(jnp.int32, (8, K), 0)
    col = lax.broadcasted_iota(jnp.int32, (8, K), 1)
    work = []
    for g in mats:
        left = [g[8 * i : 8 * i + 8, :] for i in range(nb)]
        right = [jnp.where(row + 8 * i == col, 1.0, 0.0).astype(F32) for i in range(nb)]
        work.append((left, right))
    for k in range(0, K, 2):
        kb, kr = divmod(k, 8)
        for m, (left, right) in enumerate(work):
            r0, r1 = left[kb][kr : kr + 1, :], left[kb][kr + 1 : kr + 2, :]
            q0, q1 = right[kb][kr : kr + 1, :], right[kb][kr + 1 : kr + 2, :]
            a = jnp.broadcast_to(r0[:, k : k + 1], (1, K))
            b = jnp.broadcast_to(r0[:, k + 1 : k + 2], (1, K))
            c = jnp.broadcast_to(r1[:, k + 1 : k + 2], (1, K))
            inv = 1.0 / (a * c - b * b)
            if k < K - 2:
                p0, p1 = (c * r0 - b * r1) * inv, (a * r1 - b * r0) * inv
                s0, s1 = (c * q0 - b * q1) * inv, (a * q1 - b * q0) * inv
                for i in range(kb, nb):
                    if i == kb and kr == 6:
                        continue
                    f0, f1 = left[i][:, k : k + 1], left[i][:, k + 1 : k + 2]
                    if i == kb:
                        below = row[:, :1] > kr + 1
                        f0, f1 = jnp.where(below, f0, 0.0), jnp.where(below, f1, 0.0)
                    left[i] = left[i] - (f0 * p0 + f1 * p1)
                    right[i] = right[i] - (f0 * s0 + f1 * s1)
            t = b / a
            out_ref[m, k : k + 1, :] = q0 * lax.rsqrt(a)
            out_ref[m, k + 1 : k + 2, :] = (q1 - t * q0) * lax.rsqrt(c - b * t)


def split(x):
    hi = x.astype(BF16)
    return hi, (x - hi.astype(F32)).astype(BF16)


def lanes(ref):
    return jnp.concatenate([ref[b] for b in range(BR)], axis=1)


def gram_of(a, others):
    a_hi, a_lo = a
    o_hi = jnp.concatenate([o[0] for o in others], axis=0)
    o_lo = jnp.concatenate([o[1] for o in others], axis=0)
    main = bdot(jnp.concatenate([a_hi, a_lo], axis=0), o_hi, NT)
    return main[0:K] + (main[K : 2 * K] + bdot(a_hi, o_lo, NT))


def combine(weights, parts):
    w_hi, w_lo = split(weights)
    rhs = jnp.concatenate([p[0] for p in parts] + [p[1] for p in parts], axis=0)
    m = weights.shape[0]
    lhs = jnp.concatenate([w_hi, w_lo], axis=0)
    lhs = jnp.concatenate([lhs, lhs], axis=1)
    out = bdot(lhs, rhs, NN)
    return out[0:m] + out[m : 2 * m]


def start_gram_kernel(x_ref, g_ref):
    g = jnp.zeros((K, K), F32)
    for b in range(BR):
        g = g + hdot(x_ref[b], x_ref[b], NT)
    g_ref[...] = g


def start_norm_kernel(g_ref, x_ref, n_ref, basis_ref, low_ref, inv_ref):
    inverse_factors([g_ref[...] * (1.0 / n_ref[0])], inv_ref)
    inv = inv_ref[0]
    for b in range(BR):
        v = hdot(inv, x_ref[b])
        basis_ref[b] = v
        low_ref[b] = v.astype(BF16)


def mid_kernel(low_ref, q1_ref, q2_ref, q3_ref, pa_ref, cp_ref, zp_ref, own4_ref, o0_ref, o1_ref, o2_ref, o3_ref):
    for k, src in enumerate((low_ref, q1_ref, q2_ref, q3_ref)):
        own4_ref[8 * k : 8 * k + 8] = src[...]
    o0_ref[...] = pa_ref[0:8]
    o1_ref[...] = pa_ref[8:16].astype(BF16)
    for k, out in ((0, o2_ref), (8, o3_ref)):
        v = pa_ref[16 + k : 24 + k] + cp_ref[k : 8 + k].astype(F32) + zp_ref[k : 8 + k].astype(F32)
        out[...] = v.astype(BF16)


def join_kernel(a_ref, b_ref, out_ref):
    out_ref[0:8] = a_ref[0:8]
    out_ref[8:16] = b_ref[0:8]


def apply_m_kernel(col_ref, row_ref, own_ref, cp_ref, zp_ref, tiles_ref, out_ref, low_ref, win, acc):
    win[0:32] = own_ref[...]
    win[32:64] = cp_ref[...]
    win[64:96] = zp_ref[...]
    acc[...] = jnp.zeros_like(acc)
    slots = tiles_ref.shape[0]

    def step(s, carry):
        base = s * UNROLL
        parts = []
        for u in range(UNROLL):
            parts.append(bdot(win[col_ref[base + u]], tiles_ref[base + u], NT))
        for u in range(UNROLL):
            r = row_ref[base + u]
            acc[r] = acc[r] + parts[u]
        return carry

    lax.fori_loop(0, slots // UNROLL, step, 0)
    for b in range(BR):
        v = acc[b]
        out_ref[b] = v
        low_ref[b] = v.astype(BF16)


def apply_mt_kernel(
    col_ref, row_ref, back0_ref, b1_ref, b2_ref, b3_ref, tiles_ref, own_ref, cp_ref, zp_ref, low, acc
):
    for b in range(BR):
        v = back0_ref[b] + b1_ref[b].astype(F32) + b2_ref[b].astype(F32) + b3_ref[b].astype(F32)
        low[b] = v.astype(BF16)
    low[BR] = jnp.zeros((K, TILE), BF16)
    acc[...] = jnp.zeros_like(acc)
    slots = tiles_ref.shape[0]

    def step(s, carry):
        base = s * UNROLL
        parts = []
        for u in range(UNROLL):
            parts.append(bdot(low[row_ref[base + u]], tiles_ref[base + u], NN))
        for u in range(UNROLL):
            c = col_ref[base + u]
            acc[c] = acc[c] + parts[u]
        return carry

    lax.fori_loop(0, slots // UNROLL, step, 0)
    own_ref[...] = acc[0:32]
    cp_ref[...] = acc[32:64].astype(BF16)
    zp_ref[...] = acc[64:96].astype(BF16)


def apply_at_kernel(col_ref, low_ref, tiles_ref, own_ref, cp_ref, zp_ref, acc):
    acc[...] = jnp.zeros_like(acc)
    slots = tiles_ref.shape[1]
    for b in range(BR):
        x = low_ref[b]
        parts = [bdot(x, tiles_ref[b, j], NN) for j in range(slots)]
        for j in range(slots):
            c = col_ref[b * slots + j]
            acc[c] = acc[c] + parts[j]
    own_ref[...] = acc[0:32]
    cp_ref[...] = acc[32:48].astype(BF16)
    zp_ref[...] = acc[48:64].astype(BF16)


def collect_m_kernel(low_ref, own_ref, cp_ref, zp_ref, o0_ref, s1_ref, s2_ref, s3_ref):
    v = own_ref[...] + cp_ref[...].astype(F32) + zp_ref[...].astype(F32)
    o0_ref[...] = v[0:8]
    for k, out in ((1, s1_ref), (2, s2_ref), (3, s3_ref)):
        out[0:8] = low_ref[...]
        out[8:16] = v[8 * k : 8 * k + 8].astype(BF16)


def apply_a_kernel(
    col_ref, low_ref, r1_ref, r2_ref, r3_ref, cp_ref, zp_ref, tiles_ref, basis_ref, shadow_ref, res_ref, image_ref, g_ref, win
):
    for k, src in enumerate((low_ref, r1_ref, r2_ref, r3_ref)):
        win[8 * k : 8 * k + 8] = src[0:8]
    win[32:48] = cp_ref[...]
    win[48:64] = zp_ref[...]
    slots = tiles_ref.shape[1]
    rows = []
    for b in range(BR):
        x = jnp.concatenate([win[col_ref[b * slots + j]] for j in range(slots)], axis=1)
        t = jnp.concatenate([tiles_ref[b, j] for j in range(slots)], axis=1)
        v = bdot(x, t, NT)
        image_ref[b] = v
        rows.append(v)
    image = split(jnp.concatenate(rows, axis=1))
    g = gram_of(image, [split(lanes(shadow_ref)), image, split(lanes(res_ref)), split(lanes(basis_ref))])
    g_ref[0:64] = g[:, 0:128]
    g_ref[64:128] = g[:, 128:256]


def back_gram_kernel(o0_ref, r1_ref, r2_ref, r3_ref, shadow_ref, bi_ref, g_ref):
    rows = []
    for b in range(BR):
        v = o0_ref[b] + r1_ref[8 + b].astype(F32) + r2_ref[8 + b].astype(F32) + r3_ref[8 + b].astype(F32)
        bi_ref[b] = v
        rows.append(v)
    back = split(jnp.concatenate(rows, axis=1))
    g_ref[...] = gram_of(back, [back, split(lanes(shadow_ref))])


def update_kernel(first, last, g_ref, n_ref, image_ref, bi_ref, basis_ref, shadow_ref, precond_ref, res_ref, *refs):
    refs, inv_ref, w_ref = refs[:-2], refs[-2], refs[-1]
    if first:
        sol_ref, outs = None, refs
    else:
        sol_ref, outs = refs[0], refs[1:]
    if last:
        sol_out, res_out, basis_out, shadow_out = outs
    else:
        sol_out, res_out, basis_out, shadow_out, blow_out, slow_out = outs
    total = n_ref[0]
    coup_t = g_ref[0:64, 0:64] * (1.0 / total)
    coup = coup_t.T
    normal = g_ref[0:64, 64:128]
    target = g_ref[64:128, 0:64]
    ib = g_ref[64:128, 64:128]
    bb = g_ref[128:192, 0:64]
    bs = g_ref[128:192, 64:128]
    y = hdot(ib, coup)
    uu = normal - y - y.T + total * hdot(coup_t, coup)
    y = hdot(bs, coup_t)
    ss = bb - y - y.T + total * hdot(coup, coup_t)
    inverse_factors([normal, uu * (1.0 / total), ss * (1.0 / total)], inv_ref)
    inv_n, inv_u, inv_s = inv_ref[0], inv_ref[1], inv_ref[2]
    w_t = hdot(hdot(inv_n, target), inv_n, TN)
    w_ref[0:64, 0:64] = inv_u
    w_ref[0:64, 64:128] = -hdot(inv_u, coup_t)
    w_ref[64:128, 0:64] = -w_t
    w_ref[64:128, 64:128] = jnp.zeros((K, K), F32)
    w_ref[128:192, 0:64] = inv_s
    w_ref[128:192, 64:128] = -hdot(inv_s, coup)
    w_ref[192:256, 0:64] = w_t
    w_ref[192:256, 64:128] = jnp.zeros((K, K), F32)
    zero = jnp.zeros((K, BR * TILE), BF16)
    first_two = combine(w_ref[0:128], [split(lanes(image_ref)), split(lanes(basis_ref))])
    third = combine(w_ref[128:192], [split(lanes(bi_ref)), split(lanes(shadow_ref))])
    fourth = combine(w_ref[192:256], [split(lanes(precond_ref)), (zero, zero)])
    for b in range(BR):
        at = slice(b * TILE, (b + 1) * TILE)
        v = fourth[:, at]
        sol_out[b] = v if first else sol_ref[b] + v
        res_out[b] = res_ref[b] + first_two[K : 2 * K, at]
        v = first_two[0:K, at]
        basis_out[b] = v
        if not last:
            blow_out[b] = v.astype(BF16)
        v = third[:, at]
        shadow_out[b] = v
        if not last:
            slow_out[b] = v.astype(BF16)


def shards(right_side, a_tiles, a_cols, m_tiles, m_rows, m_cols, m_count):
    blk = (BR, K, TILE)
    total = BR * TILE * lax.axis_size((DOM, BAL))
    group = lax.axis_index(DOM)
    y = lax.axis_index(BAL)
    first_row = (group * lax.axis_size(BAL) + y) * BR
    n_arr = jnp.full((1,), float(total), F32)

    def place(cols, skip):
        dev = cols // BR
        g, rel = dev // 4, (dev % 4) ^ y
        width = 4 - skip
        local = jnp.where(
            g == group, rel, jnp.where(g == (group ^ 1), 4 + rel - skip, 4 + width + rel - skip)
        )
        return local * BR + cols % BR

    a_place = place(a_cols, 2).reshape(-1)
    m_place = place(m_cols, 0)
    live = jnp.arange(m_tiles.shape[0], dtype=jnp.int32) < m_count[0]
    m_local = jnp.where(live, m_rows - first_row, BR)

    (g0,) = call(start_gram_kernel, "start_gram", [VM], [((K, K), F32)], [], (right_side,))
    g0 = reduce_all(g0)
    basis, blow = call(
        start_norm_kernel, "start_norm", [VM, VM, SM], [(blk, F32), (blk, BF16)],
        [pltpu.VMEM((1, K, K), F32)], (g0, right_side, n_arr)
    )
    shadow, slow = basis, blow
    solution, residual = None, right_side
    for iteration in range(ITERS):
        last = iteration == ITERS - 1
        q = [swap_y(blow, k) for k in (1, 2, 3)]
        pa_own, pa_cp, pa_zp = call(
            apply_at_kernel,
            "apply_at",
            [SM, VM, VM],
            [((32, K, TILE), F32), ((16, K, TILE), BF16), ((16, K, TILE), BF16)],
            [pltpu.VMEM((64, K, TILE), F32)],
            (a_place, slow, a_tiles),
            flops=84_000_000,
            nbytes=3_000_000,
        )
        ra_zp, ra_cp = swap_next(pa_zp), swap_core(pa_cp)
        own4, o0, o1, o2, o3 = call(
            mid_kernel,
            "mid",
            [VM] * 7,
            [((32, K, TILE), BF16), (blk, F32)] + [(blk, BF16)] * 3,
            [],
            (blow, *q, pa_own, ra_cp, ra_zp),
        )
        m_zp = swap_next(own4)
        b1, b2, b3 = swap_y(o1, 1), swap_y(o2, 2), swap_y(o3, 3)
        m_cp = swap_core(own4)
        pm_own, pm_cp, pm_zp = call(
            apply_mt_kernel,
            "apply_mt",
            [SM, SM] + [VM] * 5,
            [((32, K, TILE), F32), ((32, K, TILE), BF16), ((32, K, TILE), BF16)],
            [pltpu.VMEM((BR + 1, K, TILE), BF16), pltpu.VMEM((96, K, TILE), F32)],
            (m_place, m_local, o0, b1, b2, b3, m_tiles),
            flops=218_000_000,
            nbytes=5_000_000,
        )
        rm_zp, rm_cp = swap_next(pm_zp), swap_core(pm_cp)
        precond, plow = call(
            apply_m_kernel,
            "apply_m",
            [SM, SM] + [VM] * 4,
            [(blk, F32), (blk, BF16)],
            [pltpu.VMEM((96, K, TILE), BF16), pltpu.VMEM((BR + 1, K, TILE), F32)],
            (m_place, m_local, own4, m_cp, m_zp, m_tiles),
            flops=218_000_000,
            nbytes=5_000_000,
        )
        o0, s1, s2, s3 = call(
            collect_m_kernel,
            "collect_m",
            [VM] * 4,
            [(blk, F32)] + [((16, K, TILE), BF16)] * 3,
            [],
            (plow, pm_own, rm_cp, rm_zp),
        )
        r = [swap_y(s1, 1), swap_y(s2, 2), swap_y(s3, 3)]
        (far,) = call(join_kernel, "join", [VM] * 2, [((16, K, TILE), BF16)], [], (r[1], r[2]))
        a_zp, a_cp = swap_next(far), swap_core(far)
        image, g_fwd = call(
            apply_a_kernel,
            "apply_a",
            [SM] + [VM] * 10,
            [(blk, F32), ((128, 128), F32)],
            [pltpu.VMEM((64, K, TILE), BF16)],
            (a_place, plow, *r, a_cp, a_zp, a_tiles, basis, shadow, residual),
            flops=84_000_000,
            nbytes=3_000_000,
        )
        back_image, g_bwd = call(
            back_gram_kernel,
            "back_gram",
            [VM] * 5,
            [(blk, F32), ((64, 128), F32)],
            [],
            (o0, *r, shadow),
        )
        grams = reduce_all(jnp.concatenate([g_fwd, g_bwd], 0))
        args = [grams, n_arr, image, back_image, basis, shadow, precond, residual]
        if iteration:
            args.append(solution)
        outs = [(blk, F32)] * 4 + ([] if last else [(blk, BF16)] * 2)
        result = call(
            lambda *refs, f=iteration == 0, l=last: update_kernel(f, l, *refs),
            "update",
            [VM, SM] + [VM] * (len(args) - 2),
            outs,
            [pltpu.VMEM((3, K, K), F32), pltpu.VMEM((256, 128), F32)],
            args,
            final=last,
        )
        solution, residual, basis, shadow = result[:4]
        if not last:
            blow, slow = result[4:]
    return (solution, residual, basis, shadow)


def solution(mesh):
    rows = P((DOM, BAL))
    return jax.shard_map(
        shards,
        mesh=mesh,
        in_specs=(rows,) * 7,
        out_specs=(rows,) * 4,
        check_vma=False,
    )
```

profile of v0, /device:TPU:0, one launch (start us, length us, event | category | flops | bytes accessed | tf_op | source)
XLA Modules:
  0.0 248.3 jit_solution(15658321917876445883)
XLA Ops:
  3.4 3.1 %collective-permute-start.3 = (f32[64,64]{1,0:T(8,128)S(1)}, f32[64,64]{1,0:T(8,128)S(1)}, u32[]{:S(2)}, u32[]{:S(2)}) collective-permute-start(f32[64,64]{1,0:T(8,128)S(1)} %add.149), channel_id=1, source_target_pairs={{0,3},{1,2},{2,1},{3,0},{4,7},{5,6},{6,5},{7,4},{8,11},{9,10},{10,... | collective-permute-start | bytes 49160 | tf_op jit(solution)/shard_map/ppermute | solution.py:30
  8.5 3.4 %collective-permute-done.2 = f32[64,64]{1,0:T(8,128)S(1)} collective-permute-done((f32[64,64]{1,0:T(8,128)S(1)}, f32[64,64]{1,0:T(8,128)S(1)}, u32[]{:S(2)}, u32[]{:S(2)}) %collective-permute-start.2) | collective-permute-done | bytes 16416 | tf_op jit(solution)/shard_map/ppermute | solution.py:30
  12.0 4.1 %collective-permute-start.6 = (f32[64,64]{1,0:T(8,128)S(1)}, f32[64,64]{1,0:T(8,128)S(1)}, u32[]{:S(2)}, u32[]{:S(2)}) collective-permute-start(f32[64,64]{1,0:T(8,128)S(1)} %add_add_fusion.8), channel_id=1, source_target_pairs={{0,24},{4,28},{8,16},{12,20},{16,8},{20,12},{24,0},{28,4},{32,56},... | collective-permute-start | bytes 49160 | tf_op jit(solution)/shard_map/ppermute | solution.py:30
  18.0 3.5 %collective-permute-done.5 = f32[64,64]{1,0:T(8,128)S(1)} collective-permute-done((f32[64,64]{1,0:T(8,128)S(1)}, f32[64,64]{1,0:T(8,128)S(1)}, u32[]{:S(2)}, u32[]{:S(2)}) %collective-permute-start.5) | collective-permute-done | bytes 16416 | tf_op jit(solution)/shard_map/ppermute | solution.py:30
  22.3 2.8 %collective-permute-start.9 = (f32[64,64]{1,0:T(8,128)S(1)}, f32[64,64]{1,0:T(8,128)S(1)}, u32[]{:S(2)}, u32[]{:S(2)}) collective-permute-start(f32[64,64]{1,0:T(8,128)S(1)} %add_add_fusion.7), channel_id=1, source_target_pairs={{0,96},{4,100},{8,104},{12,108},{16,112},{20,116},{24,120},{28,124... | collective-permute-start | bytes 49160 | tf_op jit(solution)/shard_map/ppermute | solution.py:30
  27.5 3.1 %collective-permute-done.8 = f32[64,64]{1,0:T(8,128)S(1)} collective-permute-done((f32[64,64]{1,0:T(8,128)S(1)}, f32[64,64]{1,0:T(8,128)S(1)}, u32[]{:S(2)}, u32[]{:S(2)}) %collective-permute-start.8) | collective-permute-done | bytes 16416 | tf_op jit(solution)/shard_map/ppermute | solution.py:30
  31.5 3.3 %start_norm.1 = (f32[8,64,128]{2,1,0:T(8,128)S(1)}, bf16[8,64,128]{2,1,0:T(8,128)(2,1)S(1)}) custom-call(f32[64,64]{1,0:T(8,128)S(1)} %add_add_fusion.6.g_ref, f32[8,64,128]{2,1,0:T(8,128)S(1)} %copy-done.6, f32[1]{0:T(128)} %constant.97.clone.1.n_ref.refs_1_), custom_call_target="tpu_custom_call" | custom-call | tf_op jit(solution)/shard_map/start_norm/pallas_call | solution.py:66
  45.9 5.6 %collective-permute-done.12.q3_ref = bf16[8,64,128]{2,1,0:T(8,128)(2,1)} collective-permute-done((bf16[8,64,128]{2,1,0:T(8,128)(2,1)S(1)}, bf16[8,64,128]{2,1,0:T(8,128)(2,1)}, u32[]{:S(2)}, u32[]{:S(2)}) %collective-permute-start.12) | collective-permute-done | bytes 131104 | tf_op jit(solution)/shard_map/ppermute | solution.py:30
  61.2 3.1 %collective-permute-start.15 = (bf16[32,64,128]{2,1,0:T(8,128)(2,1)S(1)}, bf16[32,64,128]{2,1,0:T(8,128)(2,1)S(1)}, u32[]{:S(2)}, u32[]{:S(2)}) collective-permute-start(bf16[32,64,128]{2,1,0:T(8,128)(2,1)S(1)} %get-tuple-element.58.own_ref), channel_id=1, source_target_pairs={{0,4},{4,0},{8,12},{12,8},{16,20},{20,16},{24,28},{28,24},{32,36},... | collective-permute-start | bytes 1572872 | tf_op jit(solution)/shard_map/ppermute | solution.py:30
  66.3 3.7 %apply_mt.2 = (f32[32,64,128]{2,1,0:T(8,128)S(1)}, bf16[32,64,128]{2,1,0:T(8,128)(2,1)S(1)}, bf16[32,64,128]{2,1,0:T(8,128)(2,1)S(1)}) custom-call(s32[104]{0:T(128)S(1)} %get-tuple-element.105.col_ref, s32[104]{0:T(128)S(1)} %get-tuple-element.104.row_ref, f32[8,64,128]{2,1,0:T(8,128)S(1)} %get-tuple-element.60.back0_ref, ...), custom_call_target="tpu_custom_call" | custom-call | flops 218000000 | bytes 5000000 | tf_op jit(solution)/shard_map/apply_mt/pallas_call | solution.py:66
  71.0 4.4 %apply_m.2 = (f32[8,64,128]{2,1,0:T(8,128)S(1)}, bf16[8,64,128]{2,1,0:T(8,128)(2,1)S(1)}) custom-call(s32[104]{0:T(128)S(1)} %get-tuple-element.105.col_ref, s32[104]{0:T(128)S(1)} %get-tuple-element.104.row_ref, bf16[32,64,128]{2,1,0:T(8,128)(2,1)S(1)} %get-tuple-element.58.own_ref, bf16[32,64,128]{2,1,0:T(8,128)(2,1)S(1)} %collective-permute-done.15.cp_ref, ...), custom_call_target="tpu_custom_call" | custom-call | flops 218000000 | bytes 5000000 | tf_op jit(solution)/shard_map/apply_m/pallas_call | solution.py:66
  79.2 4.5 %collective-permute-done.23.a_ref.r2_ref = bf16[16,64,128]{2,1,0:T(8,128)(2,1)S(1)} collective-permute-done((bf16[16,64,128]{2,1,0:T(8,128)(2,1)S(1)}, bf16[16,64,128]{2,1,0:T(8,128)(2,1)S(1)}, u32[]{:S(2)}, u32[]{:S(2)}) %collective-permute-start.23) | collective-permute-done | bytes 262176 | tf_op jit(solution)/shard_map/ppermute | solution.py:30
  83.7 6.2 %collective-permute-done.24.b_ref.r3_ref = bf16[16,64,128]{2,1,0:T(8,128)(2,1)S(1)} collective-permute-done((bf16[16,64,128]{2,1,0:T(8,128)(2,1)S(1)}, bf16[16,64,128]{2,1,0:T(8,128)(2,1)S(1)}, u32[]{:S(2)}, u32[]{:S(2)}) %collective-permute-start.24) | collective-permute-done | bytes 262176 | tf_op jit(solution)/shard_map/ppermute | solution.py:30
  90.6 8.4 %collective-permute-start.25 = (bf16[16,64,128]{2,1,0:T(8,128)(2,1)S(1)}, bf16[16,64,128]{2,1,0:T(8,128)(2,1)S(1)}, u32[]{:S(2)}, u32[]{:S(2)}) collective-permute-start(bf16[16,64,128]{2,1,0:T(8,128)(2,1)S(1)} %join.2), channel_id=1, source_target_pairs={{0,4},{4,0},{8,12},{12,8},{16,20},{20,16},{24,28},{28,24},{32,36},... | collective-permute-start | bytes 786440 | tf_op jit(solution)/shard_map/ppermute | solution.py:30
  101.9 2.9 %collective-permute-start.27 = (f32[192,128]{1,0:T(8,128)S(1)}, f32[192,128]{1,0:T(8,128)S(1)}, u32[]{:S(2)}, u32[]{:S(2)}) collective-permute-start(f32[192,128]{1,0:T(8,128)S(1)} %constant_dynamic-update-slice_fusion), channel_id=1, source_target_pairs={{0,4},{4,0},{8,12},{12,8},{16,20},{20,16},{24,28},{28,24},{32,36},... | collective-permute-start | bytes 294920 | tf_op jit(solution)/shard_map/ppermute | solution.py:30
  110.1 3.5 %collective-permute-done.30 = f32[192,128]{1,0:T(8,128)S(1)} collective-permute-done((f32[192,128]{1,0:T(8,128)S(1)}, f32[192,128]{1,0:T(8,128)S(1)}, u32[]{:S(2)}, u32[]{:S(2)}) %collective-permute-start.30) | collective-permute-done | bytes 98336 | tf_op jit(solution)/shard_map/ppermute | solution.py:30
  115.2 5.4 %collective-permute-start.33 = (f32[192,128]{1,0:T(8,128)S(1)}, f32[192,128]{1,0:T(8,128)S(1)}, u32[]{:S(2)}, u32[]{:S(2)}) collective-permute-start(f32[192,128]{1,0:T(8,128)S(1)} %add_add_fusion.5), channel_id=1, source_target_pairs={{0,24},{4,28},{8,16},{12,20},{16,8},{20,12},{24,0},{28,4},{32,56},... | collective-permute-start | bytes 294920 | tf_op jit(solution)/shard_map/ppermute | solution.py:30
  127.9 3.4 %collective-permute-start.35 = (f32[192,128]{1,0:T(8,128)S(1)}, f32[192,128]{1,0:T(8,128)S(1)}, u32[]{:S(2)}, u32[]{:S(2)}) collective-permute-start(f32[192,128]{1,0:T(8,128)S(1)} %add_add_fusion.4), channel_id=1, source_target_pairs={{0,64},{4,68},{8,72},{12,76},{16,80},{20,84},{24,88},{28,92},{32,9... | collective-permute-start | bytes 294920 | tf_op jit(solution)/shard_map/ppermute | solution.py:30
  136.0 8.0 %update.2 = (f32[8,64,128]{2,1,0:T(8,128)S(1)}, f32[8,64,128]{2,1,0:T(8,128)S(1)}, f32[8,64,128]{2,1,0:T(8,128)S(1)}, f32[8,64,128]{2,1,0:T(8,128)S(1)}, bf16[8,...) custom-call(f32[192,128]{1,0:T(8,128)S(1)} %add_add_fusion.3.refs_0_, f32[1]{0:T(128)} %constant.97.clone.1.n_ref.refs_1_, ...), custom_call_target="tpu_custom_call" | custom-call | tf_op jit(solution)/shard_map/update/pallas_call | solution.py:66
  150.1 2.7 %collective-permute-done.39.q3_ref = bf16[8,64,128]{2,1,0:T(8,128)(2,1)S(1)} collective-permute-done((bf16[8,64,128]{2,1,0:T(8,128)(2,1)S(1)}, bf16[8,64,128]{2,1,0:T(8,128)(2,1)S(1)}, u32[]{:S(2)}, u32[]{:S(2)}) %collective-permute-start.39) | collective-permute-done | bytes 131104 | tf_op jit(solution)/shard_map/ppermute | solution.py:30
  157.4 3.0 %collective-permute-start.45 = (bf16[8,64,128]{2,1,0:T(8,128)(2,1)S(1)}, bf16[8,64,128]{2,1,0:T(8,128)(2,1)S(1)}, u32[]{:S(2)}, u32[]{:S(2)}) collective-permute-start(bf16[8,64,128]{2,1,0:T(8,128)(2,1)S(1)} %get-tuple-element.86), channel_id=1, source_target_pairs={{0,2},{1,3},{2,0},{3,1},{4,6},{5,7},{6,4},{7,5},{8,10},{9,11},{10,... | collective-permute-start | bytes 393224 | tf_op jit(solution)/shard_map/ppermute | solution.py:30
  162.4 4.0 %collective-permute-start.42 = (bf16[32,64,128]{2,1,0:T(8,128)(2,1)S(1)}, bf16[32,64,128]{2,1,0:T(8,128)(2,1)S(1)}, u32[]{:S(2)}, u32[]{:S(2)}) collective-permute-start(bf16[32,64,128]{2,1,0:T(8,128)(2,1)S(1)} %get-tuple-element.82.own_ref), channel_id=1, source_target_pairs={{0,4},{4,0},{8,12},{12,8},{16,20},{20,16},{24,28},{28,24},{32,36},... | collective-permute-start | bytes 1572872 | tf_op jit(solution)/shard_map/ppermute | solution.py:30
  169.3 3.7 %apply_mt.3 = (f32[32,64,128]{2,1,0:T(8,128)S(1)}, bf16[32,64,128]{2,1,0:T(8,128)(2,1)S(1)}, bf16[32,64,128]{2,1,0:T(8,128)(2,1)S(1)}) custom-call(s32[104]{0:T(128)S(1)} %get-tuple-element.105.col_ref, s32[104]{0:T(128)S(1)} %get-tuple-element.104.row_ref, f32[8,64,128]{2,1,0:T(8,128)S(1)} %get-tuple-element.84.back0_ref, ...), custom_call_target="tpu_custom_call" | custom-call | flops 218000000 | bytes 5000000 | tf_op jit(solution)/shard_map/apply_mt/pallas_call | solution.py:66
  173.8 4.4 %apply_m.3 = (f32[8,64,128]{2,1,0:T(8,128)S(1)}, bf16[8,64,128]{2,1,0:T(8,128)(2,1)S(1)}) custom-call(s32[104]{0:T(128)S(1)} %get-tuple-element.105.col_ref, s32[104]{0:T(128)S(1)} %get-tuple-element.104.row_ref, bf16[32,64,128]{2,1,0:T(8,128)(2,1)S(1)} %get-tuple-element.82.own_ref, bf16[32,64,128]{2,1,0:T(8,128)(2,1)S(1)} %collective-permute-done.42.cp_ref, ...), custom_call_target="tpu_custom_call" | custom-call | flops 218000000 | bytes 5000000 | tf_op jit(solution)/shard_map/apply_m/pallas_call | solution.py:66
  182.0 4.5 %collective-permute-done.50.a_ref.r2_ref = bf16[16,64,128]{2,1,0:T(8,128)(2,1)S(1)} collective-permute-done((bf16[16,64,128]{2,1,0:T(8,128)(2,1)S(1)}, bf16[16,64,128]{2,1,0:T(8,128)(2,1)S(1)}, u32[]{:S(2)}, u32[]{:S(2)}) %collective-permute-start.50) | collective-permute-done | bytes 262176 | tf_op jit(solution)/shard_map/ppermute | solution.py:30
  186.5 5.8 %collective-permute-done.51.b_ref.r3_ref = bf16[16,64,128]{2,1,0:T(8,128)(2,1)S(1)} collective-permute-done((bf16[16,64,128]{2,1,0:T(8,128)(2,1)S(1)}, bf16[16,64,128]{2,1,0:T(8,128)(2,1)S(1)}, u32[]{:S(2)}, u32[]{:S(2)}) %collective-permute-start.51) | collective-permute-done | bytes 262176 | tf_op jit(solution)/shard_map/ppermute | solution.py:30
  193.0 9.9 %collective-permute-start.52 = (bf16[16,64,128]{2,1,0:T(8,128)(2,1)S(1)}, bf16[16,64,128]{2,1,0:T(8,128)(2,1)S(1)}, u32[]{:S(2)}, u32[]{:S(2)}) collective-permute-start(bf16[16,64,128]{2,1,0:T(8,128)(2,1)S(1)} %join.3), channel_id=1, source_target_pairs={{0,4},{4,0},{8,12},{12,8},{16,20},{20,16},{24,28},{28,24},{32,36},... | collective-permute-start | bytes 786440 | tf_op jit(solution)/shard_map/ppermute | solution.py:30
  213.5 4.0 %collective-permute-done.57 = f32[192,128]{1,0:T(8,128)S(1)} collective-permute-done((f32[192,128]{1,0:T(8,128)S(1)}, f32[192,128]{1,0:T(8,128)S(1)}, u32[]{:S(2)}, u32[]{:S(2)}) %collective-permute-start.57) | collective-permute-done | bytes 98336 | tf_op jit(solution)/shard_map/ppermute | solution.py:30
  218.4 7.0 %collective-permute-start.60 = (f32[192,128]{1,0:T(8,128)S(1)}, f32[192,128]{1,0:T(8,128)S(1)}, u32[]{:S(2)}, u32[]{:S(2)}) collective-permute-start(f32[192,128]{1,0:T(8,128)S(1)} %add_add_fusion.2), channel_id=1, source_target_pairs={{0,24},{4,28},{8,16},{12,20},{16,8},{20,12},{24,0},{28,4},{32,56},... | collective-permute-start | bytes 294920 | tf_op jit(solution)/shard_map/ppermute | solution.py:30
  231.8 2.8 %collective-permute-start.62 = (f32[192,128]{1,0:T(8,128)S(1)}, f32[192,128]{1,0:T(8,128)S(1)}, u32[]{:S(2)}, u32[]{:S(2)}) collective-permute-start(f32[192,128]{1,0:T(8,128)S(1)} %add_add_fusion.1), channel_id=1, source_target_pairs={{0,64},{4,68},{8,72},{12,76},{16,80},{20,84},{24,88},{28,92},{32,9... | collective-permute-start | bytes 294920 | tf_op jit(solution)/shard_map/ppermute | solution.py:30
  235.8 2.8 %collective-permute-done.63 = f32[192,128]{1,0:T(8,128)S(1)} collective-permute-done((f32[192,128]{1,0:T(8,128)S(1)}, f32[192,128]{1,0:T(8,128)S(1)}, u32[]{:S(2)}, u32[]{:S(2)}) %collective-permute-start.63) | collective-permute-done | bytes 98336 | tf_op jit(solution)/shard_map/ppermute | solution.py:30
  239.5 8.8 %update.3 = (f32[8,64,128]{2,1,0:T(8,128)}, f32[8,64,128]{2,1,0:T(8,128)}, f32[8,64,128]{2,1,0:T(8,128)}, f32[8,64,128]{2,1,0:T(8,128)}) custom-call(f32[192,128]{1,0:T(8,128)S(1)} %add_add_fusion.refs_0_, f32[1]{0:T(128)} %constant.97.clone.1.n_ref.refs_1_, f32[8,64,128]{2,1,0:T(8,128)S(1)} %get-tuple-element.100.refs_2_, ...), custom_call_target="tpu_custom_call" | custom-call | tf_op jit(solution)/shard_map/update/pallas_call | solution.py:66
  (155 shorter events, 100.7 us)
Async XLA Ops:
  39.8 12.7 %collective-permute-start.13 = (bf16[16,64,128]{2,1,0:T(8,128)(2,1)}, bf16[16,64,128]{2,1,0:T(8,128)(2,1)}, u32[]{:S(2)}, u32[]{:S(2)}) collective-permute-start(bf16[16,64,128]{2,1,0:T(8,128)(2,1)} %get-tuple-element.56), channel_id=1, source_target_pairs={{0,4},{4,0},{8,12},{12,8},{16,20},{20,16},{24,28},{28,24},{32,36},... | collective-permute-start | bytes 786440 | tf_op jit(solution)/shard_map/ppermute | solution.py:30
  39.8 12.7 %collective-permute-start.14 = (bf16[16,64,128]{2,1,0:T(8,128)(2,1)}, bf16[16,64,128]{2,1,0:T(8,128)(2,1)}, u32[]{:S(2)}, u32[]{:S(2)}) collective-permute-start(bf16[16,64,128]{2,1,0:T(8,128)(2,1)} %get-tuple-element.57), channel_id=1, source_target_pairs={{4,8},{8,4},{12,16},{16,12},{20,24},{24,20},{28,32},{32,28},{36,40... | collective-permute-start | bytes 786440 | tf_op jit(solution)/shard_map/ppermute | solution.py:46
  41.1 10.3 %collective-permute-start.12 = (bf16[8,64,128]{2,1,0:T(8,128)(2,1)S(1)}, bf16[8,64,128]{2,1,0:T(8,128)(2,1)}, u32[]{:S(2)}, u32[]{:S(2)}) collective-permute-start(bf16[8,64,128]{2,1,0:T(8,128)(2,1)S(1)} %get-tuple-element.54.low_ref), channel_id=1, source_target_pairs={{0,3},{1,2},{2,1},{3,0},{4,7},{5,6},{6,5},{7,4},{8,11},{9,10},{10,... | collective-permute-start | bytes 393224 | tf_op jit(solution)/shard_map/ppermute | solution.py:30
  42.4 9.0 %collective-permute-start.11 = (bf16[8,64,128]{2,1,0:T(8,128)(2,1)S(1)}, bf16[8,64,128]{2,1,0:T(8,128)(2,1)}, u32[]{:S(2)}, u32[]{:S(2)}) collective-permute-start(bf16[8,64,128]{2,1,0:T(8,128)(2,1)S(1)} %get-tuple-element.54.low_ref), channel_id=1, source_target_pairs={{0,2},{1,3},{2,0},{3,1},{4,6},{5,7},{6,4},{7,5},{8,10},{9,11},{10,... | collective-permute-start | bytes 393224 | tf_op jit(solution)/shard_map/ppermute | solution.py:30
  43.6 8.8 %collective-permute-start.10 = (bf16[8,64,128]{2,1,0:T(8,128)(2,1)S(1)}, bf16[8,64,128]{2,1,0:T(8,128)(2,1)}, u32[]{:S(2)}, u32[]{:S(2)}) collective-permute-start(bf16[8,64,128]{2,1,0:T(8,128)(2,1)S(1)} %get-tuple-element.54.low_ref), channel_id=1, source_target_pairs={{0,1},{1,0},{2,3},{3,2},{4,5},{5,4},{6,7},{7,6},{8,9},{9,8},{10,11... | collective-permute-start | bytes 393224 | tf_op jit(solution)/shard_map/ppermute | solution.py:30
  55.0 9.3 %collective-permute-start.17 = (bf16[8,64,128]{2,1,0:T(8,128)(2,1)S(1)}, bf16[8,64,128]{2,1,0:T(8,128)(2,1)S(1)}, u32[]{:S(2)}, u32[]{:S(2)}) collective-permute-start(bf16[8,64,128]{2,1,0:T(8,128)(2,1)S(1)} %get-tuple-element.61), channel_id=1, source_target_pairs={{0,1},{1,0},{2,3},{3,2},{4,5},{5,4},{6,7},{7,6},{8,9},{9,8},{10,11... | collective-permute-start | bytes 393224 | tf_op jit(solution)/shard_map/ppermute | solution.py:30
  55.5 8.8 %collective-permute-start.18 = (bf16[8,64,128]{2,1,0:T(8,128)(2,1)S(1)}, bf16[8,64,128]{2,1,0:T(8,128)(2,1)S(1)}, u32[]{:S(2)}, u32[]{:S(2)}) collective-permute-start(bf16[8,64,128]{2,1,0:T(8,128)(2,1)S(1)} %get-tuple-element.62), channel_id=1, source_target_pairs={{0,2},{1,3},{2,0},{3,1},{4,6},{5,7},{6,4},{7,5},{8,10},{9,11},{10,... | collective-permute-start | bytes 393224 | tf_op jit(solution)/shard_map/ppermute | solution.py:30
  57.8 8.5 %collective-permute-start.19 = (bf16[8,64,128]{2,1,0:T(8,128)(2,1)S(1)}, bf16[8,64,128]{2,1,0:T(8,128)(2,1)S(1)}, u32[]{:S(2)}, u32[]{:S(2)}) collective-permute-start(bf16[8,64,128]{2,1,0:T(8,128)(2,1)S(1)} %get-tuple-element.63), channel_id=1, source_target_pairs={{0,3},{1,2},{2,1},{3,0},{4,7},{5,6},{6,5},{7,4},{8,11},{9,10},{10,... | collective-permute-start | bytes 393224 | tf_op jit(solution)/shard_map/ppermute | solution.py:30
  60.5 10.5 %collective-permute-start.16 = (bf16[32,64,128]{2,1,0:T(8,128)(2,1)S(1)}, bf16[32,64,128]{2,1,0:T(8,128)(2,1)S(1)}, u32[]{:S(2)}, u32[]{:S(2)}) collective-permute-start(bf16[32,64,128]{2,1,0:T(8,128)(2,1)S(1)} %get-tuple-element.58.own_ref), channel_id=1, source_target_pairs={{4,8},{8,4},{12,16},{16,12},{20,24},{24,20},{28,32},{32,28},{36,40... | collective-permute-start | bytes 1572872 | tf_op jit(solution)/shard_map/ppermute | solution.py:46
  61.2 9.8 %collective-permute-start.15 = (bf16[32,64,128]{2,1,0:T(8,128)(2,1)S(1)}, bf16[32,64,128]{2,1,0:T(8,128)(2,1)S(1)}, u32[]{:S(2)}, u32[]{:S(2)}) collective-permute-start(bf16[32,64,128]{2,1,0:T(8,128)(2,1)S(1)} %get-tuple-element.58.own_ref), channel_id=1, source_target_pairs={{0,4},{4,0},{8,12},{12,8},{16,20},{20,16},{24,28},{28,24},{32,36},... | collective-permute-start | bytes 1572872 | tf_op jit(solution)/shard_map/ppermute | solution.py:30
  75.6 8.1 %collective-permute-start.23 = (bf16[16,64,128]{2,1,0:T(8,128)(2,1)S(1)}, bf16[16,64,128]{2,1,0:T(8,128)(2,1)S(1)}, u32[]{:S(2)}, u32[]{:S(2)}) collective-permute-start(bf16[16,64,128]{2,1,0:T(8,128)(2,1)S(1)} %get-tuple-element.68), channel_id=1, source_target_pairs={{0,2},{1,3},{2,0},{3,1},{4,6},{5,7},{6,4},{7,5},{8,10},{9,11},{10,... | collective-permute-start | bytes 786440 | tf_op jit(solution)/shard_map/ppermute | solution.py:30
  76.1 13.9 %collective-permute-start.24 = (bf16[16,64,128]{2,1,0:T(8,128)(2,1)S(1)}, bf16[16,64,128]{2,1,0:T(8,128)(2,1)S(1)}, u32[]{:S(2)}, u32[]{:S(2)}) collective-permute-start(bf16[16,64,128]{2,1,0:T(8,128)(2,1)S(1)} %get-tuple-element.69), channel_id=1, source_target_pairs={{0,3},{1,2},{2,1},{3,0},{4,7},{5,6},{6,5},{7,4},{8,11},{9,10},{10,... | collective-permute-start | bytes 786440 | tf_op jit(solution)/shard_map/ppermute | solution.py:30
  78.2 20.9 %collective-permute-start.22 = (bf16[16,64,128]{2,1,0:T(8,128)(2,1)S(1)}, bf16[16,64,128]{2,1,0:T(8,128)(2,1)S(1)}, u32[]{:S(2)}, u32[]{:S(2)}) collective-permute-start(bf16[16,64,128]{2,1,0:T(8,128)(2,1)S(1)} %get-tuple-element.67), channel_id=1, source_target_pairs={{0,1},{1,0},{2,3},{3,2},{4,5},{5,4},{6,7},{7,6},{8,9},{9,8},{10,11... | collective-permute-start | bytes 786440 | tf_op jit(solution)/shard_map/ppermute | solution.py:30
  90.0 9.4 %collective-permute-start.26 = (bf16[16,64,128]{2,1,0:T(8,128)(2,1)S(1)}, bf16[16,64,128]{2,1,0:T(8,128)(2,1)S(1)}, u32[]{:S(2)}, u32[]{:S(2)}) collective-permute-start(bf16[16,64,128]{2,1,0:T(8,128)(2,1)S(1)} %join.2), channel_id=1, source_target_pairs={{4,8},{8,4},{12,16},{16,12},{20,24},{24,20},{28,32},{32,28},{36,40... | collective-permute-start | bytes 786440 | tf_op jit(solution)/shard_map/ppermute | solution.py:46
  90.6 9.6 %collective-permute-start.25 = (bf16[16,64,128]{2,1,0:T(8,128)(2,1)S(1)}, bf16[16,64,128]{2,1,0:T(8,128)(2,1)S(1)}, u32[]{:S(2)}, u32[]{:S(2)}) collective-permute-start(bf16[16,64,128]{2,1,0:T(8,128)(2,1)S(1)} %join.2), channel_id=1, source_target_pairs={{0,4},{4,0},{8,12},{12,8},{16,20},{20,16},{24,28},{28,24},{32,36},... | collective-permute-start | bytes 786440 | tf_op jit(solution)/shard_map/ppermute | solution.py:30
  105.7 7.9 %collective-permute-start.30 = (f32[192,128]{1,0:T(8,128)S(1)}, f32[192,128]{1,0:T(8,128)S(1)}, u32[]{:S(2)}, u32[]{:S(2)}) collective-permute-start(f32[192,128]{1,0:T(8,128)S(1)} %add.159), channel_id=1, source_target_pairs={{0,3},{1,2},{2,1},{3,0},{4,7},{5,6},{6,5},{7,4},{8,11},{9,10},{10,... | collective-permute-start | bytes 294920 | tf_op jit(solution)/shard_map/ppermute | solution.py:30
  115.2 8.8 %collective-permute-start.33 = (f32[192,128]{1,0:T(8,128)S(1)}, f32[192,128]{1,0:T(8,128)S(1)}, u32[]{:S(2)}, u32[]{:S(2)}) collective-permute-start(f32[192,128]{1,0:T(8,128)S(1)} %add_add_fusion.5), channel_id=1, source_target_pairs={{0,24},{4,28},{8,16},{12,20},{16,8},{20,12},{24,0},{28,4},{32,56},... | collective-permute-start | bytes 294920 | tf_op jit(solution)/shard_map/ppermute | solution.py:30
  145.2 11.7 %collective-permute-start.40 = (bf16[16,64,128]{2,1,0:T(8,128)(2,1)S(1)}, bf16[16,64,128]{2,1,0:T(8,128)(2,1)S(1)}, u32[]{:S(2)}, u32[]{:S(2)}) collective-permute-start(bf16[16,64,128]{2,1,0:T(8,128)(2,1)S(1)} %get-tuple-element.80), channel_id=1, source_target_pairs={{0,4},{4,0},{8,12},{12,8},{16,20},{20,16},{24,28},{28,24},{32,36},... | collective-permute-start | bytes 786440 | tf_op jit(solution)/shard_map/ppermute | solution.py:30
  145.2 11.6 %collective-permute-start.41 = (bf16[16,64,128]{2,1,0:T(8,128)(2,1)S(1)}, bf16[16,64,128]{2,1,0:T(8,128)(2,1)S(1)}, u32[]{:S(2)}, u32[]{:S(2)}) collective-permute-start(bf16[16,64,128]{2,1,0:T(8,128)(2,1)S(1)} %get-tuple-element.81), channel_id=1, source_target_pairs={{4,8},{8,4},{12,16},{16,12},{20,24},{24,20},{28,32},{32,28},{36,40... | collective-permute-start | bytes 786440 | tf_op jit(solution)/shard_map/ppermute | solution.py:46
  148.4 8.4 %collective-permute-start.37 = (bf16[8,64,128]{2,1,0:T(8,128)(2,1)S(1)}, bf16[8,64,128]{2,1,0:T(8,128)(2,1)S(1)}, u32[]{:S(2)}, u32[]{:S(2)}) collective-permute-start(bf16[8,64,128]{2,1,0:T(8,128)(2,1)S(1)} %get-tuple-element.77.low_ref), channel_id=1, source_target_pairs={{0,1},{1,0},{2,3},{3,2},{4,5},{5,4},{6,7},{7,6},{8,9},{9,8},{10,11... | collective-permute-start | bytes 393224 | tf_op jit(solution)/shard_map/ppermute | solution.py:30
  157.0 9.4 %collective-permute-start.44 = (bf16[8,64,128]{2,1,0:T(8,128)(2,1)S(1)}, bf16[8,64,128]{2,1,0:T(8,128)(2,1)S(1)}, u32[]{:S(2)}, u32[]{:S(2)}) collective-permute-start(bf16[8,64,128]{2,1,0:T(8,128)(2,1)S(1)} %get-tuple-element.85), channel_id=1, source_target_pairs={{0,1},{1,0},{2,3},{3,2},{4,5},{5,4},{6,7},{7,6},{8,9},{9,8},{10,11... | collective-permute-start | bytes 393224 | tf_op jit(solution)/shard_map/ppermute | solution.py:30
  157.4 9.6 %collective-permute-start.45 = (bf16[8,64,128]{2,1,0:T(8,128)(2,1)S(1)}, bf16[8,64,128]{2,1,0:T(8,128)(2,1)S(1)}, u32[]{:S(2)}, u32[]{:S(2)}) collective-permute-start(bf16[8,64,128]{2,1,0:T(8,128)(2,1)S(1)} %get-tuple-element.86), channel_id=1, source_target_pairs={{0,2},{1,3},{2,0},{3,1},{4,6},{5,7},{6,4},{7,5},{8,10},{9,11},{10,... | collective-permute-start | bytes 393224 | tf_op jit(solution)/shard_map/ppermute | solution.py:30
  160.4 8.9 %collective-permute-start.46 = (bf16[8,64,128]{2,1,0:T(8,128)(2,1)S(1)}, bf16[8,64,128]{2,1,0:T(8,128)(2,1)S(1)}, u32[]{:S(2)}, u32[]{:S(2)}) collective-permute-start(bf16[8,64,128]{2,1,0:T(8,128)(2,1)S(1)} %get-tuple-element.87), channel_id=1, source_target_pairs={{0,3},{1,2},{2,1},{3,0},{4,7},{5,6},{6,5},{7,4},{8,11},{9,10},{10,... | collective-permute-start | bytes 393224 | tf_op jit(solution)/shard_map/ppermute | solution.py:30
  161.8 12.0 %collective-permute-start.43 = (bf16[32,64,128]{2,1,0:T(8,128)(2,1)S(1)}, bf16[32,64,128]{2,1,0:T(8,128)(2,1)S(1)}, u32[]{:S(2)}, u32[]{:S(2)}) collective-permute-start(bf16[32,64,128]{2,1,0:T(8,128)(2,1)S(1)} %get-tuple-element.82.own_ref), channel_id=1, source_target_pairs={{4,8},{8,4},{12,16},{16,12},{20,24},{24,20},{28,32},{32,28},{36,40... | collective-permute-start | bytes 1572872 | tf_op jit(solution)/shard_map/ppermute | solution.py:46
  162.4 11.3 %collective-permute-start.42 = (bf16[32,64,128]{2,1,0:T(8,128)(2,1)S(1)}, bf16[32,64,128]{2,1,0:T(8,128)(2,1)S(1)}, u32[]{:S(2)}, u32[]{:S(2)}) collective-permute-start(bf16[32,64,128]{2,1,0:T(8,128)(2,1)S(1)} %get-tuple-element.82.own_ref), channel_id=1, source_target_pairs={{0,4},{4,0},{8,12},{12,8},{16,20},{20,16},{24,28},{28,24},{32,36},... | collective-permute-start | bytes 1572872 | tf_op jit(solution)/shard_map/ppermute | solution.py:30
  178.4 8.1 %collective-permute-start.50 = (bf16[16,64,128]{2,1,0:T(8,128)(2,1)S(1)}, bf16[16,64,128]{2,1,0:T(8,128)(2,1)S(1)}, u32[]{:S(2)}, u32[]{:S(2)}) collective-permute-start(bf16[16,64,128]{2,1,0:T(8,128)(2,1)S(1)} %get-tuple-element.92), channel_id=1, source_target_pairs={{0,2},{1,3},{2,0},{3,1},{4,6},{5,7},{6,4},{7,5},{8,10},{9,11},{10,... | collective-permute-start | bytes 786440 | tf_op jit(solution)/shard_map/ppermute | solution.py:30
  178.5 13.8 %collective-permute-start.51 = (bf16[16,64,128]{2,1,0:T(8,128)(2,1)S(1)}, bf16[16,64,128]{2,1,0:T(8,128)(2,1)S(1)}, u32[]{:S(2)}, u32[]{:S(2)}) collective-permute-start(bf16[16,64,128]{2,1,0:T(8,128)(2,1)S(1)} %get-tuple-element.93), channel_id=1, source_target_pairs={{0,3},{1,2},{2,1},{3,0},{4,7},{5,6},{6,5},{7,4},{8,11},{9,10},{10,... | collective-permute-start | bytes 786440 | tf_op jit(solution)/shard_map/ppermute | solution.py:30
  180.0 22.9 %collective-permute-start.49 = (bf16[16,64,128]{2,1,0:T(8,128)(2,1)S(1)}, bf16[16,64,128]{2,1,0:T(8,128)(2,1)S(1)}, u32[]{:S(2)}, u32[]{:S(2)}) collective-permute-start(bf16[16,64,128]{2,1,0:T(8,128)(2,1)S(1)} %get-tuple-element.91), channel_id=1, source_target_pairs={{0,1},{1,0},{2,3},{3,2},{4,5},{5,4},{6,7},{7,6},{8,9},{9,8},{10,11... | collective-permute-start | bytes 786440 | tf_op jit(solution)/shard_map/ppermute | solution.py:30
  192.3 10.9 %collective-permute-start.53 = (bf16[16,64,128]{2,1,0:T(8,128)(2,1)S(1)}, bf16[16,64,128]{2,1,0:T(8,128)(2,1)S(1)}, u32[]{:S(2)}, u32[]{:S(2)}) collective-permute-start(bf16[16,64,128]{2,1,0:T(8,128)(2,1)S(1)} %join.3), channel_id=1, source_target_pairs={{4,8},{8,4},{12,16},{16,12},{20,24},{24,20},{28,32},{32,28},{36,40... | collective-permute-start | bytes 786440 | tf_op jit(solution)/shard_map/ppermute | solution.py:46
  193.0 11.0 %collective-permute-start.52 = (bf16[16,64,128]{2,1,0:T(8,128)(2,1)S(1)}, bf16[16,64,128]{2,1,0:T(8,128)(2,1)S(1)}, u32[]{:S(2)}, u32[]{:S(2)}) collective-permute-start(bf16[16,64,128]{2,1,0:T(8,128)(2,1)S(1)} %join.3), channel_id=1, source_target_pairs={{0,4},{4,0},{8,12},{12,8},{16,20},{20,16},{24,28},{28,24},{32,36},... | collective-permute-start | bytes 786440 | tf_op jit(solution)/shard_map/ppermute | solution.py:30
  209.3 8.2 %collective-permute-start.57 = (f32[192,128]{1,0:T(8,128)S(1)}, f32[192,128]{1,0:T(8,128)S(1)}, u32[]{:S(2)}, u32[]{:S(2)}) collective-permute-start(f32[192,128]{1,0:T(8,128)S(1)} %add.169), channel_id=1, source_target_pairs={{0,3},{1,2},{2,1},{3,0},{4,7},{5,6},{6,5},{7,4},{8,11},{9,10},{10,... | collective-permute-start | bytes 294920 | tf_op jit(solution)/shard_map/ppermute | solution.py:30
  218.4 10.6 %collective-permute-start.60 = (f32[192,128]{1,0:T(8,128)S(1)}, f32[192,128]{1,0:T(8,128)S(1)}, u32[]{:S(2)}, u32[]{:S(2)}) collective-permute-start(f32[192,128]{1,0:T(8,128)S(1)} %add_add_fusion.2), channel_id=1, source_target_pairs={{0,24},{4,28},{8,16},{12,20},{16,8},{20,12},{24,0},{28,4},{32,56},... | collective-permute-start | bytes 294920 | tf_op jit(solution)/shard_map/ppermute | solution.py:30
  (42 other events, 330.1 us)
where the time goes:
time: 249 us; the launch traced here: 248 us
  starting transfers between devices  107 us (43%)
  waiting for transfers between devices  84.8 us (34%)
  Pallas kernels  45.7 us (18%)
  local copies, waits for them, and re-layouts  6.23 us (3%)
    ppermute x56, starting transfers between devices, swap(): return lax.ppermute(value, axis, [(i, i ^ distance) for i in range(size)])  101 us
    ppermute x56, waiting for transfers between devices, swap(): return lax.ppermute(value, axis, [(i, i ^ distance) for i in range(size)])  84.8 us
    pallas_call x20, Pallas kernels, call(): pl.pallas_call(body, name=name, in_specs=specs, out_specs=tuple((VM for _...  45.7 us
    ppermute x8, starting transfers between devices, swap_next(): return lax.ppermute(value, DOM, route)  6.28 us
    unnamed x22, local copies, waits for them, and re-layouts  6.14 us
  transfers between devices with their start and end apart: 64, of which 37 were waited for; matrix products, arithmetic and copies ran while one was open for 1% of the time, Pallas kernels for 7%

commit v1 on v0

--- a/solution.py
+++ b/solution.py
@@ -46,15 +46,25 @@
     return lax.ppermute(value, DOM, route)
 
 
-def reduce_all(value):
+def reduce_yzx(value):
     size = lax.axis_size(DOM)
-    value = value + swap(value, DOM, size, 1)
     parts = [swap_y(value, k) for k in (1, 2, 3)]
     value = (value + parts[0]) + (parts[1] + parts[2])
     for unit in (2, 8):
         parts = [swap(value, DOM, size, k * unit) for k in (1, 2, 3)]
         value = (value + parts[0]) + (parts[1] + parts[2])
     return value
+
+
+def reduce_all(value):
+    return reduce_yzx(value + swap_core(value))
+
+
+def reduce_halves(first, second, take_first):
+    mine = jnp.where(take_first, first, second) + swap_core(jnp.where(take_first, second, first))
+    mine = reduce_yzx(mine)
+    other = swap_core(mine)
+    return jnp.where(take_first, mine, other), jnp.where(take_first, other, mine)
 
 
 VM = pl.BlockSpec(memory_space=pltpu.VMEM)
@@ -144,9 +154,11 @@
     g_ref[...] = g
 
 
-def start_norm_kernel(g_ref, x_ref, n_ref, basis_ref, low_ref, inv_ref):
-    inverse_factors([g_ref[...] * (1.0 / n_ref[0])], inv_ref)
+def start_norm_kernel(g_ref, x_ref, n_ref, basis_ref, low_ref, lt_ref, inv_ref):
+    g = g_ref[...] * (1.0 / n_ref[0])
+    inverse_factors([g], inv_ref)
     inv = inv_ref[0]
+    lt_ref[...] = hdot(inv, g)
     for b in range(BR):
         v = hdot(inv, x_ref[b])
         basis_ref[b] = v
@@ -164,8 +176,8 @@
 
 
 def join_kernel(a_ref, b_ref, out_ref):
-    out_ref[0:8] = a_ref[0:8]
-    out_ref[8:16] = b_ref[0:8]
+    out_ref[0:8] = a_ref[...]
+    out_ref[8:16] = b_ref[...]
 
 
 def apply_m_kernel(col_ref, row_ref, own_ref, cp_ref, zp_ref, tiles_ref, out_ref, low_ref, win, acc):
@@ -232,19 +244,21 @@
     zp_ref[...] = acc[48:64].astype(BF16)
 
 
-def collect_m_kernel(low_ref, own_ref, cp_ref, zp_ref, o0_ref, s1_ref, s2_ref, s3_ref):
+def collect_m_kernel(own_ref, cp_ref, zp_ref, o0_ref, o1_ref, o2_ref, o3_ref):
     v = own_ref[...] + cp_ref[...].astype(F32) + zp_ref[...].astype(F32)
     o0_ref[...] = v[0:8]
-    for k, out in ((1, s1_ref), (2, s2_ref), (3, s3_ref)):
-        out[0:8] = low_ref[...]
-        out[8:16] = v[8 * k : 8 * k + 8].astype(BF16)
-
-
-def apply_a_kernel(
-    col_ref, low_ref, r1_ref, r2_ref, r3_ref, cp_ref, zp_ref, tiles_ref, basis_ref, shadow_ref, res_ref, image_ref, g_ref, win
-):
+    o1_ref[...] = v[8:16].astype(BF16)
+    o2_ref[...] = v[16:24].astype(BF16)
+    o3_ref[...] = v[24:32].astype(BF16)
+
+
+def apply_a_kernel(first, col_ref, low_ref, r1_ref, r2_ref, r3_ref, cp_ref, zp_ref, tiles_ref, shadow_ref, *refs):
+    if first:
+        image_ref, g_ref, win = refs
+    else:
+        basis_ref, res_ref, image_ref, g_ref, rest_ref, win = refs
     for k, src in enumerate((low_ref, r1_ref, r2_ref, r3_ref)):
-        win[8 * k : 8 * k + 8] = src[0:8]
+        win[8 * k : 8 * k + 8] = src[...]
     win[32:48] = cp_ref[...]
     win[48:64] = zp_ref[...]
     slots = tiles_ref.shape[1]
@@ -256,25 +270,35 @@
         image_ref[b] = v
         rows.append(v)
     image = split(jnp.concatenate(rows, axis=1))
-    g = gram_of(image, [split(lanes(shadow_ref)), image, split(lanes(res_ref)), split(lanes(basis_ref))])
+    others = [split(lanes(shadow_ref)), image]
+    if not first:
+        others += [split(lanes(res_ref)), split(lanes(basis_ref))]
+    g = gram_of(image, others)
     g_ref[0:64] = g[:, 0:128]
-    g_ref[64:128] = g[:, 128:256]
-
-
-def back_gram_kernel(o0_ref, r1_ref, r2_ref, r3_ref, shadow_ref, bi_ref, g_ref):
+    if not first:
+        g_ref[64:96] = g[0:32, 128:256]
+        rest_ref[...] = g[32:64, 128:256]
+
+
+def back_gram_kernel(first, o0_ref, b1_ref, b2_ref, b3_ref, shadow_ref, *refs):
+    if first:
+        bi_ref, g_ref = refs
+    else:
+        rest_ref, bi_ref, g_ref = refs
+        g_ref[64:96] = rest_ref[...]
     rows = []
     for b in range(BR):
-        v = o0_ref[b] + r1_ref[8 + b].astype(F32) + r2_ref[8 + b].astype(F32) + r3_ref[8 + b].astype(F32)
+        v = o0_ref[b] + b1_ref[b].astype(F32) + b2_ref[b].astype(F32) + b3_ref[b].astype(F32)
         bi_ref[b] = v
         rows.append(v)
     back = split(jnp.concatenate(rows, axis=1))
-    g_ref[...] = gram_of(back, [back, split(lanes(shadow_ref))])
-
-
-def update_kernel(first, last, g_ref, n_ref, image_ref, bi_ref, basis_ref, shadow_ref, precond_ref, res_ref, *refs):
+    g_ref[0:64] = gram_of(back, [back, split(lanes(shadow_ref))])
+
+
+def update_kernel(first, last, f_ref, b_ref, n_ref, image_ref, bi_ref, basis_ref, shadow_ref, precond_ref, res_ref, *refs):
     refs, inv_ref, w_ref = refs[:-2], refs[-2], refs[-1]
     if first:
-        sol_ref, outs = None, refs
+        lt_ref, outs = refs[0], refs[1:]
     else:
         sol_ref, outs = refs[0], refs[1:]
     if last:
@@ -282,13 +306,18 @@
     else:
         sol_out, res_out, basis_out, shadow_out, blow_out, slow_out = outs
     total = n_ref[0]
-    coup_t = g_ref[0:64, 0:64] * (1.0 / total)
+    image_shadow = f_ref[0:64, 0:64]
+    coup_t = image_shadow * (1.0 / total)
     coup = coup_t.T
-    normal = g_ref[0:64, 64:128]
-    target = g_ref[64:128, 0:64]
-    ib = g_ref[64:128, 64:128]
-    bb = g_ref[128:192, 0:64]
-    bs = g_ref[128:192, 64:128]
+    normal = f_ref[0:64, 64:128]
+    bb = b_ref[0:64, 0:64]
+    bs = b_ref[0:64, 64:128]
+    if first:
+        ib = image_shadow
+        target = hdot(image_shadow, lt_ref[...])
+    else:
+        target = jnp.concatenate([f_ref[64:96, 0:64], b_ref[64:96, 0:64]], axis=0)
+        ib = jnp.concatenate([f_ref[64:96, 64:128], b_ref[64:96, 64:128]], axis=0)
     y = hdot(ib, coup)
     uu = normal - y - y.T + total * hdot(coup_t, coup)
     y = hdot(bs, coup_t)
@@ -345,11 +374,20 @@
     live = jnp.arange(m_tiles.shape[0], dtype=jnp.int32) < m_count[0]
     m_local = jnp.where(live, m_rows - first_row, BR)
 
+    is_first_core = jnp.broadcast_to(group % 2 == 0, (1, 128))
+    right_side, a_place, m_place, m_local, n_arr, is_first_core = lax.optimization_barrier(
+        (right_side, a_place, m_place, m_local, n_arr, is_first_core)
+    )
+
     (g0,) = call(start_gram_kernel, "start_gram", [VM], [((K, K), F32)], [], (right_side,))
     g0 = reduce_all(g0)
-    basis, blow = call(
-        start_norm_kernel, "start_norm", [VM, VM, SM], [(blk, F32), (blk, BF16)],
-        [pltpu.VMEM((1, K, K), F32)], (g0, right_side, n_arr)
+    basis, blow, lt = call(
+        start_norm_kernel,
+        "start_norm",
+        [VM, VM, SM],
+        [(blk, F32), (blk, BF16), ((K, K), F32)],
+        [pltpu.VMEM((1, K, K), F32)],
+        (g0, right_side, n_arr),
     )
     shadow, slow = basis, blow
     solution, residual = None, right_side
@@ -399,44 +437,47 @@
             flops=218_000_000,
             nbytes=5_000_000,
         )
-        o0, s1, s2, s3 = call(
+        r = [swap_y(plow, k) for k in (1, 2, 3)]
+        (far,) = call(join_kernel, "join", [VM] * 2, [((16, K, TILE), BF16)], [], (r[1], r[2]))
+        a_zp, a_cp = swap_next(far), swap_core(far)
+        far, pm_own, rm_cp, rm_zp = lax.optimization_barrier((far, pm_own, rm_cp, rm_zp))
+        o0, o1, o2, o3 = call(
             collect_m_kernel,
             "collect_m",
-            [VM] * 4,
-            [(blk, F32)] + [((16, K, TILE), BF16)] * 3,
+            [VM] * 3,
+            [(blk, F32)] + [(blk, BF16)] * 3,
             [],
-            (plow, pm_own, rm_cp, rm_zp),
-        )
-        r = [swap_y(s1, 1), swap_y(s2, 2), swap_y(s3, 3)]
-        (far,) = call(join_kernel, "join", [VM] * 2, [((16, K, TILE), BF16)], [], (r[1], r[2]))
-        a_zp, a_cp = swap_next(far), swap_core(far)
-        image, g_fwd = call(
-            apply_a_kernel,
+            (pm_own, rm_cp, rm_zp),
+        )
+        b1, b2, b3 = swap_y(o1, 1), swap_y(o2, 2), swap_y(o3, 3)
+        first = iteration == 0
+        height = 64 if first else 96
+        image, g_fwd, *rest = call(
+            lambda *refs, f=first: apply_a_kernel(f, *refs),
             "apply_a",
-            [SM] + [VM] * 10,
-            [(blk, F32), ((128, 128), F32)],
+            [SM] + [VM] * (8 if first else 10),
+            [(blk, F32), ((height, 128), F32)] + ([] if first else [((32, 128), F32)]),
             [pltpu.VMEM((64, K, TILE), BF16)],
-            (a_place, plow, *r, a_cp, a_zp, a_tiles, basis, shadow, residual),
+            (a_place, plow, *r, a_cp, a_zp, a_tiles, shadow, *([] if first else [basis, residual])),
             flops=84_000_000,
             nbytes=3_000_000,
         )
         back_image, g_bwd = call(
-            back_gram_kernel,
+            lambda *refs, f=first: back_gram_kernel(f, *refs),
             "back_gram",
-            [VM] * 5,
-            [(blk, F32), ((64, 128), F32)],
+            [VM] * (5 if first else 6),
+            [(blk, F32), ((height, 128), F32)],
             [],
-            (o0, *r, shadow),
-        )
-        grams = reduce_all(jnp.concatenate([g_fwd, g_bwd], 0))
-        args = [grams, n_arr, image, back_image, basis, shadow, precond, residual]
-        if iteration:
-            args.append(solution)
+            (o0, b1, b2, b3, shadow, *rest),
+        )
+        g_fwd, g_bwd = reduce_halves(g_fwd, g_bwd, is_first_core)
+        args = [g_fwd, g_bwd, n_arr, image, back_image, basis, shadow, precond, residual]
+        args.append(lt if first else solution)
         outs = [(blk, F32)] * 4 + ([] if last else [(blk, BF16)] * 2)
         result = call(
             lambda *refs, f=iteration == 0, l=last: update_kernel(f, l, *refs),
             "update",
-            [VM, SM] + [VM] * (len(args) - 2),
+            [VM, VM, SM] + [VM] * (len(args) - 3),
             outs,
             [pltpu.VMEM((3, K, K), F32), pltpu.VMEM((256, 128), F32)],
             args,

time: 249 us -> 239 us (0.960)
  starting transfers between devices: 107 us -> 94.6 us
  waiting for transfers between devices: 84.8 us -> 92.9 us
  local copies, waits for them, and re-layouts: 6.23 us -> 2.36 us
    ppermute x56 -> x64, starting transfers between devices: 101 us -> 89 us  [swap(): return lax.ppermute(value, axis, [(i, i ^ distance) for i in range(size)])]
    ppermute x56 -> x64, waiting for transfers between devices: 84.8 us -> 92.9 us  [swap(): return lax.ppermute(value, axis, [(i, i ^ distance) for i in range(size)])]
    unnamed x22 -> x10, local copies, waits for them, and re-layouts: 6.14 us -> 2.28 us
  transfers between devices with their start and end apart: 64 -> 72, of which waited for: 37 -> 41; matrix products, arithmetic and copies ran while one was open for 1% -> 0% of each run, Pallas kernels for 7% -> 8%
where the time goes in v1:
time: 239 us; the launch traced here: 237 us
  starting transfers between devices  94.6 us (40%)
  waiting for transfers between devices  92.9 us (39%)
  Pallas kernels  43.7 us (18%)
    ppermute x64, waiting for transfers between devices, swap(): return lax.ppermute(value, axis, [(i, i ^ distance) for i in range(size)])  92.9 us
    ppermute x64, starting transfers between devices, swap(): return lax.ppermute(value, axis, [(i, i ^ distance) for i in range(size)])  89 us
    pallas_call x20, Pallas kernels, call(): pl.pallas_call(body, name=name, in_specs=specs, out_specs=tuple((VM for _...  43.7 us
    ppermute x8, starting transfers between devices, swap_next(): return lax.ppermute(value, DOM, route)  5.59 us
  transfers between devices with their start and end apart: 72, of which 41 were waited for; matrix products, arithmetic and copies ran while one was open for 0% of the time, Pallas kernels for 8%

profile of v1, /device:TPU:0, one launch (start us, length us, event | category | flops | bytes accessed | tf_op | source)
XLA Modules:
  0.0 237.3 jit_solution(9971635542850613853)
XLA Ops:
  5.9 3.1 %collective-permute-start.3 = (f32[64,64]{1,0:T(8,128)S(1)}, f32[64,64]{1,0:T(8,128)S(1)}, u32[]{:S(2)}, u32[]{:S(2)}) collective-permute-start(f32[64,64]{1,0:T(8,128)S(1)} %add.154), channel_id=1, source_target_pairs={{0,3},{1,2},{2,1},{3,0},{4,7},{5,6},{6,5},{7,4},{8,11},{9,10},{10,... | collective-permute-start | bytes 49160 | tf_op jit(solution)/shard_map/ppermute | solution.py:30
  11.0 3.4 %collective-permute-done.2 = f32[64,64]{1,0:T(8,128)S(1)} collective-permute-done((f32[64,64]{1,0:T(8,128)S(1)}, f32[64,64]{1,0:T(8,128)S(1)}, u32[]{:S(2)}, u32[]{:S(2)}) %collective-permute-start.2) | collective-permute-done | bytes 16416 | tf_op jit(solution)/shard_map/ppermute | solution.py:30
  14.5 4.1 %collective-permute-start.6 = (f32[64,64]{1,0:T(8,128)S(1)}, f32[64,64]{1,0:T(8,128)S(1)}, u32[]{:S(2)}, u32[]{:S(2)}) collective-permute-start(f32[64,64]{1,0:T(8,128)S(1)} %add_add_fusion.8), channel_id=1, source_target_pairs={{0,24},{4,28},{8,16},{12,20},{16,8},{20,12},{24,0},{28,4},{32,56},... | collective-permute-start | bytes 49160 | tf_op jit(solution)/shard_map/ppermute | solution.py:30
  20.5 3.5 %collective-permute-done.5 = f32[64,64]{1,0:T(8,128)S(1)} collective-permute-done((f32[64,64]{1,0:T(8,128)S(1)}, f32[64,64]{1,0:T(8,128)S(1)}, u32[]{:S(2)}, u32[]{:S(2)}) %collective-permute-start.5) | collective-permute-done | bytes 16416 | tf_op jit(solution)/shard_map/ppermute | solution.py:30
  24.0 2.8 %collective-permute-start.9 = (f32[64,64]{1,0:T(8,128)S(1)}, f32[64,64]{1,0:T(8,128)S(1)}, u32[]{:S(2)}, u32[]{:S(2)}) collective-permute-start(f32[64,64]{1,0:T(8,128)S(1)} %add_add_fusion.7), channel_id=1, source_target_pairs={{0,96},{4,100},{8,104},{12,108},{16,112},{20,116},{24,120},{28,124... | collective-permute-start | bytes 49160 | tf_op jit(solution)/shard_map/ppermute | solution.py:30
  29.2 3.1 %collective-permute-done.8 = f32[64,64]{1,0:T(8,128)S(1)} collective-permute-done((f32[64,64]{1,0:T(8,128)S(1)}, f32[64,64]{1,0:T(8,128)S(1)}, u32[]{:S(2)}, u32[]{:S(2)}) %collective-permute-start.8) | collective-permute-done | bytes 16416 | tf_op jit(solution)/shard_map/ppermute | solution.py:30
  32.3 3.3 %start_norm.1 = (f32[8,64,128]{2,1,0:T(8,128)S(1)}, bf16[8,64,128]{2,1,0:T(8,128)(2,1)S(1)}, f32[64,64]{1,0:T(8,128)S(1)}) custom-call(f32[64,64]{1,0:T(8,128)S(1)} %add_add_fusion.6.g_ref, f32[8,64,128]{2,1,0:T(8,128)S(1)} %copy-done.3, f32[1]{0:T(128)} %constant.108.clone.1.n_ref.refs_2_), custom_call_target="tpu_custom_call" | custom-call | tf_op jit(solution)/shard_map/start_norm/pallas_call | solution.py:76
  43.1 5.4 %collective-permute-done.12.q3_ref = bf16[8,64,128]{2,1,0:T(8,128)(2,1)S(1)} collective-permute-done((bf16[8,64,128]{2,1,0:T(8,128)(2,1)S(1)}, bf16[8,64,128]{2,1,0:T(8,128)(2,1)S(1)}, u32[]{:S(2)}, u32[]{:S(2)}) %collective-permute-start.12) | collective-permute-done | bytes 131104 | tf_op jit(solution)/shard_map/ppermute | solution.py:30
  55.4 4.0 %collective-permute-start.15 = (bf16[32,64,128]{2,1,0:T(8,128)(2,1)S(1)}, bf16[32,64,128]{2,1,0:T(8,128)(2,1)S(1)}, u32[]{:S(2)}, u32[]{:S(2)}) collective-permute-start(bf16[32,64,128]{2,1,0:T(8,128)(2,1)S(1)} %get-tuple-element.78.own_ref), channel_id=1, source_target_pairs={{0,4},{4,0},{8,12},{12,8},{16,20},{20,16},{24,28},{28,24},{32,36},... | collective-permute-start | bytes 1572872 | tf_op jit(solution)/shard_map/ppermute | solution.py:30
  61.7 3.7 %apply_mt.2 = (f32[32,64,128]{2,1,0:T(8,128)S(1)}, bf16[32,64,128]{2,1,0:T(8,128)(2,1)S(1)}, bf16[32,64,128]{2,1,0:T(8,128)(2,1)S(1)}) custom-call(s32[104]{0:T(128)S(1)} %get-tuple-element.70.col_ref, s32[104]{0:T(128)S(1)} %get-tuple-element.71.row_ref, f32[8,64,128]{2,1,0:T(8,128)S(1)} %get-tuple-element.82.back0_ref, ...), custom_call_target="tpu_custom_call" | custom-call | flops 218000000 | bytes 5000000 | tf_op jit(solution)/shard_map/apply_mt/pallas_call | solution.py:76
  66.4 4.4 %apply_m.2 = (f32[8,64,128]{2,1,0:T(8,128)S(1)}, bf16[8,64,128]{2,1,0:T(8,128)(2,1)S(1)}) custom-call(s32[104]{0:T(128)S(1)} %get-tuple-element.70.col_ref, s32[104]{0:T(128)S(1)} %get-tuple-element.71.row_ref, bf16[32,64,128]{2,1,0:T(8,128)(2,1)S(1)} %get-tuple-element.78.own_ref, bf16[32,64,128]{2,1,0:T(8,128)(2,1)S(1)} %collective-permute-done.15.cp_ref, ...), custom_call_target="tpu_custom_call" | custom-call | flops 218000000 | bytes 5000000 | tf_op jit(solution)/shard_map/apply_m/pallas_call | solution.py:76
  72.8 4.9 %collective-permute-done.19.b_ref.refs_4_ = bf16[8,64,128]{2,1,0:T(8,128)(2,1)S(1)} collective-permute-done((bf16[8,64,128]{2,1,0:T(8,128)(2,1)S(1)}, bf16[8,64,128]{2,1,0:T(8,128)(2,1)S(1)}, u32[]{:S(2)}, u32[]{:S(2)}) %collective-permute-start.19) | collective-permute-done | bytes 131104 | tf_op jit(solution)/shard_map/ppermute | solution.py:30
  81.2 4.4 %collective-permute-start.20 = (bf16[16,64,128]{2,1,0:T(8,128)(2,1)S(1)}, bf16[16,64,128]{2,1,0:T(8,128)(2,1)S(1)}, u32[]{:S(2)}, u32[]{:S(2)}) collective-permute-start(bf16[16,64,128]{2,1,0:T(8,128)(2,1)S(1)} %join.2), channel_id=1, source_target_pairs={{0,4},{4,0},{8,12},{12,8},{16,20},{20,16},{24,28},{28,24},{32,36},... | collective-permute-start | bytes 786440 | tf_op jit(solution)/shard_map/ppermute | solution.py:30
  85.6 3.4 %collective-permute-start.28 = (bf16[8,64,128]{2,1,0:T(8,128)(2,1)S(1)}, bf16[8,64,128]{2,1,0:T(8,128)(2,1)S(1)}, u32[]{:S(2)}, u32[]{:S(2)}) collective-permute-start(bf16[8,64,128]{2,1,0:T(8,128)(2,1)S(1)} %get-tuple-element.94), channel_id=1, source_target_pairs={{0,2},{1,3},{2,0},{3,1},{4,6},{5,7},{6,4},{7,5},{8,10},{9,11},{10,... | collective-permute-start | bytes 393224 | tf_op jit(solution)/shard_map/ppermute | solution.py:30
  90.3 2.6 %collective-permute-done.28.refs_2_ = bf16[8,64,128]{2,1,0:T(8,128)(2,1)S(1)} collective-permute-done((bf16[8,64,128]{2,1,0:T(8,128)(2,1)S(1)}, bf16[8,64,128]{2,1,0:T(8,128)(2,1)S(1)}, u32[]{:S(2)}, u32[]{:S(2)}) %collective-permute-start.28) | collective-permute-done | bytes 131104 | tf_op jit(solution)/shard_map/ppermute | solution.py:30
  92.9 2.6 %collective-permute-done.29.refs_3_ = bf16[8,64,128]{2,1,0:T(8,128)(2,1)S(1)} collective-permute-done((bf16[8,64,128]{2,1,0:T(8,128)(2,1)S(1)}, bf16[8,64,128]{2,1,0:T(8,128)(2,1)S(1)}, u32[]{:S(2)}, u32[]{:S(2)}) %collective-permute-start.29) | collective-permute-done | bytes 131104 | tf_op jit(solution)/shard_map/ppermute | solution.py:30
  106.2 3.3 %collective-permute-start.36 = (f32[64,128]{1,0:T(8,128)S(1)}, f32[64,128]{1,0:T(8,128)S(1)}, u32[]{:S(2)}, u32[]{:S(2)}) collective-permute-start(f32[64,128]{1,0:T(8,128)S(1)} %add_add_fusion.5), channel_id=1, source_target_pairs={{0,24},{4,28},{8,16},{12,20},{16,8},{20,12},{24,0},{28,4},{32,56},... | collective-permute-start | bytes 98312 | tf_op jit(solution)/shard_map/ppermute | solution.py:30
  111.4 3.5 %collective-permute-done.35 = f32[64,128]{1,0:T(8,128)S(1)} collective-permute-done((f32[64,128]{1,0:T(8,128)S(1)}, f32[64,128]{1,0:T(8,128)S(1)}, u32[]{:S(2)}, u32[]{:S(2)}) %collective-permute-start.35) | collective-permute-done | bytes 32800 | tf_op jit(solution)/shard_map/ppermute | solution.py:30
  116.5 3.6 %collective-permute-start.38 = (f32[64,128]{1,0:T(8,128)S(1)}, f32[64,128]{1,0:T(8,128)S(1)}, u32[]{:S(2)}, u32[]{:S(2)}) collective-permute-start(f32[64,128]{1,0:T(8,128)S(1)} %add_add_fusion.4), channel_id=1, source_target_pairs={{0,64},{4,68},{8,72},{12,76},{16,80},{20,84},{24,88},{28,92},{32,9... | collective-permute-start | bytes 98312 | tf_op jit(solution)/shard_map/ppermute | solution.py:30
  125.4 8.0 %update.2 = (f32[8,64,128]{2,1,0:T(8,128)S(1)}, f32[8,64,128]{2,1,0:T(8,128)S(1)}, f32[8,64,128]{2,1,0:T(8,128)S(1)}, f32[8,64,128]{2,1,0:T(8,128)S(1)}, bf16[8,...) custom-call(f32[64,128]{1,0:T(8,128)S(1)} %get-tuple-element.135.refs_0_, ...), custom_call_target="tpu_custom_call" | custom-call | tf_op jit(solution)/shard_map/update/pallas_call | solution.py:76
  139.7 5.4 %collective-permute-done.43.q3_ref = bf16[8,64,128]{2,1,0:T(8,128)(2,1)S(1)} collective-permute-done((bf16[8,64,128]{2,1,0:T(8,128)(2,1)S(1)}, bf16[8,64,128]{2,1,0:T(8,128)(2,1)S(1)}, u32[]{:S(2)}, u32[]{:S(2)}) %collective-permute-start.43) | collective-permute-done | bytes 131104 | tf_op jit(solution)/shard_map/ppermute | solution.py:30
  147.4 3.8 %collective-permute-start.46 = (bf16[32,64,128]{2,1,0:T(8,128)(2,1)S(1)}, bf16[32,64,128]{2,1,0:T(8,128)(2,1)S(1)}, u32[]{:S(2)}, u32[]{:S(2)}) collective-permute-start(bf16[32,64,128]{2,1,0:T(8,128)(2,1)S(1)} %get-tuple-element.106.own_ref), channel_id=1, source_target_pairs={{0,4},{4,0},{8,12},{12,8},{16,20},{20,16},{24,28},{28,24},{32,36},... | collective-permute-start | bytes 1572872 | tf_op jit(solution)/shard_map/ppermute | solution.py:30
  157.6 3.2 %collective-permute-done.54.b2_ref = bf16[8,64,128]{2,1,0:T(8,128)(2,1)S(1)} collective-permute-done((bf16[8,64,128]{2,1,0:T(8,128)(2,1)S(1)}, bf16[8,64,128]{2,1,0:T(8,128)(2,1)S(1)}, u32[]{:S(2)}, u32[]{:S(2)}) %collective-permute-start.54) | collective-permute-done | bytes 131104 | tf_op jit(solution)/shard_map/ppermute | solution.py:30
  163.0 3.7 %apply_mt.3 = (f32[32,64,128]{2,1,0:T(8,128)S(1)}, bf16[32,64,128]{2,1,0:T(8,128)(2,1)S(1)}, bf16[32,64,128]{2,1,0:T(8,128)(2,1)S(1)}) custom-call(s32[104]{0:T(128)S(1)} %get-tuple-element.70.col_ref, s32[104]{0:T(128)S(1)} %get-tuple-element.71.row_ref, f32[8,64,128]{2,1,0:T(8,128)S(1)} %get-tuple-element.112.back0_ref, ...), custom_call_target="tpu_custom_call" | custom-call | flops 218000000 | bytes 5000000 | tf_op jit(solution)/shard_map/apply_mt/pallas_call | solution.py:76
  167.7 4.4 %apply_m.3 = (f32[8,64,128]{2,1,0:T(8,128)S(1)}, bf16[8,64,128]{2,1,0:T(8,128)(2,1)S(1)}) custom-call(s32[104]{0:T(128)S(1)} %get-tuple-element.70.col_ref, s32[104]{0:T(128)S(1)} %get-tuple-element.71.row_ref, bf16[32,64,128]{2,1,0:T(8,128)(2,1)S(1)} %get-tuple-element.106.own_ref, bf16[32,64,128]{2,1,0:T(8,128)(2,1)S(1)} %collective-permute-done.46.cp_ref, ...), custom_call_target="tpu_custom_call" | custom-call | flops 218000000 | bytes 5000000 | tf_op jit(solution)/shard_map/apply_m/pallas_call | solution.py:76
  173.7 8.1 %collective-permute-done.50.b_ref.refs_4_ = bf16[8,64,128]{2,1,0:T(8,128)(2,1)S(1)} collective-permute-done((bf16[8,64,128]{2,1,0:T(8,128)(2,1)S(1)}, bf16[8,64,128]{2,1,0:T(8,128)(2,1)S(1)}, u32[]{:S(2)}, u32[]{:S(2)}) %collective-permute-start.50) | collective-permute-done | bytes 131104 | tf_op jit(solution)/shard_map/ppermute | solution.py:30
  182.6 5.4 %collective-permute-start.51 = (bf16[16,64,128]{2,1,0:T(8,128)(2,1)S(1)}, bf16[16,64,128]{2,1,0:T(8,128)(2,1)S(1)}, u32[]{:S(2)}, u32[]{:S(2)}) collective-permute-start(bf16[16,64,128]{2,1,0:T(8,128)(2,1)S(1)} %join.3), channel_id=1, source_target_pairs={{0,4},{4,0},{8,12},{12,8},{16,20},{20,16},{24,28},{28,24},{32,36},... | collective-permute-start | bytes 786440 | tf_op jit(solution)/shard_map/ppermute | solution.py:30
  191.4 3.0 %collective-permute-done.48.refs_2_ = bf16[8,64,128]{2,1,0:T(8,128)(2,1)S(1)} collective-permute-done((bf16[8,64,128]{2,1,0:T(8,128)(2,1)S(1)}, bf16[8,64,128]{2,1,0:T(8,128)(2,1)S(1)}, u32[]{:S(2)}, u32[]{:S(2)}) %collective-permute-start.48) | collective-permute-done | bytes 131104 | tf_op jit(solution)/shard_map/ppermute | solution.py:30
  197.6 2.6 %collective-permute-done.59.refs_2_ = bf16[8,64,128]{2,1,0:T(8,128)(2,1)S(1)} collective-permute-done((bf16[8,64,128]{2,1,0:T(8,128)(2,1)S(1)}, bf16[8,64,128]{2,1,0:T(8,128)(2,1)S(1)}, u32[]{:S(2)}, u32[]{:S(2)}) %collective-permute-start.59) | collective-permute-done | bytes 131104 | tf_op jit(solution)/shard_map/ppermute | solution.py:30
  211.1 3.1 %collective-permute-start.67 = (f32[96,128]{1,0:T(8,128)S(1)}, f32[96,128]{1,0:T(8,128)S(1)}, u32[]{:S(2)}, u32[]{:S(2)}) collective-permute-start(f32[96,128]{1,0:T(8,128)S(1)} %add_add_fusion.2), channel_id=1, source_target_pairs={{0,24},{4,28},{8,16},{12,20},{16,8},{20,12},{24,0},{28,4},{32,56},... | collective-permute-start | bytes 147464 | tf_op jit(solution)/shard_map/ppermute | solution.py:30
  216.4 3.3 %collective-permute-done.66 = f32[96,128]{1,0:T(8,128)S(1)} collective-permute-done((f32[96,128]{1,0:T(8,128)S(1)}, f32[96,128]{1,0:T(8,128)S(1)}, u32[]{:S(2)}, u32[]{:S(2)}) %collective-permute-start.66) | collective-permute-done | bytes 49184 | tf_op jit(solution)/shard_map/ppermute | solution.py:30
  228.5 8.8 %update.3 = (f32[8,64,128]{2,1,0:T(8,128)}, f32[8,64,128]{2,1,0:T(8,128)}, f32[8,64,128]{2,1,0:T(8,128)}, f32[8,64,128]{2,1,0:T(8,128)}) custom-call(f32[96,128]{1,0:T(8,128)S(1)} %get-tuple-element.133.refs_0_, f32[96,128]{1,0:T(8,128)S(1)} %get-tuple-element.132.refs_1_, f32[1]{0:T(128)} %constant.108.clone.1.n_ref.refs_2_, ...), custom_call_target="tpu_custom_call" | custom-call | tf_op jit(solution)/shard_map/update/pallas_call | solution.py:76
  (162 shorter events, 103.1 us)
Async XLA Ops:
  38.1 11.7 %collective-permute-start.13 = (bf16[16,64,128]{2,1,0:T(8,128)(2,1)S(1)}, bf16[16,64,128]{2,1,0:T(8,128)(2,1)S(1)}, u32[]{:S(2)}, u32[]{:S(2)}) collective-permute-start(bf16[16,64,128]{2,1,0:T(8,128)(2,1)S(1)} %get-tuple-element.76), channel_id=1, source_target_pairs={{0,4},{4,0},{8,12},{12,8},{16,20},{20,16},{24,28},{28,24},{32,36},... | collective-permute-start | bytes 786440 | tf_op jit(solution)/shard_map/ppermute | solution.py:30
  38.2 11.6 %collective-permute-start.14 = (bf16[16,64,128]{2,1,0:T(8,128)(2,1)S(1)}, bf16[16,64,128]{2,1,0:T(8,128)(2,1)S(1)}, u32[]{:S(2)}, u32[]{:S(2)}) collective-permute-start(bf16[16,64,128]{2,1,0:T(8,128)(2,1)S(1)} %get-tuple-element.77), channel_id=1, source_target_pairs={{4,8},{8,4},{12,16},{16,12},{20,24},{24,20},{28,32},{32,28},{36,40... | collective-permute-start | bytes 786440 | tf_op jit(solution)/shard_map/ppermute | solution.py:46
  38.9 9.6 %collective-permute-start.12 = (bf16[8,64,128]{2,1,0:T(8,128)(2,1)S(1)}, bf16[8,64,128]{2,1,0:T(8,128)(2,1)S(1)}, u32[]{:S(2)}, u32[]{:S(2)}) collective-permute-start(bf16[8,64,128]{2,1,0:T(8,128)(2,1)S(1)} %get-tuple-element.74.low_ref), channel_id=1, source_target_pairs={{0,3},{1,2},{2,1},{3,0},{4,7},{5,6},{6,5},{7,4},{8,11},{9,10},{10,... | collective-permute-start | bytes 393224 | tf_op jit(solution)/shard_map/ppermute | solution.py:30
  40.3 8.2 %collective-permute-start.11 = (bf16[8,64,128]{2,1,0:T(8,128)(2,1)S(1)}, bf16[8,64,128]{2,1,0:T(8,128)(2,1)S(1)}, u32[]{:S(2)}, u32[]{:S(2)}) collective-permute-start(bf16[8,64,128]{2,1,0:T(8,128)(2,1)S(1)} %get-tuple-element.74.low_ref), channel_id=1, source_target_pairs={{0,2},{1,3},{2,0},{3,1},{4,6},{5,7},{6,4},{7,5},{8,10},{9,11},{10,... | collective-permute-start | bytes 393224 | tf_op jit(solution)/shard_map/ppermute | solution.py:30
  41.5 8.3 %collective-permute-start.10 = (bf16[8,64,128]{2,1,0:T(8,128)(2,1)S(1)}, bf16[8,64,128]{2,1,0:T(8,128)(2,1)S(1)}, u32[]{:S(2)}, u32[]{:S(2)}) collective-permute-start(bf16[8,64,128]{2,1,0:T(8,128)(2,1)S(1)} %get-tuple-element.74.low_ref), channel_id=1, source_target_pairs={{0,1},{1,0},{2,3},{3,2},{4,5},{5,4},{6,7},{7,6},{8,9},{9,8},{10,11... | collective-permute-start | bytes 393224 | tf_op jit(solution)/shard_map/ppermute | solution.py:30
  50.0 9.4 %collective-permute-start.22 = (bf16[8,64,128]{2,1,0:T(8,128)(2,1)S(1)}, bf16[8,64,128]{2,1,0:T(8,128)(2,1)S(1)}, u32[]{:S(2)}, u32[]{:S(2)}) collective-permute-start(bf16[8,64,128]{2,1,0:T(8,128)(2,1)S(1)} %get-tuple-element.83), channel_id=1, source_target_pairs={{0,1},{1,0},{2,3},{3,2},{4,5},{5,4},{6,7},{7,6},{8,9},{9,8},{10,11... | collective-permute-start | bytes 393224 | tf_op jit(solution)/shard_map/ppermute | solution.py:30
  50.4 9.0 %collective-permute-start.23 = (bf16[8,64,128]{2,1,0:T(8,128)(2,1)S(1)}, bf16[8,64,128]{2,1,0:T(8,128)(2,1)S(1)}, u32[]{:S(2)}, u32[]{:S(2)}) collective-permute-start(bf16[8,64,128]{2,1,0:T(8,128)(2,1)S(1)} %get-tuple-element.84), channel_id=1, source_target_pairs={{0,2},{1,3},{2,0},{3,1},{4,6},{5,7},{6,4},{7,5},{8,10},{9,11},{10,... | collective-permute-start | bytes 393224 | tf_op jit(solution)/shard_map/ppermute | solution.py:30
  52.8 8.9 %collective-permute-start.24 = (bf16[8,64,128]{2,1,0:T(8,128)(2,1)S(1)}, bf16[8,64,128]{2,1,0:T(8,128)(2,1)S(1)}, u32[]{:S(2)}, u32[]{:S(2)}) collective-permute-start(bf16[8,64,128]{2,1,0:T(8,128)(2,1)S(1)} %get-tuple-element.85), channel_id=1, source_target_pairs={{0,3},{1,2},{2,1},{3,0},{4,7},{5,6},{6,5},{7,4},{8,11},{9,10},{10,... | collective-permute-start | bytes 393224 | tf_op jit(solution)/shard_map/ppermute | solution.py:30
  54.7 11.6 %collective-permute-start.16 = (bf16[32,64,128]{2,1,0:T(8,128)(2,1)S(1)}, bf16[32,64,128]{2,1,0:T(8,128)(2,1)S(1)}, u32[]{:S(2)}, u32[]{:S(2)}) collective-permute-start(bf16[32,64,128]{2,1,0:T(8,128)(2,1)S(1)} %get-tuple-element.78.own_ref), channel_id=1, source_target_pairs={{4,8},{8,4},{12,16},{16,12},{20,24},{24,20},{28,32},{32,28},{36,40... | collective-permute-start | bytes 1572872 | tf_op jit(solution)/shard_map/ppermute | solution.py:46
  55.4 10.9 %collective-permute-start.15 = (bf16[32,64,128]{2,1,0:T(8,128)(2,1)S(1)}, bf16[32,64,128]{2,1,0:T(8,128)(2,1)S(1)}, u32[]{:S(2)}, u32[]{:S(2)}) collective-permute-start(bf16[32,64,128]{2,1,0:T(8,128)(2,1)S(1)} %get-tuple-element.78.own_ref), channel_id=1, source_target_pairs={{0,4},{4,0},{8,12},{12,8},{16,20},{20,16},{24,28},{28,24},{32,36},... | collective-permute-start | bytes 1572872 | tf_op jit(solution)/shard_map/ppermute | solution.py:30
  65.4 14.9 %collective-permute-start.25 = (bf16[32,64,128]{2,1,0:T(8,128)(2,1)S(1)}, bf16[32,64,128]{2,1,0:T(8,128)(2,1)S(1)}, u32[]{:S(2)}, u32[]{:S(2)}) collective-permute-start(bf16[32,64,128]{2,1,0:T(8,128)(2,1)S(1)} %get-tuple-element.87), channel_id=1, source_target_pairs={{0,4},{4,0},{8,12},{12,8},{16,20},{20,16},{24,28},{28,24},{32,36},... | collective-permute-start | bytes 1572872 | tf_op jit(solution)/shard_map/ppermute | solution.py:30
  65.5 14.8 %collective-permute-start.26 = (bf16[32,64,128]{2,1,0:T(8,128)(2,1)S(1)}, bf16[32,64,128]{2,1,0:T(8,128)(2,1)S(1)}, u32[]{:S(2)}, u32[]{:S(2)}) collective-permute-start(bf16[32,64,128]{2,1,0:T(8,128)(2,1)S(1)} %get-tuple-element.88), channel_id=1, source_target_pairs={{4,8},{8,4},{12,16},{16,12},{20,24},{24,20},{28,32},{32,28},{36,40... | collective-permute-start | bytes 1572872 | tf_op jit(solution)/shard_map/ppermute | solution.py:46
  80.5 9.8 %collective-permute-start.27 = (bf16[8,64,128]{2,1,0:T(8,128)(2,1)S(1)}, bf16[8,64,128]{2,1,0:T(8,128)(2,1)S(1)}, u32[]{:S(2)}, u32[]{:S(2)}) collective-permute-start(bf16[8,64,128]{2,1,0:T(8,128)(2,1)S(1)} %get-tuple-element.93), channel_id=1, source_target_pairs={{0,1},{1,0},{2,3},{3,2},{4,5},{5,4},{6,7},{7,6},{8,9},{9,8},{10,11... | collective-permute-start | bytes 393224 | tf_op jit(solution)/shard_map/ppermute | solution.py:30
  80.6 15.3 %collective-permute-start.21 = (bf16[16,64,128]{2,1,0:T(8,128)(2,1)S(1)}, bf16[16,64,128]{2,1,0:T(8,128)(2,1)S(1)}, u32[]{:S(2)}, u32[]{:S(2)}) collective-permute-start(bf16[16,64,128]{2,1,0:T(8,128)(2,1)S(1)} %join.2), channel_id=1, source_target_pairs={{4,8},{8,4},{12,16},{16,12},{20,24},{24,20},{28,32},{32,28},{36,40... | collective-permute-start | bytes 786440 | tf_op jit(solution)/shard_map/ppermute | solution.py:46
  81.2 14.6 %collective-permute-start.20 = (bf16[16,64,128]{2,1,0:T(8,128)(2,1)S(1)}, bf16[16,64,128]{2,1,0:T(8,128)(2,1)S(1)}, u32[]{:S(2)}, u32[]{:S(2)}) collective-permute-start(bf16[16,64,128]{2,1,0:T(8,128)(2,1)S(1)} %join.2), channel_id=1, source_target_pairs={{0,4},{4,0},{8,12},{12,8},{16,20},{20,16},{24,28},{28,24},{32,36},... | collective-permute-start | bytes 786440 | tf_op jit(solution)/shard_map/ppermute | solution.py:30
  134.6 11.9 %collective-permute-start.44 = (bf16[16,64,128]{2,1,0:T(8,128)(2,1)S(1)}, bf16[16,64,128]{2,1,0:T(8,128)(2,1)S(1)}, u32[]{:S(2)}, u32[]{:S(2)}) collective-permute-start(bf16[16,64,128]{2,1,0:T(8,128)(2,1)S(1)} %get-tuple-element.104), channel_id=1, source_target_pairs={{0,4},{4,0},{8,12},{12,8},{16,20},{20,16},{24,28},{28,24},{32,36},... | collective-permute-start | bytes 786440 | tf_op jit(solution)/shard_map/ppermute | solution.py:30
  134.8 11.7 %collective-permute-start.45 = (bf16[16,64,128]{2,1,0:T(8,128)(2,1)S(1)}, bf16[16,64,128]{2,1,0:T(8,128)(2,1)S(1)}, u32[]{:S(2)}, u32[]{:S(2)}) collective-permute-start(bf16[16,64,128]{2,1,0:T(8,128)(2,1)S(1)} %get-tuple-element.105), channel_id=1, source_target_pairs={{4,8},{8,4},{12,16},{16,12},{20,24},{24,20},{28,32},{32,28},{36,40... | collective-permute-start | bytes 786440 | tf_op jit(solution)/shard_map/ppermute | solution.py:46
  135.5 9.6 %collective-permute-start.43 = (bf16[8,64,128]{2,1,0:T(8,128)(2,1)S(1)}, bf16[8,64,128]{2,1,0:T(8,128)(2,1)S(1)}, u32[]{:S(2)}, u32[]{:S(2)}) collective-permute-start(bf16[8,64,128]{2,1,0:T(8,128)(2,1)S(1)} %get-tuple-element.101.low_ref), channel_id=1, source_target_pairs={{0,3},{1,2},{2,1},{3,0},{4,7},{5,6},{6,5},{7,4},{8,11},{9,10},{10,... | collective-permute-start | bytes 393224 | tf_op jit(solution)/shard_map/ppermute | solution.py:30
  137.3 7.8 %collective-permute-start.42 = (bf16[8,64,128]{2,1,0:T(8,128)(2,1)S(1)}, bf16[8,64,128]{2,1,0:T(8,128)(2,1)S(1)}, u32[]{:S(2)}, u32[]{:S(2)}) collective-permute-start(bf16[8,64,128]{2,1,0:T(8,128)(2,1)S(1)} %get-tuple-element.101.low_ref), channel_id=1, source_target_pairs={{0,2},{1,3},{2,0},{3,1},{4,6},{5,7},{6,4},{7,5},{8,10},{9,11},{10,... | collective-permute-start | bytes 393224 | tf_op jit(solution)/shard_map/ppermute | solution.py:30
  138.5 8.0 %collective-permute-start.41 = (bf16[8,64,128]{2,1,0:T(8,128)(2,1)S(1)}, bf16[8,64,128]{2,1,0:T(8,128)(2,1)S(1)}, u32[]{:S(2)}, u32[]{:S(2)}) collective-permute-start(bf16[8,64,128]{2,1,0:T(8,128)(2,1)S(1)} %get-tuple-element.101.low_ref), channel_id=1, source_target_pairs={{0,1},{1,0},{2,3},{3,2},{4,5},{5,4},{6,7},{7,6},{8,9},{9,8},{10,11... | collective-permute-start | bytes 393224 | tf_op jit(solution)/shard_map/ppermute | solution.py:30
  146.7 21.0 %collective-permute-start.47 = (bf16[32,64,128]{2,1,0:T(8,128)(2,1)S(1)}, bf16[32,64,128]{2,1,0:T(8,128)(2,1)S(1)}, u32[]{:S(2)}, u32[]{:S(2)}) collective-permute-start(bf16[32,64,128]{2,1,0:T(8,128)(2,1)S(1)} %get-tuple-element.106.own_ref), channel_id=1, source_target_pairs={{4,8},{8,4},{12,16},{16,12},{20,24},{24,20},{28,32},{32,28},{36,40... | collective-permute-start | bytes 1572872 | tf_op jit(solution)/shard_map/ppermute | solution.py:46
  147.4 20.3 %collective-permute-start.46 = (bf16[32,64,128]{2,1,0:T(8,128)(2,1)S(1)}, bf16[32,64,128]{2,1,0:T(8,128)(2,1)S(1)}, u32[]{:S(2)}, u32[]{:S(2)}) collective-permute-start(bf16[32,64,128]{2,1,0:T(8,128)(2,1)S(1)} %get-tuple-element.106.own_ref), channel_id=1, source_target_pairs={{0,4},{4,0},{8,12},{12,8},{16,20},{20,16},{24,28},{28,24},{32,36},... | collective-permute-start | bytes 1572872 | tf_op jit(solution)/shard_map/ppermute | solution.py:30
  152.1 8.7 %collective-permute-start.54 = (bf16[8,64,128]{2,1,0:T(8,128)(2,1)S(1)}, bf16[8,64,128]{2,1,0:T(8,128)(2,1)S(1)}, u32[]{:S(2)}, u32[]{:S(2)}) collective-permute-start(bf16[8,64,128]{2,1,0:T(8,128)(2,1)S(1)} %get-tuple-element.114), channel_id=1, source_target_pairs={{0,2},{1,3},{2,0},{3,1},{4,6},{5,7},{6,4},{7,5},{8,10},{9,11},{10,... | collective-permute-start | bytes 393224 | tf_op jit(solution)/shard_map/ppermute | solution.py:30
  154.4 8.6 %collective-permute-start.55 = (bf16[8,64,128]{2,1,0:T(8,128)(2,1)S(1)}, bf16[8,64,128]{2,1,0:T(8,128)(2,1)S(1)}, u32[]{:S(2)}, u32[]{:S(2)}) collective-permute-start(bf16[8,64,128]{2,1,0:T(8,128)(2,1)S(1)} %get-tuple-element.115), channel_id=1, source_target_pairs={{0,3},{1,2},{2,1},{3,0},{4,7},{5,6},{6,5},{7,4},{8,11},{9,10},{10,... | collective-permute-start | bytes 393224 | tf_op jit(solution)/shard_map/ppermute | solution.py:30
  166.7 21.3 %collective-permute-start.56 = (bf16[32,64,128]{2,1,0:T(8,128)(2,1)S(1)}, bf16[32,64,128]{2,1,0:T(8,128)(2,1)S(1)}, u32[]{:S(2)}, u32[]{:S(2)}) collective-permute-start(bf16[32,64,128]{2,1,0:T(8,128)(2,1)S(1)} %get-tuple-element.117), channel_id=1, source_target_pairs={{0,4},{4,0},{8,12},{12,8},{16,20},{20,16},{24,28},{28,24},{32,36},... | collective-permute-start | bytes 1572872 | tf_op jit(solution)/shard_map/ppermute | solution.py:30
  167.0 21.0 %collective-permute-start.57 = (bf16[32,64,128]{2,1,0:T(8,128)(2,1)S(1)}, bf16[32,64,128]{2,1,0:T(8,128)(2,1)S(1)}, u32[]{:S(2)}, u32[]{:S(2)}) collective-permute-start(bf16[32,64,128]{2,1,0:T(8,128)(2,1)S(1)} %get-tuple-element.118), channel_id=1, source_target_pairs={{4,8},{8,4},{12,16},{16,12},{20,24},{24,20},{28,32},{32,28},{36,40... | collective-permute-start | bytes 1572872 | tf_op jit(solution)/shard_map/ppermute | solution.py:46
  172.2 9.7 %collective-permute-start.50 = (bf16[8,64,128]{2,1,0:T(8,128)(2,1)S(1)}, bf16[8,64,128]{2,1,0:T(8,128)(2,1)S(1)}, u32[]{:S(2)}, u32[]{:S(2)}) collective-permute-start(bf16[8,64,128]{2,1,0:T(8,128)(2,1)S(1)} %get-tuple-element.107.refs_1_), channel_id=1, source_target_pairs={{0,3},{1,2},{2,1},{3,0},{4,7},{5,6},{6,5},{7,4},{8,11},{9,10},{10,... | collective-permute-start | bytes 393224 | tf_op jit(solution)/shard_map/ppermute | solution.py:30
  173.7 8.1 %collective-permute-start.49 = (bf16[8,64,128]{2,1,0:T(8,128)(2,1)S(1)}, bf16[8,64,128]{2,1,0:T(8,128)(2,1)S(1)}, u32[]{:S(2)}, u32[]{:S(2)}) collective-permute-start(bf16[8,64,128]{2,1,0:T(8,128)(2,1)S(1)} %get-tuple-element.107.refs_1_), channel_id=1, source_target_pairs={{0,2},{1,3},{2,0},{3,1},{4,6},{5,7},{6,4},{7,5},{8,10},{9,11},{10,... | collective-permute-start | bytes 393224 | tf_op jit(solution)/shard_map/ppermute | solution.py:30
  181.9 14.0 %collective-permute-start.52 = (bf16[16,64,128]{2,1,0:T(8,128)(2,1)S(1)}, bf16[16,64,128]{2,1,0:T(8,128)(2,1)S(1)}, u32[]{:S(2)}, u32[]{:S(2)}) collective-permute-start(bf16[16,64,128]{2,1,0:T(8,128)(2,1)S(1)} %join.3), channel_id=1, source_target_pairs={{4,8},{8,4},{12,16},{16,12},{20,24},{24,20},{28,32},{32,28},{36,40... | collective-permute-start | bytes 786440 | tf_op jit(solution)/shard_map/ppermute | solution.py:46
  182.6 13.3 %collective-permute-start.51 = (bf16[16,64,128]{2,1,0:T(8,128)(2,1)S(1)}, bf16[16,64,128]{2,1,0:T(8,128)(2,1)S(1)}, u32[]{:S(2)}, u32[]{:S(2)}) collective-permute-start(bf16[16,64,128]{2,1,0:T(8,128)(2,1)S(1)} %join.3), channel_id=1, source_target_pairs={{0,4},{4,0},{8,12},{12,8},{16,20},{20,16},{24,28},{28,24},{32,36},... | collective-permute-start | bytes 786440 | tf_op jit(solution)/shard_map/ppermute | solution.py:30
  188.2 9.3 %collective-permute-start.58 = (bf16[8,64,128]{2,1,0:T(8,128)(2,1)S(1)}, bf16[8,64,128]{2,1,0:T(8,128)(2,1)S(1)}, u32[]{:S(2)}, u32[]{:S(2)}) collective-permute-start(bf16[8,64,128]{2,1,0:T(8,128)(2,1)S(1)} %get-tuple-element.123), channel_id=1, source_target_pairs={{0,1},{1,0},{2,3},{3,2},{4,5},{5,4},{6,7},{7,6},{8,9},{9,8},{10,11... | collective-permute-start | bytes 393224 | tf_op jit(solution)/shard_map/ppermute | solution.py:30
  190.3 9.9 %collective-permute-start.59 = (bf16[8,64,128]{2,1,0:T(8,128)(2,1)S(1)}, bf16[8,64,128]{2,1,0:T(8,128)(2,1)S(1)}, u32[]{:S(2)}, u32[]{:S(2)}) collective-permute-start(bf16[8,64,128]{2,1,0:T(8,128)(2,1)S(1)} %get-tuple-element.124), channel_id=1, source_target_pairs={{0,2},{1,3},{2,0},{3,1},{4,6},{5,7},{6,4},{7,5},{8,10},{9,11},{10,... | collective-permute-start | bytes 393224 | tf_op jit(solution)/shard_map/ppermute | solution.py:30
  (45 other events, 349.2 us)

commit v2 on v1

--- a/solution.py
+++ b/solution.py
@@ -15,7 +15,7 @@
 F32 = jnp.float32
 BF16 = jnp.bfloat16
 DOM, BAL = "dom", "bal"
-UNROLL = 8
+UNROLL = 26
 
 
 def hdot(a, b, dims=NN):
@@ -318,10 +318,8 @@
     else:
         target = jnp.concatenate([f_ref[64:96, 0:64], b_ref[64:96, 0:64]], axis=0)
         ib = jnp.concatenate([f_ref[64:96, 64:128], b_ref[64:96, 64:128]], axis=0)
-    y = hdot(ib, coup)
-    uu = normal - y - y.T + total * hdot(coup_t, coup)
-    y = hdot(bs, coup_t)
-    ss = bb - y - y.T + total * hdot(coup, coup_t)
+    uu = normal - hdot(ib, coup_t, NT) - hdot(coup_t, ib, NT) + total * hdot(coup_t, coup_t, NT)
+    ss = bb - hdot(bs, coup_t) - hdot(coup, bs, NT) + total * hdot(coup_t, coup_t, TN)
     inverse_factors([normal, uu * (1.0 / total), ss * (1.0 / total)], inv_ref)
     inv_n, inv_u, inv_s = inv_ref[0], inv_ref[1], inv_ref[2]
     w_t = hdot(hdot(inv_n, target), inv_n, TN)
@@ -331,12 +329,9 @@
     w_ref[64:128, 64:128] = jnp.zeros((K, K), F32)
     w_ref[128:192, 0:64] = inv_s
     w_ref[128:192, 64:128] = -hdot(inv_s, coup)
-    w_ref[192:256, 0:64] = w_t
-    w_ref[192:256, 64:128] = jnp.zeros((K, K), F32)
-    zero = jnp.zeros((K, BR * TILE), BF16)
     first_two = combine(w_ref[0:128], [split(lanes(image_ref)), split(lanes(basis_ref))])
     third = combine(w_ref[128:192], [split(lanes(bi_ref)), split(lanes(shadow_ref))])
-    fourth = combine(w_ref[192:256], [split(lanes(precond_ref)), (zero, zero)])
+    fourth = combine(w_t, [split(lanes(precond_ref))])
     for b in range(BR):
         at = slice(b * TILE, (b + 1) * TILE)
         v = fourth[:, at]
@@ -479,7 +474,7 @@
             "update",
             [VM, VM, SM] + [VM] * (len(args) - 3),
             outs,
-            [pltpu.VMEM((3, K, K), F32), pltpu.VMEM((256, 128), F32)],
+            [pltpu.VMEM((3, K, K), F32), pltpu.VMEM((192, 128), F32)],
             args,
             final=last,
         )

time: 239 us -> 234 us (0.979)
  Pallas kernels: 43.7 us -> 39.2 us
    pallas_call x20, Pallas kernels: 43.7 us -> 39.2 us  [call(): pl.pallas_call(body, name=name, in_specs=specs, out_specs=tuple((VM for _...]
  transfers between devices with their start and end apart: 72 -> 72, of which waited for: 41 -> 42; matrix products, arithmetic and copies ran while one was open for 0% -> 0% of each run, Pallas kernels for 8% -> 6%
where the time goes in v2:
time: 234 us; the launch traced here: 233 us
  starting transfers between devices  94.4 us (40%)
  waiting for transfers between devices  92.9 us (40%)
  Pallas kernels  39.2 us (17%)
  local copies, waits for them, and re-layouts  2.36 us (1%)
    ppermute x64, waiting for transfers between devices, swap(): return lax.ppermute(value, axis, [(i, i ^ distance) for i in range(size)])  92.9 us
    ppermute x64, starting transfers between devices, swap(): return lax.ppermute(value, axis, [(i, i ^ distance) for i in range(size)])  88.8 us
    pallas_call x20, Pallas kernels, call(): pl.pallas_call(body, name=name, in_specs=specs, out_specs=tuple((VM for _...  39.2 us
    ppermute x8, starting transfers between devices, swap_next(): return lax.ppermute(value, DOM, route)  5.59 us
  transfers between devices with their start and end apart: 72, of which 42 were waited for; matrix products, arithmetic and copies ran while one was open for 0% of the time, Pallas kernels for 6%

profile of v2, /device:TPU:0, one launch (start us, length us, event | category | flops | bytes accessed | tf_op | source)
XLA Modules:
  0.0 232.6 jit_solution(15475264110772051355)
XLA Ops:
  5.9 3.1 %collective-permute-start.3 = (f32[64,64]{1,0:T(8,128)S(1)}, f32[64,64]{1,0:T(8,128)S(1)}, u32[]{:S(2)}, u32[]{:S(2)}) collective-permute-start(f32[64,64]{1,0:T(8,128)S(1)} %add.154), channel_id=1, source_target_pairs={{0,3},{1,2},{2,1},{3,0},{4,7},{5,6},{6,5},{7,4},{8,11},{9,10},{10,... | collective-permute-start | bytes 49160 | tf_op jit(solution)/shard_map/ppermute | solution.py:30
  11.0 3.4 %collective-permute-done.2 = f32[64,64]{1,0:T(8,128)S(1)} collective-permute-done((f32[64,64]{1,0:T(8,128)S(1)}, f32[64,64]{1,0:T(8,128)S(1)}, u32[]{:S(2)}, u32[]{:S(2)}) %collective-permute-start.2) | collective-permute-done | bytes 16416 | tf_op jit(solution)/shard_map/ppermute | solution.py:30
  14.5 4.1 %collective-permute-start.6 = (f32[64,64]{1,0:T(8,128)S(1)}, f32[64,64]{1,0:T(8,128)S(1)}, u32[]{:S(2)}, u32[]{:S(2)}) collective-permute-start(f32[64,64]{1,0:T(8,128)S(1)} %add_add_fusion.8), channel_id=1, source_target_pairs={{0,24},{4,28},{8,16},{12,20},{16,8},{20,12},{24,0},{28,4},{32,56},... | collective-permute-start | bytes 49160 | tf_op jit(solution)/shard_map/ppermute | solution.py:30
  20.5 3.5 %collective-permute-done.5 = f32[64,64]{1,0:T(8,128)S(1)} collective-permute-done((f32[64,64]{1,0:T(8,128)S(1)}, f32[64,64]{1,0:T(8,128)S(1)}, u32[]{:S(2)}, u32[]{:S(2)}) %collective-permute-start.5) | collective-permute-done | bytes 16416 | tf_op jit(solution)/shard_map/ppermute | solution.py:30
  24.0 2.8 %collective-permute-start.9 = (f32[64,64]{1,0:T(8,128)S(1)}, f32[64,64]{1,0:T(8,128)S(1)}, u32[]{:S(2)}, u32[]{:S(2)}) collective-permute-start(f32[64,64]{1,0:T(8,128)S(1)} %add_add_fusion.7), channel_id=1, source_target_pairs={{0,96},{4,100},{8,104},{12,108},{16,112},{20,116},{24,120},{28,124... | collective-permute-start | bytes 49160 | tf_op jit(solution)/shard_map/ppermute | solution.py:30
  29.2 3.1 %collective-permute-done.8 = f32[64,64]{1,0:T(8,128)S(1)} collective-permute-done((f32[64,64]{1,0:T(8,128)S(1)}, f32[64,64]{1,0:T(8,128)S(1)}, u32[]{:S(2)}, u32[]{:S(2)}) %collective-permute-start.8) | collective-permute-done | bytes 16416 | tf_op jit(solution)/shard_map/ppermute | solution.py:30
  32.3 3.3 %start_norm.1 = (f32[8,64,128]{2,1,0:T(8,128)S(1)}, bf16[8,64,128]{2,1,0:T(8,128)(2,1)S(1)}, f32[64,64]{1,0:T(8,128)S(1)}) custom-call(f32[64,64]{1,0:T(8,128)S(1)} %add_add_fusion.6.g_ref, f32[8,64,128]{2,1,0:T(8,128)S(1)} %copy-done.3, f32[1]{0:T(128)} %constant.108.clone.1.n_ref.refs_2_), custom_call_target="tpu_custom_call" | custom-call | tf_op jit(solution)/shard_map/start_norm/pallas_call | solution.py:76
  43.1 5.5 %collective-permute-done.12.q3_ref = bf16[8,64,128]{2,1,0:T(8,128)(2,1)S(1)} collective-permute-done((bf16[8,64,128]{2,1,0:T(8,128)(2,1)S(1)}, bf16[8,64,128]{2,1,0:T(8,128)(2,1)S(1)}, u32[]{:S(2)}, u32[]{:S(2)}) %collective-permute-start.12) | collective-permute-done | bytes 131104 | tf_op jit(solution)/shard_map/ppermute | solution.py:30
  55.4 4.0 %collective-permute-start.15 = (bf16[32,64,128]{2,1,0:T(8,128)(2,1)S(1)}, bf16[32,64,128]{2,1,0:T(8,128)(2,1)S(1)}, u32[]{:S(2)}, u32[]{:S(2)}) collective-permute-start(bf16[32,64,128]{2,1,0:T(8,128)(2,1)S(1)} %get-tuple-element.78.own_ref), channel_id=1, source_target_pairs={{0,4},{4,0},{8,12},{12,8},{16,20},{20,16},{24,28},{28,24},{32,36},... | collective-permute-start | bytes 1572872 | tf_op jit(solution)/shard_map/ppermute | solution.py:30
  65.1 3.4 %apply_m.2 = (f32[8,64,128]{2,1,0:T(8,128)S(1)}, bf16[8,64,128]{2,1,0:T(8,128)(2,1)S(1)}) custom-call(s32[104]{0:T(128)S(1)} %get-tuple-element.70.col_ref, s32[104]{0:T(128)S(1)} %get-tuple-element.71.row_ref, bf16[32,64,128]{2,1,0:T(8,128)(2,1)S(1)} %get-tuple-element.78.own_ref, bf16[32,64,128]{2,1,0:T(8,128)(2,1)S(1)} %collective-permute-done.15.cp_ref, ...), custom_call_target="tpu_custom_call" | custom-call | flops 218000000 | bytes 5000000 | tf_op jit(solution)/shard_map/apply_m/pallas_call | solution.py:76
  70.6 4.9 %collective-permute-done.19.b_ref.refs_4_ = bf16[8,64,128]{2,1,0:T(8,128)(2,1)S(1)} collective-permute-done((bf16[8,64,128]{2,1,0:T(8,128)(2,1)S(1)}, bf16[8,64,128]{2,1,0:T(8,128)(2,1)S(1)}, u32[]{:S(2)}, u32[]{:S(2)}) %collective-permute-start.19) | collective-permute-done | bytes 131104 | tf_op jit(solution)/shard_map/ppermute | solution.py:30
  75.4 2.6 %collective-permute-done.18.a_ref.refs_3_ = bf16[8,64,128]{2,1,0:T(8,128)(2,1)S(1)} collective-permute-done((bf16[8,64,128]{2,1,0:T(8,128)(2,1)S(1)}, bf16[8,64,128]{2,1,0:T(8,128)(2,1)S(1)}, u32[]{:S(2)}, u32[]{:S(2)}) %collective-permute-start.18) | collective-permute-done | bytes 131104 | tf_op jit(solution)/shard_map/ppermute | solution.py:30
  79.0 4.3 %collective-permute-start.20 = (bf16[16,64,128]{2,1,0:T(8,128)(2,1)S(1)}, bf16[16,64,128]{2,1,0:T(8,128)(2,1)S(1)}, u32[]{:S(2)}, u32[]{:S(2)}) collective-permute-start(bf16[16,64,128]{2,1,0:T(8,128)(2,1)S(1)} %join.2), channel_id=1, source_target_pairs={{0,4},{4,0},{8,12},{12,8},{16,20},{20,16},{24,28},{28,24},{32,36},... | collective-permute-start | bytes 786440 | tf_op jit(solution)/shard_map/ppermute | solution.py:30
  83.4 3.4 %collective-permute-start.28 = (bf16[8,64,128]{2,1,0:T(8,128)(2,1)S(1)}, bf16[8,64,128]{2,1,0:T(8,128)(2,1)S(1)}, u32[]{:S(2)}, u32[]{:S(2)}) collective-permute-start(bf16[8,64,128]{2,1,0:T(8,128)(2,1)S(1)} %get-tuple-element.94), channel_id=1, source_target_pairs={{0,2},{1,3},{2,0},{3,1},{4,6},{5,7},{6,4},{7,5},{8,10},{9,11},{10,... | collective-permute-start | bytes 393224 | tf_op jit(solution)/shard_map/ppermute | solution.py:30
  88.0 2.6 %collective-permute-done.28.refs_2_ = bf16[8,64,128]{2,1,0:T(8,128)(2,1)S(1)} collective-permute-done((bf16[8,64,128]{2,1,0:T(8,128)(2,1)S(1)}, bf16[8,64,128]{2,1,0:T(8,128)(2,1)S(1)}, u32[]{:S(2)}, u32[]{:S(2)}) %collective-permute-start.28) | collective-permute-done | bytes 131104 | tf_op jit(solution)/shard_map/ppermute | solution.py:30
  90.6 2.6 %collective-permute-done.29.refs_3_ = bf16[8,64,128]{2,1,0:T(8,128)(2,1)S(1)} collective-permute-done((bf16[8,64,128]{2,1,0:T(8,128)(2,1)S(1)}, bf16[8,64,128]{2,1,0:T(8,128)(2,1)S(1)}, u32[]{:S(2)}, u32[]{:S(2)}) %collective-permute-start.29) | collective-permute-done | bytes 131104 | tf_op jit(solution)/shard_map/ppermute | solution.py:30
  104.0 3.3 %collective-permute-start.36 = (f32[64,128]{1,0:T(8,128)S(1)}, f32[64,128]{1,0:T(8,128)S(1)}, u32[]{:S(2)}, u32[]{:S(2)}) collective-permute-start(f32[64,128]{1,0:T(8,128)S(1)} %add_add_fusion.5), channel_id=1, source_target_pairs={{0,24},{4,28},{8,16},{12,20},{16,8},{20,12},{24,0},{28,4},{32,56},... | collective-permute-start | bytes 98312 | tf_op jit(solution)/shard_map/ppermute | solution.py:30
  109.2 3.5 %collective-permute-done.35 = f32[64,128]{1,0:T(8,128)S(1)} collective-permute-done((f32[64,128]{1,0:T(8,128)S(1)}, f32[64,128]{1,0:T(8,128)S(1)}, u32[]{:S(2)}, u32[]{:S(2)}) %collective-permute-start.35) | collective-permute-done | bytes 32800 | tf_op jit(solution)/shard_map/ppermute | solution.py:30
  114.2 3.5 %collective-permute-start.38 = (f32[64,128]{1,0:T(8,128)S(1)}, f32[64,128]{1,0:T(8,128)S(1)}, u32[]{:S(2)}, u32[]{:S(2)}) collective-permute-start(f32[64,128]{1,0:T(8,128)S(1)} %add_add_fusion.4), channel_id=1, source_target_pairs={{0,64},{4,68},{8,72},{12,76},{16,80},{20,84},{24,88},{28,92},{32,9... | collective-permute-start | bytes 98312 | tf_op jit(solution)/shard_map/ppermute | solution.py:30
  122.9 8.0 %update.2 = (f32[8,64,128]{2,1,0:T(8,128)S(1)}, f32[8,64,128]{2,1,0:T(8,128)S(1)}, f32[8,64,128]{2,1,0:T(8,128)S(1)}, f32[8,64,128]{2,1,0:T(8,128)S(1)}, bf16[8,...) custom-call(f32[64,128]{1,0:T(8,128)S(1)} %get-tuple-element.135.refs_0_, ...), custom_call_target="tpu_custom_call" | custom-call | tf_op jit(solution)/shard_map/update/pallas_call | solution.py:76
  137.2 5.4 %collective-permute-done.43.q3_ref = bf16[8,64,128]{2,1,0:T(8,128)(2,1)S(1)} collective-permute-done((bf16[8,64,128]{2,1,0:T(8,128)(2,1)S(1)}, bf16[8,64,128]{2,1,0:T(8,128)(2,1)S(1)}, u32[]{:S(2)}, u32[]{:S(2)}) %collective-permute-start.43) | collective-permute-done | bytes 131104 | tf_op jit(solution)/shard_map/ppermute | solution.py:30
  144.9 3.8 %collective-permute-start.46 = (bf16[32,64,128]{2,1,0:T(8,128)(2,1)S(1)}, bf16[32,64,128]{2,1,0:T(8,128)(2,1)S(1)}, u32[]{:S(2)}, u32[]{:S(2)}) collective-permute-start(bf16[32,64,128]{2,1,0:T(8,128)(2,1)S(1)} %get-tuple-element.106.own_ref), channel_id=1, source_target_pairs={{0,4},{4,0},{8,12},{12,8},{16,20},{20,16},{24,28},{28,24},{32,36},... | collective-permute-start | bytes 1572872 | tf_op jit(solution)/shard_map/ppermute | solution.py:30
  155.1 3.2 %collective-permute-done.54.b2_ref = bf16[8,64,128]{2,1,0:T(8,128)(2,1)S(1)} collective-permute-done((bf16[8,64,128]{2,1,0:T(8,128)(2,1)S(1)}, bf16[8,64,128]{2,1,0:T(8,128)(2,1)S(1)}, u32[]{:S(2)}, u32[]{:S(2)}) %collective-permute-start.54) | collective-permute-done | bytes 131104 | tf_op jit(solution)/shard_map/ppermute | solution.py:30
  163.8 3.4 %apply_m.3 = (f32[8,64,128]{2,1,0:T(8,128)S(1)}, bf16[8,64,128]{2,1,0:T(8,128)(2,1)S(1)}) custom-call(s32[104]{0:T(128)S(1)} %get-tuple-element.70.col_ref, s32[104]{0:T(128)S(1)} %get-tuple-element.71.row_ref, bf16[32,64,128]{2,1,0:T(8,128)(2,1)S(1)} %get-tuple-element.106.own_ref, bf16[32,64,128]{2,1,0:T(8,128)(2,1)S(1)} %collective-permute-done.46.cp_ref, ...), custom_call_target="tpu_custom_call" | custom-call | flops 218000000 | bytes 5000000 | tf_op jit(solution)/shard_map/apply_m/pallas_call | solution.py:76
  168.8 8.1 %collective-permute-done.50.b_ref.refs_4_ = bf16[8,64,128]{2,1,0:T(8,128)(2,1)S(1)} collective-permute-done((bf16[8,64,128]{2,1,0:T(8,128)(2,1)S(1)}, bf16[8,64,128]{2,1,0:T(8,128)(2,1)S(1)}, u32[]{:S(2)}, u32[]{:S(2)}) %collective-permute-start.50) | collective-permute-done | bytes 131104 | tf_op jit(solution)/shard_map/ppermute | solution.py:30
  177.7 5.4 %collective-permute-start.51 = (bf16[16,64,128]{2,1,0:T(8,128)(2,1)S(1)}, bf16[16,64,128]{2,1,0:T(8,128)(2,1)S(1)}, u32[]{:S(2)}, u32[]{:S(2)}) collective-permute-start(bf16[16,64,128]{2,1,0:T(8,128)(2,1)S(1)} %join.3), channel_id=1, source_target_pairs={{0,4},{4,0},{8,12},{12,8},{16,20},{20,16},{24,28},{28,24},{32,36},... | collective-permute-start | bytes 786440 | tf_op jit(solution)/shard_map/ppermute | solution.py:30
  186.4 3.0 %collective-permute-done.48.refs_2_ = bf16[8,64,128]{2,1,0:T(8,128)(2,1)S(1)} collective-permute-done((bf16[8,64,128]{2,1,0:T(8,128)(2,1)S(1)}, bf16[8,64,128]{2,1,0:T(8,128)(2,1)S(1)}, u32[]{:S(2)}, u32[]{:S(2)}) %collective-permute-start.48) | collective-permute-done | bytes 131104 | tf_op jit(solution)/shard_map/ppermute | solution.py:30
  192.6 2.6 %collective-permute-done.59.refs_2_ = bf16[8,64,128]{2,1,0:T(8,128)(2,1)S(1)} collective-permute-done((bf16[8,64,128]{2,1,0:T(8,128)(2,1)S(1)}, bf16[8,64,128]{2,1,0:T(8,128)(2,1)S(1)}, u32[]{:S(2)}, u32[]{:S(2)}) %collective-permute-start.59) | collective-permute-done | bytes 131104 | tf_op jit(solution)/shard_map/ppermute | solution.py:30
  200.5 2.5 %collective-permute-start.62 = (f32[96,128]{1,0:T(8,128)S(1)}, f32[96,128]{1,0:T(8,128)S(1)}, u32[]{:S(2)}, u32[]{:S(2)}) collective-permute-start(f32[96,128]{1,0:T(8,128)S(1)} %select_add_fusion), channel_id=1, source_target_pairs={{0,1},{1,0},{2,3},{3,2},{4,5},{5,4},{6,7},{7,6},{8,9},{9,8},{10,11... | collective-permute-start | bytes 147464 | tf_op jit(solution)/shard_map/ppermute | solution.py:30
  206.1 3.1 %collective-permute-start.67 = (f32[96,128]{1,0:T(8,128)S(1)}, f32[96,128]{1,0:T(8,128)S(1)}, u32[]{:S(2)}, u32[]{:S(2)}) collective-permute-start(f32[96,128]{1,0:T(8,128)S(1)} %add_add_fusion.2), channel_id=1, source_target_pairs={{0,24},{4,28},{8,16},{12,20},{16,8},{20,12},{24,0},{28,4},{32,56},... | collective-permute-start | bytes 147464 | tf_op jit(solution)/shard_map/ppermute | solution.py:30
  211.5 3.3 %collective-permute-done.66 = f32[96,128]{1,0:T(8,128)S(1)} collective-permute-done((f32[96,128]{1,0:T(8,128)S(1)}, f32[96,128]{1,0:T(8,128)S(1)}, u32[]{:S(2)}, u32[]{:S(2)}) %collective-permute-start.66) | collective-permute-done | bytes 49184 | tf_op jit(solution)/shard_map/ppermute | solution.py:30
  223.8 8.8 %update.3 = (f32[8,64,128]{2,1,0:T(8,128)}, f32[8,64,128]{2,1,0:T(8,128)}, f32[8,64,128]{2,1,0:T(8,128)}, f32[8,64,128]{2,1,0:T(8,128)}) custom-call(f32[96,128]{1,0:T(8,128)S(1)} %get-tuple-element.133.refs_0_, f32[96,128]{1,0:T(8,128)S(1)} %get-tuple-element.132.refs_1_, f32[1]{0:T(128)} %constant.108.clone.1.n_ref.refs_2_, ...), custom_call_target="tpu_custom_call" | custom-call | tf_op jit(solution)/shard_map/update/pallas_call | solution.py:76
  (162 shorter events, 102.8 us)
Async XLA Ops:
  38.1 11.7 %collective-permute-start.13 = (bf16[16,64,128]{2,1,0:T(8,128)(2,1)S(1)}, bf16[16,64,128]{2,1,0:T(8,128)(2,1)S(1)}, u32[]{:S(2)}, u32[]{:S(2)}) collective-permute-start(bf16[16,64,128]{2,1,0:T(8,128)(2,1)S(1)} %get-tuple-element.76), channel_id=1, source_target_pairs={{0,4},{4,0},{8,12},{12,8},{16,20},{20,16},{24,28},{28,24},{32,36},... | collective-permute-start | bytes 786440 | tf_op jit(solution)/shard_map/ppermute | solution.py:30
  38.2 11.6 %collective-permute-start.14 = (bf16[16,64,128]{2,1,0:T(8,128)(2,1)S(1)}, bf16[16,64,128]{2,1,0:T(8,128)(2,1)S(1)}, u32[]{:S(2)}, u32[]{:S(2)}) collective-permute-start(bf16[16,64,128]{2,1,0:T(8,128)(2,1)S(1)} %get-tuple-element.77), channel_id=1, source_target_pairs={{4,8},{8,4},{12,16},{16,12},{20,24},{24,20},{28,32},{32,28},{36,40... | collective-permute-start | bytes 786440 | tf_op jit(solution)/shard_map/ppermute | solution.py:46
  38.9 9.6 %collective-permute-start.12 = (bf16[8,64,128]{2,1,0:T(8,128)(2,1)S(1)}, bf16[8,64,128]{2,1,0:T(8,128)(2,1)S(1)}, u32[]{:S(2)}, u32[]{:S(2)}) collective-permute-start(bf16[8,64,128]{2,1,0:T(8,128)(2,1)S(1)} %get-tuple-element.74.low_ref), channel_id=1, source_target_pairs={{0,3},{1,2},{2,1},{3,0},{4,7},{5,6},{6,5},{7,4},{8,11},{9,10},{10,... | collective-permute-start | bytes 393224 | tf_op jit(solution)/shard_map/ppermute | solution.py:30
  40.3 8.3 %collective-permute-start.11 = (bf16[8,64,128]{2,1,0:T(8,128)(2,1)S(1)}, bf16[8,64,128]{2,1,0:T(8,128)(2,1)S(1)}, u32[]{:S(2)}, u32[]{:S(2)}) collective-permute-start(bf16[8,64,128]{2,1,0:T(8,128)(2,1)S(1)} %get-tuple-element.74.low_ref), channel_id=1, source_target_pairs={{0,2},{1,3},{2,0},{3,1},{4,6},{5,7},{6,4},{7,5},{8,10},{9,11},{10,... | collective-permute-start | bytes 393224 | tf_op jit(solution)/shard_map/ppermute | solution.py:30
  41.5 8.3 %collective-permute-start.10 = (bf16[8,64,128]{2,1,0:T(8,128)(2,1)S(1)}, bf16[8,64,128]{2,1,0:T(8,128)(2,1)S(1)}, u32[]{:S(2)}, u32[]{:S(2)}) collective-permute-start(bf16[8,64,128]{2,1,0:T(8,128)(2,1)S(1)} %get-tuple-element.74.low_ref), channel_id=1, source_target_pairs={{0,1},{1,0},{2,3},{3,2},{4,5},{5,4},{6,7},{7,6},{8,9},{9,8},{10,11... | collective-permute-start | bytes 393224 | tf_op jit(solution)/shard_map/ppermute | solution.py:30
  50.0 9.4 %collective-permute-start.22 = (bf16[8,64,128]{2,1,0:T(8,128)(2,1)S(1)}, bf16[8,64,128]{2,1,0:T(8,128)(2,1)S(1)}, u32[]{:S(2)}, u32[]{:S(2)}) collective-permute-start(bf16[8,64,128]{2,1,0:T(8,128)(2,1)S(1)} %get-tuple-element.83), channel_id=1, source_target_pairs={{0,1},{1,0},{2,3},{3,2},{4,5},{5,4},{6,7},{7,6},{8,9},{9,8},{10,11... | collective-permute-start | bytes 393224 | tf_op jit(solution)/shard_map/ppermute | solution.py:30
  50.4 9.0 %collective-permute-start.23 = (bf16[8,64,128]{2,1,0:T(8,128)(2,1)S(1)}, bf16[8,64,128]{2,1,0:T(8,128)(2,1)S(1)}, u32[]{:S(2)}, u32[]{:S(2)}) collective-permute-start(bf16[8,64,128]{2,1,0:T(8,128)(2,1)S(1)} %get-tuple-element.84), channel_id=1, source_target_pairs={{0,2},{1,3},{2,0},{3,1},{4,6},{5,7},{6,4},{7,5},{8,10},{9,11},{10,... | collective-permute-start | bytes 393224 | tf_op jit(solution)/shard_map/ppermute | solution.py:30
  52.8 8.9 %collective-permute-start.24 = (bf16[8,64,128]{2,1,0:T(8,128)(2,1)S(1)}, bf16[8,64,128]{2,1,0:T(8,128)(2,1)S(1)}, u32[]{:S(2)}, u32[]{:S(2)}) collective-permute-start(bf16[8,64,128]{2,1,0:T(8,128)(2,1)S(1)} %get-tuple-element.85), channel_id=1, source_target_pairs={{0,3},{1,2},{2,1},{3,0},{4,7},{5,6},{6,5},{7,4},{8,11},{9,10},{10,... | collective-permute-start | bytes 393224 | tf_op jit(solution)/shard_map/ppermute | solution.py:30
  54.7 10.3 %collective-permute-start.16 = (bf16[32,64,128]{2,1,0:T(8,128)(2,1)S(1)}, bf16[32,64,128]{2,1,0:T(8,128)(2,1)S(1)}, u32[]{:S(2)}, u32[]{:S(2)}) collective-permute-start(bf16[32,64,128]{2,1,0:T(8,128)(2,1)S(1)} %get-tuple-element.78.own_ref), channel_id=1, source_target_pairs={{4,8},{8,4},{12,16},{16,12},{20,24},{24,20},{28,32},{32,28},{36,40... | collective-permute-start | bytes 1572872 | tf_op jit(solution)/shard_map/ppermute | solution.py:46
  55.4 9.6 %collective-permute-start.15 = (bf16[32,64,128]{2,1,0:T(8,128)(2,1)S(1)}, bf16[32,64,128]{2,1,0:T(8,128)(2,1)S(1)}, u32[]{:S(2)}, u32[]{:S(2)}) collective-permute-start(bf16[32,64,128]{2,1,0:T(8,128)(2,1)S(1)} %get-tuple-element.78.own_ref), channel_id=1, source_target_pairs={{0,4},{4,0},{8,12},{12,8},{16,20},{20,16},{24,28},{28,24},{32,36},... | collective-permute-start | bytes 1572872 | tf_op jit(solution)/shard_map/ppermute | solution.py:30
  64.1 13.9 %collective-permute-start.25 = (bf16[32,64,128]{2,1,0:T(8,128)(2,1)S(1)}, bf16[32,64,128]{2,1,0:T(8,128)(2,1)S(1)}, u32[]{:S(2)}, u32[]{:S(2)}) collective-permute-start(bf16[32,64,128]{2,1,0:T(8,128)(2,1)S(1)} %get-tuple-element.87), channel_id=1, source_target_pairs={{0,4},{4,0},{8,12},{12,8},{16,20},{20,16},{24,28},{28,24},{32,36},... | collective-permute-start | bytes 1572872 | tf_op jit(solution)/shard_map/ppermute | solution.py:30
  64.2 13.8 %collective-permute-start.26 = (bf16[32,64,128]{2,1,0:T(8,128)(2,1)S(1)}, bf16[32,64,128]{2,1,0:T(8,128)(2,1)S(1)}, u32[]{:S(2)}, u32[]{:S(2)}) collective-permute-start(bf16[32,64,128]{2,1,0:T(8,128)(2,1)S(1)} %get-tuple-element.88), channel_id=1, source_target_pairs={{4,8},{8,4},{12,16},{16,12},{20,24},{24,20},{28,32},{32,28},{36,40... | collective-permute-start | bytes 1572872 | tf_op jit(solution)/shard_map/ppermute | solution.py:46
  78.2 9.8 %collective-permute-start.27 = (bf16[8,64,128]{2,1,0:T(8,128)(2,1)S(1)}, bf16[8,64,128]{2,1,0:T(8,128)(2,1)S(1)}, u32[]{:S(2)}, u32[]{:S(2)}) collective-permute-start(bf16[8,64,128]{2,1,0:T(8,128)(2,1)S(1)} %get-tuple-element.93), channel_id=1, source_target_pairs={{0,1},{1,0},{2,3},{3,2},{4,5},{5,4},{6,7},{7,6},{8,9},{9,8},{10,11... | collective-permute-start | bytes 393224 | tf_op jit(solution)/shard_map/ppermute | solution.py:30
  78.3 15.3 %collective-permute-start.21 = (bf16[16,64,128]{2,1,0:T(8,128)(2,1)S(1)}, bf16[16,64,128]{2,1,0:T(8,128)(2,1)S(1)}, u32[]{:S(2)}, u32[]{:S(2)}) collective-permute-start(bf16[16,64,128]{2,1,0:T(8,128)(2,1)S(1)} %join.2), channel_id=1, source_target_pairs={{4,8},{8,4},{12,16},{16,12},{20,24},{24,20},{28,32},{32,28},{36,40... | collective-permute-start | bytes 786440 | tf_op jit(solution)/shard_map/ppermute | solution.py:46
  79.0 14.6 %collective-permute-start.20 = (bf16[16,64,128]{2,1,0:T(8,128)(2,1)S(1)}, bf16[16,64,128]{2,1,0:T(8,128)(2,1)S(1)}, u32[]{:S(2)}, u32[]{:S(2)}) collective-permute-start(bf16[16,64,128]{2,1,0:T(8,128)(2,1)S(1)} %join.2), channel_id=1, source_target_pairs={{0,4},{4,0},{8,12},{12,8},{16,20},{20,16},{24,28},{28,24},{32,36},... | collective-permute-start | bytes 786440 | tf_op jit(solution)/shard_map/ppermute | solution.py:30
  132.1 11.9 %collective-permute-start.44 = (bf16[16,64,128]{2,1,0:T(8,128)(2,1)S(1)}, bf16[16,64,128]{2,1,0:T(8,128)(2,1)S(1)}, u32[]{:S(2)}, u32[]{:S(2)}) collective-permute-start(bf16[16,64,128]{2,1,0:T(8,128)(2,1)S(1)} %get-tuple-element.104), channel_id=1, source_target_pairs={{0,4},{4,0},{8,12},{12,8},{16,20},{20,16},{24,28},{28,24},{32,36},... | collective-permute-start | bytes 786440 | tf_op jit(solution)/shard_map/ppermute | solution.py:30
  132.4 11.7 %collective-permute-start.45 = (bf16[16,64,128]{2,1,0:T(8,128)(2,1)S(1)}, bf16[16,64,128]{2,1,0:T(8,128)(2,1)S(1)}, u32[]{:S(2)}, u32[]{:S(2)}) collective-permute-start(bf16[16,64,128]{2,1,0:T(8,128)(2,1)S(1)} %get-tuple-element.105), channel_id=1, source_target_pairs={{4,8},{8,4},{12,16},{16,12},{20,24},{24,20},{28,32},{32,28},{36,40... | collective-permute-start | bytes 786440 | tf_op jit(solution)/shard_map/ppermute | solution.py:46
  133.0 9.6 %collective-permute-start.43 = (bf16[8,64,128]{2,1,0:T(8,128)(2,1)S(1)}, bf16[8,64,128]{2,1,0:T(8,128)(2,1)S(1)}, u32[]{:S(2)}, u32[]{:S(2)}) collective-permute-start(bf16[8,64,128]{2,1,0:T(8,128)(2,1)S(1)} %get-tuple-element.101.low_ref), channel_id=1, source_target_pairs={{0,3},{1,2},{2,1},{3,0},{4,7},{5,6},{6,5},{7,4},{8,11},{9,10},{10,... | collective-permute-start | bytes 393224 | tf_op jit(solution)/shard_map/ppermute | solution.py:30
  134.8 7.8 %collective-permute-start.42 = (bf16[8,64,128]{2,1,0:T(8,128)(2,1)S(1)}, bf16[8,64,128]{2,1,0:T(8,128)(2,1)S(1)}, u32[]{:S(2)}, u32[]{:S(2)}) collective-permute-start(bf16[8,64,128]{2,1,0:T(8,128)(2,1)S(1)} %get-tuple-element.101.low_ref), channel_id=1, source_target_pairs={{0,2},{1,3},{2,0},{3,1},{4,6},{5,7},{6,4},{7,5},{8,10},{9,11},{10,... | collective-permute-start | bytes 393224 | tf_op jit(solution)/shard_map/ppermute | solution.py:30
  136.1 8.0 %collective-permute-start.41 = (bf16[8,64,128]{2,1,0:T(8,128)(2,1)S(1)}, bf16[8,64,128]{2,1,0:T(8,128)(2,1)S(1)}, u32[]{:S(2)}, u32[]{:S(2)}) collective-permute-start(bf16[8,64,128]{2,1,0:T(8,128)(2,1)S(1)} %get-tuple-element.101.low_ref), channel_id=1, source_target_pairs={{0,1},{1,0},{2,3},{3,2},{4,5},{5,4},{6,7},{7,6},{8,9},{9,8},{10,11... | collective-permute-start | bytes 393224 | tf_op jit(solution)/shard_map/ppermute | solution.py:30
  144.2 19.5 %collective-permute-start.47 = (bf16[32,64,128]{2,1,0:T(8,128)(2,1)S(1)}, bf16[32,64,128]{2,1,0:T(8,128)(2,1)S(1)}, u32[]{:S(2)}, u32[]{:S(2)}) collective-permute-start(bf16[32,64,128]{2,1,0:T(8,128)(2,1)S(1)} %get-tuple-element.106.own_ref), channel_id=1, source_target_pairs={{4,8},{8,4},{12,16},{16,12},{20,24},{24,20},{28,32},{32,28},{36,40... | collective-permute-start | bytes 1572872 | tf_op jit(solution)/shard_map/ppermute | solution.py:46
  144.9 18.9 %collective-permute-start.46 = (bf16[32,64,128]{2,1,0:T(8,128)(2,1)S(1)}, bf16[32,64,128]{2,1,0:T(8,128)(2,1)S(1)}, u32[]{:S(2)}, u32[]{:S(2)}) collective-permute-start(bf16[32,64,128]{2,1,0:T(8,128)(2,1)S(1)} %get-tuple-element.106.own_ref), channel_id=1, source_target_pairs={{0,4},{4,0},{8,12},{12,8},{16,20},{20,16},{24,28},{28,24},{32,36},... | collective-permute-start | bytes 1572872 | tf_op jit(solution)/shard_map/ppermute | solution.py:30
  149.6 8.7 %collective-permute-start.54 = (bf16[8,64,128]{2,1,0:T(8,128)(2,1)S(1)}, bf16[8,64,128]{2,1,0:T(8,128)(2,1)S(1)}, u32[]{:S(2)}, u32[]{:S(2)}) collective-permute-start(bf16[8,64,128]{2,1,0:T(8,128)(2,1)S(1)} %get-tuple-element.114), channel_id=1, source_target_pairs={{0,2},{1,3},{2,0},{3,1},{4,6},{5,7},{6,4},{7,5},{8,10},{9,11},{10,... | collective-permute-start | bytes 393224 | tf_op jit(solution)/shard_map/ppermute | solution.py:30
  151.9 8.6 %collective-permute-start.55 = (bf16[8,64,128]{2,1,0:T(8,128)(2,1)S(1)}, bf16[8,64,128]{2,1,0:T(8,128)(2,1)S(1)}, u32[]{:S(2)}, u32[]{:S(2)}) collective-permute-start(bf16[8,64,128]{2,1,0:T(8,128)(2,1)S(1)} %get-tuple-element.115), channel_id=1, source_target_pairs={{0,3},{1,2},{2,1},{3,0},{4,7},{5,6},{6,5},{7,4},{8,11},{9,10},{10,... | collective-permute-start | bytes 393224 | tf_op jit(solution)/shard_map/ppermute | solution.py:30
  163.0 20.1 %collective-permute-start.56 = (bf16[32,64,128]{2,1,0:T(8,128)(2,1)S(1)}, bf16[32,64,128]{2,1,0:T(8,128)(2,1)S(1)}, u32[]{:S(2)}, u32[]{:S(2)}) collective-permute-start(bf16[32,64,128]{2,1,0:T(8,128)(2,1)S(1)} %get-tuple-element.117), channel_id=1, source_target_pairs={{0,4},{4,0},{8,12},{12,8},{16,20},{20,16},{24,28},{28,24},{32,36},... | collective-permute-start | bytes 1572872 | tf_op jit(solution)/shard_map/ppermute | solution.py:30
  163.0 20.0 %collective-permute-start.57 = (bf16[32,64,128]{2,1,0:T(8,128)(2,1)S(1)}, bf16[32,64,128]{2,1,0:T(8,128)(2,1)S(1)}, u32[]{:S(2)}, u32[]{:S(2)}) collective-permute-start(bf16[32,64,128]{2,1,0:T(8,128)(2,1)S(1)} %get-tuple-element.118), channel_id=1, source_target_pairs={{4,8},{8,4},{12,16},{16,12},{20,24},{24,20},{28,32},{32,28},{36,40... | collective-permute-start | bytes 1572872 | tf_op jit(solution)/shard_map/ppermute | solution.py:46
  167.2 9.7 %collective-permute-start.50 = (bf16[8,64,128]{2,1,0:T(8,128)(2,1)S(1)}, bf16[8,64,128]{2,1,0:T(8,128)(2,1)S(1)}, u32[]{:S(2)}, u32[]{:S(2)}) collective-permute-start(bf16[8,64,128]{2,1,0:T(8,128)(2,1)S(1)} %get-tuple-element.107.refs_1_), channel_id=1, source_target_pairs={{0,3},{1,2},{2,1},{3,0},{4,7},{5,6},{6,5},{7,4},{8,11},{9,10},{10,... | collective-permute-start | bytes 393224 | tf_op jit(solution)/shard_map/ppermute | solution.py:30
  168.8 8.1 %collective-permute-start.49 = (bf16[8,64,128]{2,1,0:T(8,128)(2,1)S(1)}, bf16[8,64,128]{2,1,0:T(8,128)(2,1)S(1)}, u32[]{:S(2)}, u32[]{:S(2)}) collective-permute-start(bf16[8,64,128]{2,1,0:T(8,128)(2,1)S(1)} %get-tuple-element.107.refs_1_), channel_id=1, source_target_pairs={{0,2},{1,3},{2,0},{3,1},{4,6},{5,7},{6,4},{7,5},{8,10},{9,11},{10,... | collective-permute-start | bytes 393224 | tf_op jit(solution)/shard_map/ppermute | solution.py:30
  177.0 14.0 %collective-permute-start.52 = (bf16[16,64,128]{2,1,0:T(8,128)(2,1)S(1)}, bf16[16,64,128]{2,1,0:T(8,128)(2,1)S(1)}, u32[]{:S(2)}, u32[]{:S(2)}) collective-permute-start(bf16[16,64,128]{2,1,0:T(8,128)(2,1)S(1)} %join.3), channel_id=1, source_target_pairs={{4,8},{8,4},{12,16},{16,12},{20,24},{24,20},{28,32},{32,28},{36,40... | collective-permute-start | bytes 786440 | tf_op jit(solution)/shard_map/ppermute | solution.py:46
  177.7 13.3 %collective-permute-start.51 = (bf16[16,64,128]{2,1,0:T(8,128)(2,1)S(1)}, bf16[16,64,128]{2,1,0:T(8,128)(2,1)S(1)}, u32[]{:S(2)}, u32[]{:S(2)}) collective-permute-start(bf16[16,64,128]{2,1,0:T(8,128)(2,1)S(1)} %join.3), channel_id=1, source_target_pairs={{0,4},{4,0},{8,12},{12,8},{16,20},{20,16},{24,28},{28,24},{32,36},... | collective-permute-start | bytes 786440 | tf_op jit(solution)/shard_map/ppermute | solution.py:30
  183.3 9.3 %collective-permute-start.58 = (bf16[8,64,128]{2,1,0:T(8,128)(2,1)S(1)}, bf16[8,64,128]{2,1,0:T(8,128)(2,1)S(1)}, u32[]{:S(2)}, u32[]{:S(2)}) collective-permute-start(bf16[8,64,128]{2,1,0:T(8,128)(2,1)S(1)} %get-tuple-element.123), channel_id=1, source_target_pairs={{0,1},{1,0},{2,3},{3,2},{4,5},{5,4},{6,7},{7,6},{8,9},{9,8},{10,11... | collective-permute-start | bytes 393224 | tf_op jit(solution)/shard_map/ppermute | solution.py:30
  185.4 9.9 %collective-permute-start.59 = (bf16[8,64,128]{2,1,0:T(8,128)(2,1)S(1)}, bf16[8,64,128]{2,1,0:T(8,128)(2,1)S(1)}, u32[]{:S(2)}, u32[]{:S(2)}) collective-permute-start(bf16[8,64,128]{2,1,0:T(8,128)(2,1)S(1)} %get-tuple-element.124), channel_id=1, source_target_pairs={{0,2},{1,3},{2,0},{3,1},{4,6},{5,7},{6,4},{7,5},{8,10},{9,11},{10,... | collective-permute-start | bytes 393224 | tf_op jit(solution)/shard_map/ppermute | solution.py:30
  (45 other events, 348.3 us)

commit v3 on v2

--- a/solution.py
+++ b/solution.py
@@ -4,6 +4,7 @@
 from jax.experimental import pallas as pl
 from jax.experimental.pallas import tpu as pltpu
 from jax.sharding import PartitionSpec as P
+
 
 ITERS = 2
 BR = 8
@@ -71,11 +72,10 @@
 SM = pl.BlockSpec(memory_space=pltpu.SMEM)
 
 
-def call(body, name, specs, outs, scratch, args, flops=0, nbytes=0, final=False):
+def call(body, specs, outs, scratch, args, flops=0, nbytes=0, final=False):
     args = [pltpu.with_memory_space_constraint(a, pltpu.VMEM) if s is VM else a for s, a in zip(specs, args)]
     return pl.pallas_call(
         body,
-        name=name,
         in_specs=specs,
         out_specs=tuple(VM for _ in outs),
         out_shape=tuple(jax.ShapeDtypeStruct(s, d) if final else pltpu.VMEM(s, d) for s, d in outs),
@@ -320,7 +320,9 @@
         ib = jnp.concatenate([f_ref[64:96, 64:128], b_ref[64:96, 64:128]], axis=0)
     uu = normal - hdot(ib, coup_t, NT) - hdot(coup_t, ib, NT) + total * hdot(coup_t, coup_t, NT)
     ss = bb - hdot(bs, coup_t) - hdot(coup, bs, NT) + total * hdot(coup_t, coup_t, TN)
-    inverse_factors([normal, uu * (1.0 / total), ss * (1.0 / total)], inv_ref)
+    for m, v in enumerate((normal, uu * (1.0 / total), ss * (1.0 / total))):
+        inv_ref[m] = v
+    inverse_factors([inv_ref[m] for m in range(3)], inv_ref)
     inv_n, inv_u, inv_s = inv_ref[0], inv_ref[1], inv_ref[2]
     w_t = hdot(hdot(inv_n, target), inv_n, TN)
     w_ref[0:64, 0:64] = inv_u
@@ -374,11 +376,10 @@
         (right_side, a_place, m_place, m_local, n_arr, is_first_core)
     )
 
-    (g0,) = call(start_gram_kernel, "start_gram", [VM], [((K, K), F32)], [], (right_side,))
+    (g0,) = call(start_gram_kernel, [VM], [((K, K), F32)], [], (right_side,))
     g0 = reduce_all(g0)
     basis, blow, lt = call(
         start_norm_kernel,
-        "start_norm",
         [VM, VM, SM],
         [(blk, F32), (blk, BF16), ((K, K), F32)],
         [pltpu.VMEM((1, K, K), F32)],
@@ -391,7 +392,6 @@
         q = [swap_y(blow, k) for k in (1, 2, 3)]
         pa_own, pa_cp, pa_zp = call(
             apply_at_kernel,
-            "apply_at",
             [SM, VM, VM],
             [((32, K, TILE), F32), ((16, K, TILE), BF16), ((16, K, TILE), BF16)],
             [pltpu.VMEM((64, K, TILE), F32)],
@@ -402,18 +402,16 @@
         ra_zp, ra_cp = swap_next(pa_zp), swap_core(pa_cp)
         own4, o0, o1, o2, o3 = call(
             mid_kernel,
-            "mid",
             [VM] * 7,
             [((32, K, TILE), BF16), (blk, F32)] + [(blk, BF16)] * 3,
             [],
             (blow, *q, pa_own, ra_cp, ra_zp),
         )
         m_zp = swap_next(own4)
-        b1, b2, b3 = swap_y(o1, 1), swap_y(o2, 2), swap_y(o3, 3)
+        b1, b2, b3 = (swap_y(o, k) for k, o in ((1, o1), (2, o2), (3, o3)))
         m_cp = swap_core(own4)
         pm_own, pm_cp, pm_zp = call(
             apply_mt_kernel,
-            "apply_mt",
             [SM, SM] + [VM] * 5,
             [((32, K, TILE), F32), ((32, K, TILE), BF16), ((32, K, TILE), BF16)],
             [pltpu.VMEM((BR + 1, K, TILE), BF16), pltpu.VMEM((96, K, TILE), F32)],
@@ -424,7 +422,6 @@
         rm_zp, rm_cp = swap_next(pm_zp), swap_core(pm_cp)
         precond, plow = call(
             apply_m_kernel,
-            "apply_m",
             [SM, SM] + [VM] * 4,
             [(blk, F32), (blk, BF16)],
             [pltpu.VMEM((96, K, TILE), BF16), pltpu.VMEM((BR + 1, K, TILE), F32)],
@@ -433,23 +430,17 @@
             nbytes=5_000_000,
         )
         r = [swap_y(plow, k) for k in (1, 2, 3)]
-        (far,) = call(join_kernel, "join", [VM] * 2, [((16, K, TILE), BF16)], [], (r[1], r[2]))
+        (far,) = call(join_kernel, [VM] * 2, [((16, K, TILE), BF16)], [], (r[1], r[2]))
         a_zp, a_cp = swap_next(far), swap_core(far)
         far, pm_own, rm_cp, rm_zp = lax.optimization_barrier((far, pm_own, rm_cp, rm_zp))
         o0, o1, o2, o3 = call(
-            collect_m_kernel,
-            "collect_m",
-            [VM] * 3,
-            [(blk, F32)] + [(blk, BF16)] * 3,
-            [],
-            (pm_own, rm_cp, rm_zp),
-        )
-        b1, b2, b3 = swap_y(o1, 1), swap_y(o2, 2), swap_y(o3, 3)
+            collect_m_kernel, [VM] * 3, [(blk, F32)] + [(blk, BF16)] * 3, [], (pm_own, rm_cp, rm_zp)
+        )
+        b1, b2, b3 = (swap_y(o, k) for k, o in ((1, o1), (2, o2), (3, o3)))
         first = iteration == 0
         height = 64 if first else 96
         image, g_fwd, *rest = call(
             lambda *refs, f=first: apply_a_kernel(f, *refs),
-            "apply_a",
             [SM] + [VM] * (8 if first else 10),
             [(blk, F32), ((height, 128), F32)] + ([] if first else [((32, 128), F32)]),
             [pltpu.VMEM((64, K, TILE), BF16)],
@@ -459,7 +450,6 @@
         )
         back_image, g_bwd = call(
             lambda *refs, f=first: back_gram_kernel(f, *refs),
-            "back_gram",
             [VM] * (5 if first else 6),
             [(blk, F32), ((height, 128), F32)],
             [],
@@ -471,7 +461,6 @@
         outs = [(blk, F32)] * 4 + ([] if last else [(blk, BF16)] * 2)
         result = call(
             lambda *refs, f=iteration == 0, l=last: update_kernel(f, l, *refs),
-            "update",
             [VM, VM, SM] + [VM] * (len(args) - 3),
             outs,
             [pltpu.VMEM((3, K, K), F32), pltpu.VMEM((192, 128), F32)],

time: 234 us -> 228 us (0.974)
  Pallas kernels: 39.2 us -> 33.5 us
    pallas_call x20, Pallas kernels: 39.2 us -> 33.5 us  [call(): pl.pallas_call(body, in_specs=specs, out_specs=tuple((VM for _ in outs)),...]
where the time goes in v3:
time: 228 us; the launch traced here: 227 us
  starting transfers between devices  94.4 us (41%)
  waiting for transfers between devices  92.8 us (41%)
  Pallas kernels  33.5 us (15%)
  local copies, waits for them, and re-layouts  2.36 us (1%)
    ppermute x64, waiting for transfers between devices, swap(): return lax.ppermute(value, axis, [(i, i ^ distance) for i in range(size)])  92.8 us
    ppermute x64, starting transfers between devices, swap(): return lax.ppermute(value, axis, [(i, i ^ distance) for i in range(size)])  88.6 us
    pallas_call x20, Pallas kernels, call(): pl.pallas_call(body, in_specs=specs, out_specs=tuple((VM for _ in outs)),...  33.5 us
    ppermute x8, starting transfers between devices, swap_next(): return lax.ppermute(value, DOM, route)  5.81 us
  transfers between devices with their start and end apart: 72, of which 42 were waited for; matrix products, arithmetic and copies ran while one was open for 0% of the time, Pallas kernels for 6%

profile of v3, /device:TPU:0, one launch (start us, length us, event | category | flops | bytes accessed | tf_op | source)
XLA Modules:
  0.0 226.8 jit_solution(5514633437056362240)
XLA Ops:
  5.9 3.1 %collective-permute-start.3 = (f32[64,64]{1,0:T(8,128)S(1)}, f32[64,64]{1,0:T(8,128)S(1)}, u32[]{:S(2)}, u32[]{:S(2)}) collective-permute-start(f32[64,64]{1,0:T(8,128)S(1)} %add.154), channel_id=1, source_target_pairs={{0,3},{1,2},{2,1},{3,0},{4,7},{5,6},{6,5},{7,4},{8,11},{9,10},{10,... | collective-permute-start | bytes 49160 | tf_op jit(solution)/shard_map/ppermute | solution.py:31
  11.0 3.4 %collective-permute-done.2 = f32[64,64]{1,0:T(8,128)S(1)} collective-permute-done((f32[64,64]{1,0:T(8,128)S(1)}, f32[64,64]{1,0:T(8,128)S(1)}, u32[]{:S(2)}, u32[]{:S(2)}) %collective-permute-start.2) | collective-permute-done | bytes 16416 | tf_op jit(solution)/shard_map/ppermute | solution.py:31
  14.5 4.1 %collective-permute-start.6 = (f32[64,64]{1,0:T(8,128)S(1)}, f32[64,64]{1,0:T(8,128)S(1)}, u32[]{:S(2)}, u32[]{:S(2)}) collective-permute-start(f32[64,64]{1,0:T(8,128)S(1)} %add_add_fusion.8), channel_id=1, source_target_pairs={{0,24},{4,28},{8,16},{12,20},{16,8},{20,12},{24,0},{28,4},{32,56},... | collective-permute-start | bytes 49160 | tf_op jit(solution)/shard_map/ppermute | solution.py:31
  20.5 3.5 %collective-permute-done.5 = f32[64,64]{1,0:T(8,128)S(1)} collective-permute-done((f32[64,64]{1,0:T(8,128)S(1)}, f32[64,64]{1,0:T(8,128)S(1)}, u32[]{:S(2)}, u32[]{:S(2)}) %collective-permute-start.5) | collective-permute-done | bytes 16416 | tf_op jit(solution)/shard_map/ppermute | solution.py:31
  24.0 2.8 %collective-permute-start.9 = (f32[64,64]{1,0:T(8,128)S(1)}, f32[64,64]{1,0:T(8,128)S(1)}, u32[]{:S(2)}, u32[]{:S(2)}) collective-permute-start(f32[64,64]{1,0:T(8,128)S(1)} %add_add_fusion.7), channel_id=1, source_target_pairs={{0,96},{4,100},{8,104},{12,108},{16,112},{20,116},{24,120},{28,124... | collective-permute-start | bytes 49160 | tf_op jit(solution)/shard_map/ppermute | solution.py:31
  29.2 3.1 %collective-permute-done.8 = f32[64,64]{1,0:T(8,128)S(1)} collective-permute-done((f32[64,64]{1,0:T(8,128)S(1)}, f32[64,64]{1,0:T(8,128)S(1)}, u32[]{:S(2)}, u32[]{:S(2)}) %collective-permute-start.8) | collective-permute-done | bytes 16416 | tf_op jit(solution)/shard_map/ppermute | solution.py:31
  32.3 3.3 %shard_map.103 = (f32[8,64,128]{2,1,0:T(8,128)S(1)}, bf16[8,64,128]{2,1,0:T(8,128)(2,1)S(1)}, f32[64,64]{1,0:T(8,128)S(1)}) custom-call(f32[64,64]{1,0:T(8,128)S(1)} %add_add_fusion.6.g_ref, f32[8,64,128]{2,1,0:T(8,128)S(1)} %copy-done.3, f32[1]{0:T(128)} %constant.108.clone.1.n_ref.refs_2_), custom_call_target="tpu_custom_call" | custom-call | tf_op jit(solution)/shard_map/pallas_call | solution.py:77
  43.1 5.5 %collective-permute-done.12.q3_ref = bf16[8,64,128]{2,1,0:T(8,128)(2,1)S(1)} collective-permute-done((bf16[8,64,128]{2,1,0:T(8,128)(2,1)S(1)}, bf16[8,64,128]{2,1,0:T(8,128)(2,1)S(1)}, u32[]{:S(2)}, u32[]{:S(2)}) %collective-permute-start.12) | collective-permute-done | bytes 131104 | tf_op jit(solution)/shard_map/ppermute | solution.py:31
  55.4 4.0 %collective-permute-start.15 = (bf16[32,64,128]{2,1,0:T(8,128)(2,1)S(1)}, bf16[32,64,128]{2,1,0:T(8,128)(2,1)S(1)}, u32[]{:S(2)}, u32[]{:S(2)}) collective-permute-start(bf16[32,64,128]{2,1,0:T(8,128)(2,1)S(1)} %get-tuple-element.78.own_ref), channel_id=1, source_target_pairs={{0,4},{4,0},{8,12},{12,8},{16,20},{20,16},{24,28},{28,24},{32,36},... | collective-permute-start | bytes 1572872 | tf_op jit(solution)/shard_map/ppermute | solution.py:31
  65.1 3.4 %shard_map.106 = (f32[8,64,128]{2,1,0:T(8,128)S(1)}, bf16[8,64,128]{2,1,0:T(8,128)(2,1)S(1)}) custom-call(s32[104]{0:T(128)S(1)} %get-tuple-element.70.col_ref, s32[104]{0:T(128)S(1)} %get-tuple-element.71.row_ref, bf16[32,64,128]{2,1,0:T(8,128)(2,1)S(1)} %get-tuple-element.78.own_ref, bf16[32,64,128]{2,1,0:T(8,128)(2,1)S(1)} %collective-permute-done.15.cp_ref, ...), custom_call_target="tpu_custom_call" | custom-call | flops 218000000 | bytes 5000000 | tf_op jit(solution)/shard_map/pallas_call | solution.py:77
  70.6 4.9 %collective-permute-done.19.b_ref.refs_4_ = bf16[8,64,128]{2,1,0:T(8,128)(2,1)S(1)} collective-permute-done((bf16[8,64,128]{2,1,0:T(8,128)(2,1)S(1)}, bf16[8,64,128]{2,1,0:T(8,128)(2,1)S(1)}, u32[]{:S(2)}, u32[]{:S(2)}) %collective-permute-start.19) | collective-permute-done | bytes 131104 | tf_op jit(solution)/shard_map/ppermute | solution.py:31
  75.4 2.6 %collective-permute-done.18.a_ref.refs_3_ = bf16[8,64,128]{2,1,0:T(8,128)(2,1)S(1)} collective-permute-done((bf16[8,64,128]{2,1,0:T(8,128)(2,1)S(1)}, bf16[8,64,128]{2,1,0:T(8,128)(2,1)S(1)}, u32[]{:S(2)}, u32[]{:S(2)}) %collective-permute-start.18) | collective-permute-done | bytes 131104 | tf_op jit(solution)/shard_map/ppermute | solution.py:31
  79.0 4.4 %collective-permute-start.20 = (bf16[16,64,128]{2,1,0:T(8,128)(2,1)S(1)}, bf16[16,64,128]{2,1,0:T(8,128)(2,1)S(1)}, u32[]{:S(2)}, u32[]{:S(2)}) collective-permute-start(bf16[16,64,128]{2,1,0:T(8,128)(2,1)S(1)} %shard_map.107), channel_id=1, source_target_pairs={{0,4},{4,0},{8,12},{12,8},{16,20},{20,16},{24,28},{28,24},{32,36},... | collective-permute-start | bytes 786440 | tf_op jit(solution)/shard_map/ppermute | solution.py:31
  83.4 3.4 %collective-permute-start.28 = (bf16[8,64,128]{2,1,0:T(8,128)(2,1)S(1)}, bf16[8,64,128]{2,1,0:T(8,128)(2,1)S(1)}, u32[]{:S(2)}, u32[]{:S(2)}) collective-permute-start(bf16[8,64,128]{2,1,0:T(8,128)(2,1)S(1)} %get-tuple-element.94), channel_id=1, source_target_pairs={{0,2},{1,3},{2,0},{3,1},{4,6},{5,7},{6,4},{7,5},{8,10},{9,11},{10,... | collective-permute-start | bytes 393224 | tf_op jit(solution)/shard_map/ppermute | solution.py:31
  88.0 2.6 %collective-permute-done.28.refs_2_ = bf16[8,64,128]{2,1,0:T(8,128)(2,1)S(1)} collective-permute-done((bf16[8,64,128]{2,1,0:T(8,128)(2,1)S(1)}, bf16[8,64,128]{2,1,0:T(8,128)(2,1)S(1)}, u32[]{:S(2)}, u32[]{:S(2)}) %collective-permute-start.28) | collective-permute-done | bytes 131104 | tf_op jit(solution)/shard_map/ppermute | solution.py:31
  90.6 2.6 %collective-permute-done.29.refs_3_ = bf16[8,64,128]{2,1,0:T(8,128)(2,1)S(1)} collective-permute-done((bf16[8,64,128]{2,1,0:T(8,128)(2,1)S(1)}, bf16[8,64,128]{2,1,0:T(8,128)(2,1)S(1)}, u32[]{:S(2)}, u32[]{:S(2)}) %collective-permute-start.29) | collective-permute-done | bytes 131104 | tf_op jit(solution)/shard_map/ppermute | solution.py:31
  104.0 3.3 %collective-permute-start.36 = (f32[64,128]{1,0:T(8,128)S(1)}, f32[64,128]{1,0:T(8,128)S(1)}, u32[]{:S(2)}, u32[]{:S(2)}) collective-permute-start(f32[64,128]{1,0:T(8,128)S(1)} %add_add_fusion.5), channel_id=1, source_target_pairs={{0,24},{4,28},{8,16},{12,20},{16,8},{20,12},{24,0},{28,4},{32,56},... | collective-permute-start | bytes 98312 | tf_op jit(solution)/shard_map/ppermute | solution.py:31
  109.2 3.5 %collective-permute-done.35 = f32[64,128]{1,0:T(8,128)S(1)} collective-permute-done((f32[64,128]{1,0:T(8,128)S(1)}, f32[64,128]{1,0:T(8,128)S(1)}, u32[]{:S(2)}, u32[]{:S(2)}) %collective-permute-start.35) | collective-permute-done | bytes 32800 | tf_op jit(solution)/shard_map/ppermute | solution.py:31
  114.2 3.5 %collective-permute-start.38 = (f32[64,128]{1,0:T(8,128)S(1)}, f32[64,128]{1,0:T(8,128)S(1)}, u32[]{:S(2)}, u32[]{:S(2)}) collective-permute-start(f32[64,128]{1,0:T(8,128)S(1)} %add_add_fusion.4), channel_id=1, source_target_pairs={{0,64},{4,68},{8,72},{12,76},{16,80},{20,84},{24,88},{28,92},{32,9... | collective-permute-start | bytes 98312 | tf_op jit(solution)/shard_map/ppermute | solution.py:31
  122.9 5.0 %shard_map.112 = (f32[8,64,128]{2,1,0:T(8,128)S(1)}, f32[8,64,128]{2,1,0:T(8,128)S(1)}, f32[8,64,128]{2,1,0:T(8,128)S(1)}, f32[8,64,128]{2,1,0:T(8,128)S(1)}, bf...) custom-call(f32[64,128]{1,0:T(8,128)S(1)} %get-tuple-element.135.refs_0_, ...), custom_call_target="tpu_custom_call" | custom-call | tf_op jit(solution)/shard_map/pallas_call | solution.py:77
  134.2 5.4 %collective-permute-done.43.q3_ref = bf16[8,64,128]{2,1,0:T(8,128)(2,1)S(1)} collective-permute-done((bf16[8,64,128]{2,1,0:T(8,128)(2,1)S(1)}, bf16[8,64,128]{2,1,0:T(8,128)(2,1)S(1)}, u32[]{:S(2)}, u32[]{:S(2)}) %collective-permute-start.43) | collective-permute-done | bytes 131104 | tf_op jit(solution)/shard_map/ppermute | solution.py:31
  141.9 3.9 %collective-permute-start.46 = (bf16[32,64,128]{2,1,0:T(8,128)(2,1)S(1)}, bf16[32,64,128]{2,1,0:T(8,128)(2,1)S(1)}, u32[]{:S(2)}, u32[]{:S(2)}) collective-permute-start(bf16[32,64,128]{2,1,0:T(8,128)(2,1)S(1)} %get-tuple-element.106.own_ref), channel_id=1, source_target_pairs={{0,4},{4,0},{8,12},{12,8},{16,20},{20,16},{24,28},{28,24},{32,36},... | collective-permute-start | bytes 1572872 | tf_op jit(solution)/shard_map/ppermute | solution.py:31
  152.1 3.2 %collective-permute-done.54.b2_ref = bf16[8,64,128]{2,1,0:T(8,128)(2,1)S(1)} collective-permute-done((bf16[8,64,128]{2,1,0:T(8,128)(2,1)S(1)}, bf16[8,64,128]{2,1,0:T(8,128)(2,1)S(1)}, u32[]{:S(2)}, u32[]{:S(2)}) %collective-permute-start.54) | collective-permute-done | bytes 131104 | tf_op jit(solution)/shard_map/ppermute | solution.py:31
  161.0 3.4 %shard_map.115 = (f32[8,64,128]{2,1,0:T(8,128)S(1)}, bf16[8,64,128]{2,1,0:T(8,128)(2,1)S(1)}) custom-call(s32[104]{0:T(128)S(1)} %get-tuple-element.70.col_ref, s32[104]{0:T(128)S(1)} %get-tuple-element.71.row_ref, bf16[32,64,128]{2,1,0:T(8,128)(2,1)S(1)} %get-tuple-element.106.own_ref, bf16[32,64,128]{2,1,0:T(8,128)(2,1)S(1)} %collective-permute-done.46.cp_ref, ...), custom_call_target="tpu_custom_call" | custom-call | flops 218000000 | bytes 5000000 | tf_op jit(solution)/shard_map/pallas_call | solution.py:77
  166.0 8.1 %collective-permute-done.50.b_ref.refs_4_ = bf16[8,64,128]{2,1,0:T(8,128)(2,1)S(1)} collective-permute-done((bf16[8,64,128]{2,1,0:T(8,128)(2,1)S(1)}, bf16[8,64,128]{2,1,0:T(8,128)(2,1)S(1)}, u32[]{:S(2)}, u32[]{:S(2)}) %collective-permute-start.50) | collective-permute-done | bytes 131104 | tf_op jit(solution)/shard_map/ppermute | solution.py:31
  174.8 5.4 %collective-permute-start.51 = (bf16[16,64,128]{2,1,0:T(8,128)(2,1)S(1)}, bf16[16,64,128]{2,1,0:T(8,128)(2,1)S(1)}, u32[]{:S(2)}, u32[]{:S(2)}) collective-permute-start(bf16[16,64,128]{2,1,0:T(8,128)(2,1)S(1)} %shard_map.116), channel_id=1, source_target_pairs={{0,4},{4,0},{8,12},{12,8},{16,20},{20,16},{24,28},{28,24},{32,36},... | collective-permute-start | bytes 786440 | tf_op jit(solution)/shard_map/ppermute | solution.py:31
  183.6 3.0 %collective-permute-done.48.refs_2_ = bf16[8,64,128]{2,1,0:T(8,128)(2,1)S(1)} collective-permute-done((bf16[8,64,128]{2,1,0:T(8,128)(2,1)S(1)}, bf16[8,64,128]{2,1,0:T(8,128)(2,1)S(1)}, u32[]{:S(2)}, u32[]{:S(2)}) %collective-permute-start.48) | collective-permute-done | bytes 131104 | tf_op jit(solution)/shard_map/ppermute | solution.py:31
  189.8 2.6 %collective-permute-done.59.refs_2_ = bf16[8,64,128]{2,1,0:T(8,128)(2,1)S(1)} collective-permute-done((bf16[8,64,128]{2,1,0:T(8,128)(2,1)S(1)}, bf16[8,64,128]{2,1,0:T(8,128)(2,1)S(1)}, u32[]{:S(2)}, u32[]{:S(2)}) %collective-permute-start.59) | collective-permute-done | bytes 131104 | tf_op jit(solution)/shard_map/ppermute | solution.py:31
  197.6 2.5 %collective-permute-start.62 = (f32[96,128]{1,0:T(8,128)S(1)}, f32[96,128]{1,0:T(8,128)S(1)}, u32[]{:S(2)}, u32[]{:S(2)}) collective-permute-start(f32[96,128]{1,0:T(8,128)S(1)} %select_add_fusion), channel_id=1, source_target_pairs={{0,1},{1,0},{2,3},{3,2},{4,5},{5,4},{6,7},{7,6},{8,9},{9,8},{10,11... | collective-permute-start | bytes 147464 | tf_op jit(solution)/shard_map/ppermute | solution.py:31
  203.2 3.1 %collective-permute-start.67 = (f32[96,128]{1,0:T(8,128)S(1)}, f32[96,128]{1,0:T(8,128)S(1)}, u32[]{:S(2)}, u32[]{:S(2)}) collective-permute-start(f32[96,128]{1,0:T(8,128)S(1)} %add_add_fusion.2), channel_id=1, source_target_pairs={{0,24},{4,28},{8,16},{12,20},{16,8},{20,12},{24,0},{28,4},{32,56},... | collective-permute-start | bytes 147464 | tf_op jit(solution)/shard_map/ppermute | solution.py:31
  208.6 3.3 %collective-permute-done.66 = f32[96,128]{1,0:T(8,128)S(1)} collective-permute-done((f32[96,128]{1,0:T(8,128)S(1)}, f32[96,128]{1,0:T(8,128)S(1)}, u32[]{:S(2)}, u32[]{:S(2)}) %collective-permute-start.66) | collective-permute-done | bytes 49184 | tf_op jit(solution)/shard_map/ppermute | solution.py:31
  220.7 6.1 %shard_map.121 = (f32[8,64,128]{2,1,0:T(8,128)}, f32[8,64,128]{2,1,0:T(8,128)}, f32[8,64,128]{2,1,0:T(8,128)}, f32[8,64,128]{2,1,0:T(8,128)}) custom-call(f32[96,128]{1,0:T(8,128)S(1)} %get-tuple-element.133.refs_0_, f32[96,128]{1,0:T(8,128)S(1)} %get-tuple-element.132.refs_1_, f32[1]{0:T(128)} %constant.108.clone.1.n_ref.refs_2_, ...), custom_call_target="tpu_custom_call" | custom-call | tf_op jit(solution)/shard_map/pallas_call | solution.py:77
  (162 shorter events, 102.7 us)
Async XLA Ops:
  38.1 11.7 %collective-permute-start.13 = (bf16[16,64,128]{2,1,0:T(8,128)(2,1)S(1)}, bf16[16,64,128]{2,1,0:T(8,128)(2,1)S(1)}, u32[]{:S(2)}, u32[]{:S(2)}) collective-permute-start(bf16[16,64,128]{2,1,0:T(8,128)(2,1)S(1)} %get-tuple-element.76), channel_id=1, source_target_pairs={{0,4},{4,0},{8,12},{12,8},{16,20},{20,16},{24,28},{28,24},{32,36},... | collective-permute-start | bytes 786440 | tf_op jit(solution)/shard_map/ppermute | solution.py:31
  38.2 11.6 %collective-permute-start.14 = (bf16[16,64,128]{2,1,0:T(8,128)(2,1)S(1)}, bf16[16,64,128]{2,1,0:T(8,128)(2,1)S(1)}, u32[]{:S(2)}, u32[]{:S(2)}) collective-permute-start(bf16[16,64,128]{2,1,0:T(8,128)(2,1)S(1)} %get-tuple-element.77), channel_id=1, source_target_pairs={{4,8},{8,4},{12,16},{16,12},{20,24},{24,20},{28,32},{32,28},{36,40... | collective-permute-start | bytes 786440 | tf_op jit(solution)/shard_map/ppermute | solution.py:47
  38.9 9.6 %collective-permute-start.12 = (bf16[8,64,128]{2,1,0:T(8,128)(2,1)S(1)}, bf16[8,64,128]{2,1,0:T(8,128)(2,1)S(1)}, u32[]{:S(2)}, u32[]{:S(2)}) collective-permute-start(bf16[8,64,128]{2,1,0:T(8,128)(2,1)S(1)} %get-tuple-element.74.low_ref), channel_id=1, source_target_pairs={{0,3},{1,2},{2,1},{3,0},{4,7},{5,6},{6,5},{7,4},{8,11},{9,10},{10,... | collective-permute-start | bytes 393224 | tf_op jit(solution)/shard_map/ppermute | solution.py:31
  40.3 8.2 %collective-permute-start.11 = (bf16[8,64,128]{2,1,0:T(8,128)(2,1)S(1)}, bf16[8,64,128]{2,1,0:T(8,128)(2,1)S(1)}, u32[]{:S(2)}, u32[]{:S(2)}) collective-permute-start(bf16[8,64,128]{2,1,0:T(8,128)(2,1)S(1)} %get-tuple-element.74.low_ref), channel_id=1, source_target_pairs={{0,2},{1,3},{2,0},{3,1},{4,6},{5,7},{6,4},{7,5},{8,10},{9,11},{10,... | collective-permute-start | bytes 393224 | tf_op jit(solution)/shard_map/ppermute | solution.py:31
  41.5 8.3 %collective-permute-start.10 = (bf16[8,64,128]{2,1,0:T(8,128)(2,1)S(1)}, bf16[8,64,128]{2,1,0:T(8,128)(2,1)S(1)}, u32[]{:S(2)}, u32[]{:S(2)}) collective-permute-start(bf16[8,64,128]{2,1,0:T(8,128)(2,1)S(1)} %get-tuple-element.74.low_ref), channel_id=1, source_target_pairs={{0,1},{1,0},{2,3},{3,2},{4,5},{5,4},{6,7},{7,6},{8,9},{9,8},{10,11... | collective-permute-start | bytes 393224 | tf_op jit(solution)/shard_map/ppermute | solution.py:31
  50.0 9.4 %collective-permute-start.22 = (bf16[8,64,128]{2,1,0:T(8,128)(2,1)S(1)}, bf16[8,64,128]{2,1,0:T(8,128)(2,1)S(1)}, u32[]{:S(2)}, u32[]{:S(2)}) collective-permute-start(bf16[8,64,128]{2,1,0:T(8,128)(2,1)S(1)} %get-tuple-element.83), channel_id=1, source_target_pairs={{0,1},{1,0},{2,3},{3,2},{4,5},{5,4},{6,7},{7,6},{8,9},{9,8},{10,11... | collective-permute-start | bytes 393224 | tf_op jit(solution)/shard_map/ppermute | solution.py:31
  50.4 9.0 %collective-permute-start.23 = (bf16[8,64,128]{2,1,0:T(8,128)(2,1)S(1)}, bf16[8,64,128]{2,1,0:T(8,128)(2,1)S(1)}, u32[]{:S(2)}, u32[]{:S(2)}) collective-permute-start(bf16[8,64,128]{2,1,0:T(8,128)(2,1)S(1)} %get-tuple-element.84), channel_id=1, source_target_pairs={{0,2},{1,3},{2,0},{3,1},{4,6},{5,7},{6,4},{7,5},{8,10},{9,11},{10,... | collective-permute-start | bytes 393224 | tf_op jit(solution)/shard_map/ppermute | solution.py:31
  52.8 8.9 %collective-permute-start.24 = (bf16[8,64,128]{2,1,0:T(8,128)(2,1)S(1)}, bf16[8,64,128]{2,1,0:T(8,128)(2,1)S(1)}, u32[]{:S(2)}, u32[]{:S(2)}) collective-permute-start(bf16[8,64,128]{2,1,0:T(8,128)(2,1)S(1)} %get-tuple-element.85), channel_id=1, source_target_pairs={{0,3},{1,2},{2,1},{3,0},{4,7},{5,6},{6,5},{7,4},{8,11},{9,10},{10,... | collective-permute-start | bytes 393224 | tf_op jit(solution)/shard_map/ppermute | solution.py:31
  54.7 10.3 %collective-permute-start.16 = (bf16[32,64,128]{2,1,0:T(8,128)(2,1)S(1)}, bf16[32,64,128]{2,1,0:T(8,128)(2,1)S(1)}, u32[]{:S(2)}, u32[]{:S(2)}) collective-permute-start(bf16[32,64,128]{2,1,0:T(8,128)(2,1)S(1)} %get-tuple-element.78.own_ref), channel_id=1, source_target_pairs={{4,8},{8,4},{12,16},{16,12},{20,24},{24,20},{28,32},{32,28},{36,40... | collective-permute-start | bytes 1572872 | tf_op jit(solution)/shard_map/ppermute | solution.py:47
  55.4 9.6 %collective-permute-start.15 = (bf16[32,64,128]{2,1,0:T(8,128)(2,1)S(1)}, bf16[32,64,128]{2,1,0:T(8,128)(2,1)S(1)}, u32[]{:S(2)}, u32[]{:S(2)}) collective-permute-start(bf16[32,64,128]{2,1,0:T(8,128)(2,1)S(1)} %get-tuple-element.78.own_ref), channel_id=1, source_target_pairs={{0,4},{4,0},{8,12},{12,8},{16,20},{20,16},{24,28},{28,24},{32,36},... | collective-permute-start | bytes 1572872 | tf_op jit(solution)/shard_map/ppermute | solution.py:31
  64.1 13.9 %collective-permute-start.25 = (bf16[32,64,128]{2,1,0:T(8,128)(2,1)S(1)}, bf16[32,64,128]{2,1,0:T(8,128)(2,1)S(1)}, u32[]{:S(2)}, u32[]{:S(2)}) collective-permute-start(bf16[32,64,128]{2,1,0:T(8,128)(2,1)S(1)} %get-tuple-element.87), channel_id=1, source_target_pairs={{0,4},{4,0},{8,12},{12,8},{16,20},{20,16},{24,28},{28,24},{32,36},... | collective-permute-start | bytes 1572872 | tf_op jit(solution)/shard_map/ppermute | solution.py:31
  64.2 13.8 %collective-permute-start.26 = (bf16[32,64,128]{2,1,0:T(8,128)(2,1)S(1)}, bf16[32,64,128]{2,1,0:T(8,128)(2,1)S(1)}, u32[]{:S(2)}, u32[]{:S(2)}) collective-permute-start(bf16[32,64,128]{2,1,0:T(8,128)(2,1)S(1)} %get-tuple-element.88), channel_id=1, source_target_pairs={{4,8},{8,4},{12,16},{16,12},{20,24},{24,20},{28,32},{32,28},{36,40... | collective-permute-start | bytes 1572872 | tf_op jit(solution)/shard_map/ppermute | solution.py:47
  78.2 9.8 %collective-permute-start.27 = (bf16[8,64,128]{2,1,0:T(8,128)(2,1)S(1)}, bf16[8,64,128]{2,1,0:T(8,128)(2,1)S(1)}, u32[]{:S(2)}, u32[]{:S(2)}) collective-permute-start(bf16[8,64,128]{2,1,0:T(8,128)(2,1)S(1)} %get-tuple-element.93), channel_id=1, source_target_pairs={{0,1},{1,0},{2,3},{3,2},{4,5},{5,4},{6,7},{7,6},{8,9},{9,8},{10,11... | collective-permute-start | bytes 393224 | tf_op jit(solution)/shard_map/ppermute | solution.py:31
  78.3 15.3 %collective-permute-start.21 = (bf16[16,64,128]{2,1,0:T(8,128)(2,1)S(1)}, bf16[16,64,128]{2,1,0:T(8,128)(2,1)S(1)}, u32[]{:S(2)}, u32[]{:S(2)}) collective-permute-start(bf16[16,64,128]{2,1,0:T(8,128)(2,1)S(1)} %shard_map.107), channel_id=1, source_target_pairs={{4,8},{8,4},{12,16},{16,12},{20,24},{24,20},{28,32},{32,28},{36,40... | collective-permute-start | bytes 786440 | tf_op jit(solution)/shard_map/ppermute | solution.py:47
  79.0 14.6 %collective-permute-start.20 = (bf16[16,64,128]{2,1,0:T(8,128)(2,1)S(1)}, bf16[16,64,128]{2,1,0:T(8,128)(2,1)S(1)}, u32[]{:S(2)}, u32[]{:S(2)}) collective-permute-start(bf16[16,64,128]{2,1,0:T(8,128)(2,1)S(1)} %shard_map.107), channel_id=1, source_target_pairs={{0,4},{4,0},{8,12},{12,8},{16,20},{20,16},{24,28},{28,24},{32,36},... | collective-permute-start | bytes 786440 | tf_op jit(solution)/shard_map/ppermute | solution.py:31
  129.1 11.9 %collective-permute-start.44 = (bf16[16,64,128]{2,1,0:T(8,128)(2,1)S(1)}, bf16[16,64,128]{2,1,0:T(8,128)(2,1)S(1)}, u32[]{:S(2)}, u32[]{:S(2)}) collective-permute-start(bf16[16,64,128]{2,1,0:T(8,128)(2,1)S(1)} %get-tuple-element.104), channel_id=1, source_target_pairs={{0,4},{4,0},{8,12},{12,8},{16,20},{20,16},{24,28},{28,24},{32,36},... | collective-permute-start | bytes 786440 | tf_op jit(solution)/shard_map/ppermute | solution.py:31
  129.3 11.7 %collective-permute-start.45 = (bf16[16,64,128]{2,1,0:T(8,128)(2,1)S(1)}, bf16[16,64,128]{2,1,0:T(8,128)(2,1)S(1)}, u32[]{:S(2)}, u32[]{:S(2)}) collective-permute-start(bf16[16,64,128]{2,1,0:T(8,128)(2,1)S(1)} %get-tuple-element.105), channel_id=1, source_target_pairs={{4,8},{8,4},{12,16},{16,12},{20,24},{24,20},{28,32},{32,28},{36,40... | collective-permute-start | bytes 786440 | tf_op jit(solution)/shard_map/ppermute | solution.py:47
  130.0 9.6 %collective-permute-start.43 = (bf16[8,64,128]{2,1,0:T(8,128)(2,1)S(1)}, bf16[8,64,128]{2,1,0:T(8,128)(2,1)S(1)}, u32[]{:S(2)}, u32[]{:S(2)}) collective-permute-start(bf16[8,64,128]{2,1,0:T(8,128)(2,1)S(1)} %get-tuple-element.101.low_ref), channel_id=1, source_target_pairs={{0,3},{1,2},{2,1},{3,0},{4,7},{5,6},{6,5},{7,4},{8,11},{9,10},{10,... | collective-permute-start | bytes 393224 | tf_op jit(solution)/shard_map/ppermute | solution.py:31
  131.8 7.8 %collective-permute-start.42 = (bf16[8,64,128]{2,1,0:T(8,128)(2,1)S(1)}, bf16[8,64,128]{2,1,0:T(8,128)(2,1)S(1)}, u32[]{:S(2)}, u32[]{:S(2)}) collective-permute-start(bf16[8,64,128]{2,1,0:T(8,128)(2,1)S(1)} %get-tuple-element.101.low_ref), channel_id=1, source_target_pairs={{0,2},{1,3},{2,0},{3,1},{4,6},{5,7},{6,4},{7,5},{8,10},{9,11},{10,... | collective-permute-start | bytes 393224 | tf_op jit(solution)/shard_map/ppermute | solution.py:31
  133.0 8.0 %collective-permute-start.41 = (bf16[8,64,128]{2,1,0:T(8,128)(2,1)S(1)}, bf16[8,64,128]{2,1,0:T(8,128)(2,1)S(1)}, u32[]{:S(2)}, u32[]{:S(2)}) collective-permute-start(bf16[8,64,128]{2,1,0:T(8,128)(2,1)S(1)} %get-tuple-element.101.low_ref), channel_id=1, source_target_pairs={{0,1},{1,0},{2,3},{3,2},{4,5},{5,4},{6,7},{7,6},{8,9},{9,8},{10,11... | collective-permute-start | bytes 393224 | tf_op jit(solution)/shard_map/ppermute | solution.py:31
  141.2 19.8 %collective-permute-start.47 = (bf16[32,64,128]{2,1,0:T(8,128)(2,1)S(1)}, bf16[32,64,128]{2,1,0:T(8,128)(2,1)S(1)}, u32[]{:S(2)}, u32[]{:S(2)}) collective-permute-start(bf16[32,64,128]{2,1,0:T(8,128)(2,1)S(1)} %get-tuple-element.106.own_ref), channel_id=1, source_target_pairs={{4,8},{8,4},{12,16},{16,12},{20,24},{24,20},{28,32},{32,28},{36,40... | collective-permute-start | bytes 1572872 | tf_op jit(solution)/shard_map/ppermute | solution.py:47
  141.9 19.1 %collective-permute-start.46 = (bf16[32,64,128]{2,1,0:T(8,128)(2,1)S(1)}, bf16[32,64,128]{2,1,0:T(8,128)(2,1)S(1)}, u32[]{:S(2)}, u32[]{:S(2)}) collective-permute-start(bf16[32,64,128]{2,1,0:T(8,128)(2,1)S(1)} %get-tuple-element.106.own_ref), channel_id=1, source_target_pairs={{0,4},{4,0},{8,12},{12,8},{16,20},{20,16},{24,28},{28,24},{32,36},... | collective-permute-start | bytes 1572872 | tf_op jit(solution)/shard_map/ppermute | solution.py:31
  146.6 8.7 %collective-permute-start.54 = (bf16[8,64,128]{2,1,0:T(8,128)(2,1)S(1)}, bf16[8,64,128]{2,1,0:T(8,128)(2,1)S(1)}, u32[]{:S(2)}, u32[]{:S(2)}) collective-permute-start(bf16[8,64,128]{2,1,0:T(8,128)(2,1)S(1)} %get-tuple-element.114), channel_id=1, source_target_pairs={{0,2},{1,3},{2,0},{3,1},{4,6},{5,7},{6,4},{7,5},{8,10},{9,11},{10,... | collective-permute-start | bytes 393224 | tf_op jit(solution)/shard_map/ppermute | solution.py:31
  148.9 8.6 %collective-permute-start.55 = (bf16[8,64,128]{2,1,0:T(8,128)(2,1)S(1)}, bf16[8,64,128]{2,1,0:T(8,128)(2,1)S(1)}, u32[]{:S(2)}, u32[]{:S(2)}) collective-permute-start(bf16[8,64,128]{2,1,0:T(8,128)(2,1)S(1)} %get-tuple-element.115), channel_id=1, source_target_pairs={{0,3},{1,2},{2,1},{3,0},{4,7},{5,6},{6,5},{7,4},{8,11},{9,10},{10,... | collective-permute-start | bytes 393224 | tf_op jit(solution)/shard_map/ppermute | solution.py:31
  159.9 20.3 %collective-permute-start.56 = (bf16[32,64,128]{2,1,0:T(8,128)(2,1)S(1)}, bf16[32,64,128]{2,1,0:T(8,128)(2,1)S(1)}, u32[]{:S(2)}, u32[]{:S(2)}) collective-permute-start(bf16[32,64,128]{2,1,0:T(8,128)(2,1)S(1)} %get-tuple-element.117), channel_id=1, source_target_pairs={{0,4},{4,0},{8,12},{12,8},{16,20},{20,16},{24,28},{28,24},{32,36},... | collective-permute-start | bytes 1572872 | tf_op jit(solution)/shard_map/ppermute | solution.py:31
  160.0 20.2 %collective-permute-start.57 = (bf16[32,64,128]{2,1,0:T(8,128)(2,1)S(1)}, bf16[32,64,128]{2,1,0:T(8,128)(2,1)S(1)}, u32[]{:S(2)}, u32[]{:S(2)}) collective-permute-start(bf16[32,64,128]{2,1,0:T(8,128)(2,1)S(1)} %get-tuple-element.118), channel_id=1, source_target_pairs={{4,8},{8,4},{12,16},{16,12},{20,24},{24,20},{28,32},{32,28},{36,40... | collective-permute-start | bytes 1572872 | tf_op jit(solution)/shard_map/ppermute | solution.py:47
  164.4 9.7 %collective-permute-start.50 = (bf16[8,64,128]{2,1,0:T(8,128)(2,1)S(1)}, bf16[8,64,128]{2,1,0:T(8,128)(2,1)S(1)}, u32[]{:S(2)}, u32[]{:S(2)}) collective-permute-start(bf16[8,64,128]{2,1,0:T(8,128)(2,1)S(1)} %get-tuple-element.107.refs_1_), channel_id=1, source_target_pairs={{0,3},{1,2},{2,1},{3,0},{4,7},{5,6},{6,5},{7,4},{8,11},{9,10},{10,... | collective-permute-start | bytes 393224 | tf_op jit(solution)/shard_map/ppermute | solution.py:31
  166.0 8.1 %collective-permute-start.49 = (bf16[8,64,128]{2,1,0:T(8,128)(2,1)S(1)}, bf16[8,64,128]{2,1,0:T(8,128)(2,1)S(1)}, u32[]{:S(2)}, u32[]{:S(2)}) collective-permute-start(bf16[8,64,128]{2,1,0:T(8,128)(2,1)S(1)} %get-tuple-element.107.refs_1_), channel_id=1, source_target_pairs={{0,2},{1,3},{2,0},{3,1},{4,6},{5,7},{6,4},{7,5},{8,10},{9,11},{10,... | collective-permute-start | bytes 393224 | tf_op jit(solution)/shard_map/ppermute | solution.py:31
  174.1 14.0 %collective-permute-start.52 = (bf16[16,64,128]{2,1,0:T(8,128)(2,1)S(1)}, bf16[16,64,128]{2,1,0:T(8,128)(2,1)S(1)}, u32[]{:S(2)}, u32[]{:S(2)}) collective-permute-start(bf16[16,64,128]{2,1,0:T(8,128)(2,1)S(1)} %shard_map.116), channel_id=1, source_target_pairs={{4,8},{8,4},{12,16},{16,12},{20,24},{24,20},{28,32},{32,28},{36,40... | collective-permute-start | bytes 786440 | tf_op jit(solution)/shard_map/ppermute | solution.py:47
  174.8 13.3 %collective-permute-start.51 = (bf16[16,64,128]{2,1,0:T(8,128)(2,1)S(1)}, bf16[16,64,128]{2,1,0:T(8,128)(2,1)S(1)}, u32[]{:S(2)}, u32[]{:S(2)}) collective-permute-start(bf16[16,64,128]{2,1,0:T(8,128)(2,1)S(1)} %shard_map.116), channel_id=1, source_target_pairs={{0,4},{4,0},{8,12},{12,8},{16,20},{20,16},{24,28},{28,24},{32,36},... | collective-permute-start | bytes 786440 | tf_op jit(solution)/shard_map/ppermute | solution.py:31
  180.4 9.3 %collective-permute-start.58 = (bf16[8,64,128]{2,1,0:T(8,128)(2,1)S(1)}, bf16[8,64,128]{2,1,0:T(8,128)(2,1)S(1)}, u32[]{:S(2)}, u32[]{:S(2)}) collective-permute-start(bf16[8,64,128]{2,1,0:T(8,128)(2,1)S(1)} %get-tuple-element.123), channel_id=1, source_target_pairs={{0,1},{1,0},{2,3},{3,2},{4,5},{5,4},{6,7},{7,6},{8,9},{9,8},{10,11... | collective-permute-start | bytes 393224 | tf_op jit(solution)/shard_map/ppermute | solution.py:31
  182.5 9.8 %collective-permute-start.59 = (bf16[8,64,128]{2,1,0:T(8,128)(2,1)S(1)}, bf16[8,64,128]{2,1,0:T(8,128)(2,1)S(1)}, u32[]{:S(2)}, u32[]{:S(2)}) collective-permute-start(bf16[8,64,128]{2,1,0:T(8,128)(2,1)S(1)} %get-tuple-element.124), channel_id=1, source_target_pairs={{0,2},{1,3},{2,0},{3,1},{4,6},{5,7},{6,4},{7,5},{8,10},{9,11},{10,... | collective-permute-start | bytes 393224 | tf_op jit(solution)/shard_map/ppermute | solution.py:31
  (45 other events, 348.0 us)

commit v4 on v3

--- a/solution.py
+++ b/solution.py
@@ -47,25 +47,18 @@
     return lax.ppermute(value, DOM, route)
 
 
-def reduce_yzx(value):
+def reduce_all(value):
     size = lax.axis_size(DOM)
-    parts = [swap_y(value, k) for k in (1, 2, 3)]
-    value = (value + parts[0]) + (parts[1] + parts[2])
-    for unit in (2, 8):
-        parts = [swap(value, DOM, size, k * unit) for k in (1, 2, 3)]
+    value = value + swap_core(value)
+    for unit in (None, 2, 8):
+        parts = []
+        for k in (1, 2, 3):
+            if unit is None:
+                parts.append(swap_y(value, k))
+            else:
+                parts.append(swap(value, DOM, size, k * unit))
         value = (value + parts[0]) + (parts[1] + parts[2])
     return value
-
-
-def reduce_all(value):
-    return reduce_yzx(value + swap_core(value))
-
-
-def reduce_halves(first, second, take_first):
-    mine = jnp.where(take_first, first, second) + swap_core(jnp.where(take_first, second, first))
-    mine = reduce_yzx(mine)
-    other = swap_core(mine)
-    return jnp.where(take_first, mine, other), jnp.where(take_first, other, mine)
 
 
 VM = pl.BlockSpec(memory_space=pltpu.VMEM)
@@ -295,7 +288,7 @@
     g_ref[0:64] = gram_of(back, [back, split(lanes(shadow_ref))])
 
 
-def update_kernel(first, last, f_ref, b_ref, n_ref, image_ref, bi_ref, basis_ref, shadow_ref, precond_ref, res_ref, *refs):
+def update_kernel(first, last, g_ref, n_ref, image_ref, bi_ref, basis_ref, shadow_ref, precond_ref, res_ref, *refs):
     refs, inv_ref, w_ref = refs[:-2], refs[-2], refs[-1]
     if first:
         lt_ref, outs = refs[0], refs[1:]
@@ -305,6 +298,8 @@
         sol_out, res_out, basis_out, shadow_out = outs
     else:
         sol_out, res_out, basis_out, shadow_out, blow_out, slow_out = outs
+    half = g_ref.shape[0] // 2
+    f_ref, b_ref = g_ref.at[0:half], g_ref.at[half : 2 * half]
     total = n_ref[0]
     image_shadow = f_ref[0:64, 0:64]
     coup_t = image_shadow * (1.0 / total)
@@ -371,9 +366,8 @@
     live = jnp.arange(m_tiles.shape[0], dtype=jnp.int32) < m_count[0]
     m_local = jnp.where(live, m_rows - first_row, BR)
 
-    is_first_core = jnp.broadcast_to(group % 2 == 0, (1, 128))
-    right_side, a_place, m_place, m_local, n_arr, is_first_core = lax.optimization_barrier(
-        (right_side, a_place, m_place, m_local, n_arr, is_first_core)
+    right_side, a_place, m_place, m_local, n_arr = lax.optimization_barrier(
+        (right_side, a_place, m_place, m_local, n_arr)
     )
 
     (g0,) = call(start_gram_kernel, [VM], [((K, K), F32)], [], (right_side,))
@@ -455,13 +449,13 @@
             [],
             (o0, b1, b2, b3, shadow, *rest),
         )
-        g_fwd, g_bwd = reduce_halves(g_fwd, g_bwd, is_first_core)
-        args = [g_fwd, g_bwd, n_arr, image, back_image, basis, shadow, precond, residual]
+        grams = reduce_all(jnp.concatenate([g_fwd, g_bwd], 0))
+        args = [grams, n_arr, image, back_image, basis, shadow, precond, residual]
         args.append(lt if first else solution)
         outs = [(blk, F32)] * 4 + ([] if last else [(blk, BF16)] * 2)
         result = call(
             lambda *refs, f=iteration == 0, l=last: update_kernel(f, l, *refs),
-            [VM, VM, SM] + [VM] * (len(args) - 3),
+            [VM, SM] + [VM] * (len(args) - 2),
             outs,
             [pltpu.VMEM((3, K, K), F32), pltpu.VMEM((192, 128), F32)],
             args,

time: 228 us -> 229 us (level)
    ppermute x64 -> x62, starting transfers between devices: 88.6 us -> 90.2 us  [swap(): return lax.ppermute(value, axis, [(i, i ^ distance) for i in range(size)])]
    ppermute x64 -> x62, waiting for transfers between devices: 92.8 us -> 93.5 us  [swap(): return lax.ppermute(value, axis, [(i, i ^ distance) for i in range(size)])]
  transfers between devices with their start and end apart: 72 -> 70, of which waited for: 42 -> 39; matrix products, arithmetic and copies ran while one was open for 0% -> 0% of each run, Pallas kernels for 6% -> 6%
where the time goes in v4:
time: 229 us
  starting transfers between devices  95.8 us (42%)
  waiting for transfers between devices  93.5 us (41%)
  Pallas kernels  33.5 us (15%)
  local copies, waits for them, and re-layouts  2.4 us (1%)
    ppermute x62, waiting for transfers between devices, swap(): return lax.ppermute(value, axis, [(i, i ^ distance) for i in range(size)])  93.5 us
    ppermute x62, starting transfers between devices, swap(): return lax.ppermute(value, axis, [(i, i ^ distance) for i in range(size)])  90.2 us
    pallas_call x20, Pallas kernels, call(): pl.pallas_call(body, in_specs=specs, out_specs=tuple((VM for _ in outs)),...  33.5 us
    ppermute x8, starting transfers between devices, swap_next(): return lax.ppermute(value, DOM, route)  5.61 us
  transfers between devices with their start and end apart: 70, of which 39 were waited for; matrix products, arithmetic and copies ran while one was open for 0% of the time, Pallas kernels for 6%

profile of v4, /device:TPU:0, one launch (start us, length us, event | category | flops | bytes accessed | tf_op | source)
XLA Modules:
  0.0 229.0 jit_solution(6448954863089517744)
XLA Ops:
  5.9 3.1 %collective-permute-start.3 = (f32[64,64]{1,0:T(8,128)S(1)}, f32[64,64]{1,0:T(8,128)S(1)}, u32[]{:S(2)}, u32[]{:S(2)}) collective-permute-start(f32[64,64]{1,0:T(8,128)S(1)} %add.149), channel_id=1, source_target_pairs={{0,3},{1,2},{2,1},{3,0},{4,7},{5,6},{6,5},{7,4},{8,11},{9,10},{10,... | collective-permute-start | bytes 49160 | tf_op jit(solution)/shard_map/ppermute | solution.py:31
  11.0 3.4 %collective-permute-done.2 = f32[64,64]{1,0:T(8,128)S(1)} collective-permute-done((f32[64,64]{1,0:T(8,128)S(1)}, f32[64,64]{1,0:T(8,128)S(1)}, u32[]{:S(2)}, u32[]{:S(2)}) %collective-permute-start.2) | collective-permute-done | bytes 16416 | tf_op jit(solution)/shard_map/ppermute | solution.py:31
  14.4 4.1 %collective-permute-start.6 = (f32[64,64]{1,0:T(8,128)S(1)}, f32[64,64]{1,0:T(8,128)S(1)}, u32[]{:S(2)}, u32[]{:S(2)}) collective-permute-start(f32[64,64]{1,0:T(8,128)S(1)} %add_add_fusion.8), channel_id=1, source_target_pairs={{0,24},{4,28},{8,16},{12,20},{16,8},{20,12},{24,0},{28,4},{32,56},... | collective-permute-start | bytes 49160 | tf_op jit(solution)/shard_map/ppermute | solution.py:31
  20.5 3.5 %collective-permute-done.5 = f32[64,64]{1,0:T(8,128)S(1)} collective-permute-done((f32[64,64]{1,0:T(8,128)S(1)}, f32[64,64]{1,0:T(8,128)S(1)}, u32[]{:S(2)}, u32[]{:S(2)}) %collective-permute-start.5) | collective-permute-done | bytes 16416 | tf_op jit(solution)/shard_map/ppermute | solution.py:31
  24.0 2.8 %collective-permute-start.9 = (f32[64,64]{1,0:T(8,128)S(1)}, f32[64,64]{1,0:T(8,128)S(1)}, u32[]{:S(2)}, u32[]{:S(2)}) collective-permute-start(f32[64,64]{1,0:T(8,128)S(1)} %add_add_fusion.7), channel_id=1, source_target_pairs={{0,96},{4,100},{8,104},{12,108},{16,112},{20,116},{24,120},{28,124... | collective-permute-start | bytes 49160 | tf_op jit(solution)/shard_map/ppermute | solution.py:31
  29.2 3.1 %collective-permute-done.8 = f32[64,64]{1,0:T(8,128)S(1)} collective-permute-done((f32[64,64]{1,0:T(8,128)S(1)}, f32[64,64]{1,0:T(8,128)S(1)}, u32[]{:S(2)}, u32[]{:S(2)}) %collective-permute-start.8) | collective-permute-done | bytes 16416 | tf_op jit(solution)/shard_map/ppermute | solution.py:31
  32.3 3.3 %shard_map.103 = (f32[8,64,128]{2,1,0:T(8,128)S(1)}, bf16[8,64,128]{2,1,0:T(8,128)(2,1)S(1)}, f32[64,64]{1,0:T(8,128)S(1)}) custom-call(f32[64,64]{1,0:T(8,128)S(1)} %add_add_fusion.6.g_ref, f32[8,64,128]{2,1,0:T(8,128)S(1)} %copy-done.3, f32[1]{0:T(128)} %constant.97.clone.1.n_ref.refs_1_), custom_call_target="tpu_custom_call" | custom-call | tf_op jit(solution)/shard_map/pallas_call | solution.py:70
  43.1 5.5 %collective-permute-done.12.q3_ref = bf16[8,64,128]{2,1,0:T(8,128)(2,1)S(1)} collective-permute-done((bf16[8,64,128]{2,1,0:T(8,128)(2,1)S(1)}, bf16[8,64,128]{2,1,0:T(8,128)(2,1)S(1)}, u32[]{:S(2)}, u32[]{:S(2)}) %collective-permute-start.12) | collective-permute-done | bytes 131104 | tf_op jit(solution)/shard_map/ppermute | solution.py:31
  55.4 4.0 %collective-permute-start.15 = (bf16[32,64,128]{2,1,0:T(8,128)(2,1)S(1)}, bf16[32,64,128]{2,1,0:T(8,128)(2,1)S(1)}, u32[]{:S(2)}, u32[]{:S(2)}) collective-permute-start(bf16[32,64,128]{2,1,0:T(8,128)(2,1)S(1)} %get-tuple-element.76.own_ref), channel_id=1, source_target_pairs={{0,4},{4,0},{8,12},{12,8},{16,20},{20,16},{24,28},{28,24},{32,36},... | collective-permute-start | bytes 1572872 | tf_op jit(solution)/shard_map/ppermute | solution.py:31
  65.0 3.4 %shard_map.106 = (f32[8,64,128]{2,1,0:T(8,128)S(1)}, bf16[8,64,128]{2,1,0:T(8,128)(2,1)S(1)}) custom-call(s32[104]{0:T(128)S(1)} %get-tuple-element.68.col_ref, s32[104]{0:T(128)S(1)} %get-tuple-element.69.row_ref, bf16[32,64,128]{2,1,0:T(8,128)(2,1)S(1)} %get-tuple-element.76.own_ref, bf16[32,64,128]{2,1,0:T(8,128)(2,1)S(1)} %collective-permute-done.15.cp_ref, ...), custom_call_target="tpu_custom_call" | custom-call | flops 218000000 | bytes 5000000 | tf_op jit(solution)/shard_map/pallas_call | solution.py:70
  70.5 4.8 %collective-permute-done.19.b_ref.refs_4_ = bf16[8,64,128]{2,1,0:T(8,128)(2,1)S(1)} collective-permute-done((bf16[8,64,128]{2,1,0:T(8,128)(2,1)S(1)}, bf16[8,64,128]{2,1,0:T(8,128)(2,1)S(1)}, u32[]{:S(2)}, u32[]{:S(2)}) %collective-permute-start.19) | collective-permute-done | bytes 131104 | tf_op jit(solution)/shard_map/ppermute | solution.py:31
  75.4 2.6 %collective-permute-done.18.a_ref.refs_3_ = bf16[8,64,128]{2,1,0:T(8,128)(2,1)S(1)} collective-permute-done((bf16[8,64,128]{2,1,0:T(8,128)(2,1)S(1)}, bf16[8,64,128]{2,1,0:T(8,128)(2,1)S(1)}, u32[]{:S(2)}, u32[]{:S(2)}) %collective-permute-start.18) | collective-permute-done | bytes 131104 | tf_op jit(solution)/shard_map/ppermute | solution.py:31
  79.0 4.4 %collective-permute-start.20 = (bf16[16,64,128]{2,1,0:T(8,128)(2,1)S(1)}, bf16[16,64,128]{2,1,0:T(8,128)(2,1)S(1)}, u32[]{:S(2)}, u32[]{:S(2)}) collective-permute-start(bf16[16,64,128]{2,1,0:T(8,128)(2,1)S(1)} %shard_map.107), channel_id=1, source_target_pairs={{0,4},{4,0},{8,12},{12,8},{16,20},{20,16},{24,28},{28,24},{32,36},... | collective-permute-start | bytes 786440 | tf_op jit(solution)/shard_map/ppermute | solution.py:31
  83.3 3.4 %collective-permute-start.28 = (bf16[8,64,128]{2,1,0:T(8,128)(2,1)S(1)}, bf16[8,64,128]{2,1,0:T(8,128)(2,1)S(1)}, u32[]{:S(2)}, u32[]{:S(2)}) collective-permute-start(bf16[8,64,128]{2,1,0:T(8,128)(2,1)S(1)} %get-tuple-element.92), channel_id=1, source_target_pairs={{0,2},{1,3},{2,0},{3,1},{4,6},{5,7},{6,4},{7,5},{8,10},{9,11},{10,... | collective-permute-start | bytes 393224 | tf_op jit(solution)/shard_map/ppermute | solution.py:31
  88.0 2.6 %collective-permute-done.28.refs_2_ = bf16[8,64,128]{2,1,0:T(8,128)(2,1)S(1)} collective-permute-done((bf16[8,64,128]{2,1,0:T(8,128)(2,1)S(1)}, bf16[8,64,128]{2,1,0:T(8,128)(2,1)S(1)}, u32[]{:S(2)}, u32[]{:S(2)}) %collective-permute-start.28) | collective-permute-done | bytes 131104 | tf_op jit(solution)/shard_map/ppermute | solution.py:31
  90.7 2.6 %collective-permute-done.29.refs_3_ = bf16[8,64,128]{2,1,0:T(8,128)(2,1)S(1)} collective-permute-done((bf16[8,64,128]{2,1,0:T(8,128)(2,1)S(1)}, bf16[8,64,128]{2,1,0:T(8,128)(2,1)S(1)}, u32[]{:S(2)}, u32[]{:S(2)}) %collective-permute-start.29) | collective-permute-done | bytes 131104 | tf_op jit(solution)/shard_map/ppermute | solution.py:31
  104.6 3.5 %collective-permute-start.36 = (f32[128,128]{1,0:T(8,128)S(1)}, f32[128,128]{1,0:T(8,128)S(1)}, u32[]{:S(2)}, u32[]{:S(2)}) collective-permute-start(f32[128,128]{1,0:T(8,128)S(1)} %add_add_fusion.5), channel_id=1, source_target_pairs={{0,24},{4,28},{8,16},{12,20},{16,8},{20,12},{24,0},{28,4},{32,56},... | collective-permute-start | bytes 196616 | tf_op jit(solution)/shard_map/ppermute | solution.py:31
  111.0 2.8 %collective-permute-done.35 = f32[128,128]{1,0:T(8,128)S(1)} collective-permute-done((f32[128,128]{1,0:T(8,128)S(1)}, f32[128,128]{1,0:T(8,128)S(1)}, u32[]{:S(2)}, u32[]{:S(2)}) %collective-permute-start.35) | collective-permute-done | bytes 65568 | tf_op jit(solution)/shard_map/ppermute | solution.py:31
  115.7 3.1 %collective-permute-start.38 = (f32[128,128]{1,0:T(8,128)S(1)}, f32[128,128]{1,0:T(8,128)S(1)}, u32[]{:S(2)}, u32[]{:S(2)}) collective-permute-start(f32[128,128]{1,0:T(8,128)S(1)} %add_add_fusion.4), channel_id=1, source_target_pairs={{0,64},{4,68},{8,72},{12,76},{16,80},{20,84},{24,88},{28,92},{32,9... | collective-permute-start | bytes 196616 | tf_op jit(solution)/shard_map/ppermute | solution.py:31
  123.2 5.0 %shard_map.112 = (f32[8,64,128]{2,1,0:T(8,128)S(1)}, f32[8,64,128]{2,1,0:T(8,128)S(1)}, f32[8,64,128]{2,1,0:T(8,128)S(1)}, f32[8,64,128]{2,1,0:T(8,128)S(1)}, bf...) custom-call(f32[128,128]{1,0:T(8,128)S(1)} %add_add_fusion.3.refs_0_, f32[1]{0:T(128)} %constant.97.clone.1.n_ref.refs_1_, ...), custom_call_target="tpu_custom_call" | custom-call | tf_op jit(solution)/shard_map/pallas_call | solution.py:70
  134.3 5.3 %collective-permute-done.42.q3_ref = bf16[8,64,128]{2,1,0:T(8,128)(2,1)S(1)} collective-permute-done((bf16[8,64,128]{2,1,0:T(8,128)(2,1)S(1)}, bf16[8,64,128]{2,1,0:T(8,128)(2,1)S(1)}, u32[]{:S(2)}, u32[]{:S(2)}) %collective-permute-start.42) | collective-permute-done | bytes 131104 | tf_op jit(solution)/shard_map/ppermute | solution.py:31
  141.8 4.0 %collective-permute-start.45 = (bf16[32,64,128]{2,1,0:T(8,128)(2,1)S(1)}, bf16[32,64,128]{2,1,0:T(8,128)(2,1)S(1)}, u32[]{:S(2)}, u32[]{:S(2)}) collective-permute-start(bf16[32,64,128]{2,1,0:T(8,128)(2,1)S(1)} %get-tuple-element.104.own_ref), channel_id=1, source_target_pairs={{0,4},{4,0},{8,12},{12,8},{16,20},{20,16},{24,28},{28,24},{32,36},... | collective-permute-start | bytes 1572872 | tf_op jit(solution)/shard_map/ppermute | solution.py:31
  152.2 3.0 %collective-permute-done.53.b2_ref = bf16[8,64,128]{2,1,0:T(8,128)(2,1)S(1)} collective-permute-done((bf16[8,64,128]{2,1,0:T(8,128)(2,1)S(1)}, bf16[8,64,128]{2,1,0:T(8,128)(2,1)S(1)}, u32[]{:S(2)}, u32[]{:S(2)}) %collective-permute-start.53) | collective-permute-done | bytes 131104 | tf_op jit(solution)/shard_map/ppermute | solution.py:31
  160.6 3.4 %shard_map.115 = (f32[8,64,128]{2,1,0:T(8,128)S(1)}, bf16[8,64,128]{2,1,0:T(8,128)(2,1)S(1)}) custom-call(s32[104]{0:T(128)S(1)} %get-tuple-element.68.col_ref, s32[104]{0:T(128)S(1)} %get-tuple-element.69.row_ref, bf16[32,64,128]{2,1,0:T(8,128)(2,1)S(1)} %get-tuple-element.104.own_ref, bf16[32,64,128]{2,1,0:T(8,128)(2,1)S(1)} %collective-permute-done.45.cp_ref, ...), custom_call_target="tpu_custom_call" | custom-call | flops 218000000 | bytes 5000000 | tf_op jit(solution)/shard_map/pallas_call | solution.py:70
  166.1 4.8 %collective-permute-done.49.b_ref.refs_4_ = bf16[8,64,128]{2,1,0:T(8,128)(2,1)S(1)} collective-permute-done((bf16[8,64,128]{2,1,0:T(8,128)(2,1)S(1)}, bf16[8,64,128]{2,1,0:T(8,128)(2,1)S(1)}, u32[]{:S(2)}, u32[]{:S(2)}) %collective-permute-start.49) | collective-permute-done | bytes 131104 | tf_op jit(solution)/shard_map/ppermute | solution.py:31
  174.0 6.1 %collective-permute-start.50 = (bf16[16,64,128]{2,1,0:T(8,128)(2,1)S(1)}, bf16[16,64,128]{2,1,0:T(8,128)(2,1)S(1)}, u32[]{:S(2)}, u32[]{:S(2)}) collective-permute-start(bf16[16,64,128]{2,1,0:T(8,128)(2,1)S(1)} %shard_map.116), channel_id=1, source_target_pairs={{0,4},{4,0},{8,12},{12,8},{16,20},{20,16},{24,28},{28,24},{32,36},... | collective-permute-start | bytes 786440 | tf_op jit(solution)/shard_map/ppermute | solution.py:31
  183.7 2.8 %collective-permute-done.47.refs_2_ = bf16[8,64,128]{2,1,0:T(8,128)(2,1)S(1)} collective-permute-done((bf16[8,64,128]{2,1,0:T(8,128)(2,1)S(1)}, bf16[8,64,128]{2,1,0:T(8,128)(2,1)S(1)}, u32[]{:S(2)}, u32[]{:S(2)}) %collective-permute-start.47) | collective-permute-done | bytes 131104 | tf_op jit(solution)/shard_map/ppermute | solution.py:31
  200.2 3.4 %collective-permute-done.63 = f32[192,128]{1,0:T(8,128)S(1)} collective-permute-done((f32[192,128]{1,0:T(8,128)S(1)}, f32[192,128]{1,0:T(8,128)S(1)}, u32[]{:S(2)}, u32[]{:S(2)}) %collective-permute-start.63) | collective-permute-done | bytes 98336 | tf_op jit(solution)/shard_map/ppermute | solution.py:31
  204.9 3.0 %collective-permute-start.66 = (f32[192,128]{1,0:T(8,128)S(1)}, f32[192,128]{1,0:T(8,128)S(1)}, u32[]{:S(2)}, u32[]{:S(2)}) collective-permute-start(f32[192,128]{1,0:T(8,128)S(1)} %add_add_fusion.2), channel_id=1, source_target_pairs={{0,24},{4,28},{8,16},{12,20},{16,8},{20,12},{24,0},{28,4},{32,56},... | collective-permute-start | bytes 294920 | tf_op jit(solution)/shard_map/ppermute | solution.py:31
  211.3 2.7 %collective-permute-done.65 = f32[192,128]{1,0:T(8,128)S(1)} collective-permute-done((f32[192,128]{1,0:T(8,128)S(1)}, f32[192,128]{1,0:T(8,128)S(1)}, u32[]{:S(2)}, u32[]{:S(2)}) %collective-permute-start.65) | collective-permute-done | bytes 98336 | tf_op jit(solution)/shard_map/ppermute | solution.py:31
  214.1 2.6 %collective-permute-start.69 = (f32[192,128]{1,0:T(8,128)S(1)}, f32[192,128]{1,0:T(8,128)S(1)}, u32[]{:S(2)}, u32[]{:S(2)}) collective-permute-start(f32[192,128]{1,0:T(8,128)S(1)} %add_add_fusion.1), channel_id=1, source_target_pairs={{0,96},{4,100},{8,104},{12,108},{16,112},{20,116},{24,120},{28,124... | collective-permute-start | bytes 294920 | tf_op jit(solution)/shard_map/ppermute | solution.py:31
  222.9 6.1 %shard_map.121 = (f32[8,64,128]{2,1,0:T(8,128)}, f32[8,64,128]{2,1,0:T(8,128)}, f32[8,64,128]{2,1,0:T(8,128)}, f32[8,64,128]{2,1,0:T(8,128)}) custom-call(f32[192,128]{1,0:T(8,128)S(1)} %add_add_fusion.refs_0_, f32[1]{0:T(128)} %constant.97.clone.1.n_ref.refs_1_, f32[8,64,128]{2,1,0:T(8,128)S(1)} %get-tuple-element.126.refs_2_, ...), custom_call_target="tpu_custom_call" | custom-call | tf_op jit(solution)/shard_map/pallas_call | solution.py:70
  (157 shorter events, 108.7 us)
Async XLA Ops:
  38.1 11.7 %collective-permute-start.13 = (bf16[16,64,128]{2,1,0:T(8,128)(2,1)S(1)}, bf16[16,64,128]{2,1,0:T(8,128)(2,1)S(1)}, u32[]{:S(2)}, u32[]{:S(2)}) collective-permute-start(bf16[16,64,128]{2,1,0:T(8,128)(2,1)S(1)} %get-tuple-element.74), channel_id=1, source_target_pairs={{0,4},{4,0},{8,12},{12,8},{16,20},{20,16},{24,28},{28,24},{32,36},... | collective-permute-start | bytes 786440 | tf_op jit(solution)/shard_map/ppermute | solution.py:31
  38.2 11.6 %collective-permute-start.14 = (bf16[16,64,128]{2,1,0:T(8,128)(2,1)S(1)}, bf16[16,64,128]{2,1,0:T(8,128)(2,1)S(1)}, u32[]{:S(2)}, u32[]{:S(2)}) collective-permute-start(bf16[16,64,128]{2,1,0:T(8,128)(2,1)S(1)} %get-tuple-element.75), channel_id=1, source_target_pairs={{4,8},{8,4},{12,16},{16,12},{20,24},{24,20},{28,32},{32,28},{36,40... | collective-permute-start | bytes 786440 | tf_op jit(solution)/shard_map/ppermute | solution.py:47
  38.9 9.6 %collective-permute-start.12 = (bf16[8,64,128]{2,1,0:T(8,128)(2,1)S(1)}, bf16[8,64,128]{2,1,0:T(8,128)(2,1)S(1)}, u32[]{:S(2)}, u32[]{:S(2)}) collective-permute-start(bf16[8,64,128]{2,1,0:T(8,128)(2,1)S(1)} %get-tuple-element.72.low_ref), channel_id=1, source_target_pairs={{0,3},{1,2},{2,1},{3,0},{4,7},{5,6},{6,5},{7,4},{8,11},{9,10},{10,... | collective-permute-start | bytes 393224 | tf_op jit(solution)/shard_map/ppermute | solution.py:31
  40.3 8.2 %collective-permute-start.11 = (bf16[8,64,128]{2,1,0:T(8,128)(2,1)S(1)}, bf16[8,64,128]{2,1,0:T(8,128)(2,1)S(1)}, u32[]{:S(2)}, u32[]{:S(2)}) collective-permute-start(bf16[8,64,128]{2,1,0:T(8,128)(2,1)S(1)} %get-tuple-element.72.low_ref), channel_id=1, source_target_pairs={{0,2},{1,3},{2,0},{3,1},{4,6},{5,7},{6,4},{7,5},{8,10},{9,11},{10,... | collective-permute-start | bytes 393224 | tf_op jit(solution)/shard_map/ppermute | solution.py:31
  41.4 8.3 %collective-permute-start.10 = (bf16[8,64,128]{2,1,0:T(8,128)(2,1)S(1)}, bf16[8,64,128]{2,1,0:T(8,128)(2,1)S(1)}, u32[]{:S(2)}, u32[]{:S(2)}) collective-permute-start(bf16[8,64,128]{2,1,0:T(8,128)(2,1)S(1)} %get-tuple-element.72.low_ref), channel_id=1, source_target_pairs={{0,1},{1,0},{2,3},{3,2},{4,5},{5,4},{6,7},{7,6},{8,9},{9,8},{10,11... | collective-permute-start | bytes 393224 | tf_op jit(solution)/shard_map/ppermute | solution.py:31
  49.9 9.4 %collective-permute-start.22 = (bf16[8,64,128]{2,1,0:T(8,128)(2,1)S(1)}, bf16[8,64,128]{2,1,0:T(8,128)(2,1)S(1)}, u32[]{:S(2)}, u32[]{:S(2)}) collective-permute-start(bf16[8,64,128]{2,1,0:T(8,128)(2,1)S(1)} %get-tuple-element.81), channel_id=1, source_target_pairs={{0,1},{1,0},{2,3},{3,2},{4,5},{5,4},{6,7},{7,6},{8,9},{9,8},{10,11... | collective-permute-start | bytes 393224 | tf_op jit(solution)/shard_map/ppermute | solution.py:31
  50.4 9.0 %collective-permute-start.23 = (bf16[8,64,128]{2,1,0:T(8,128)(2,1)S(1)}, bf16[8,64,128]{2,1,0:T(8,128)(2,1)S(1)}, u32[]{:S(2)}, u32[]{:S(2)}) collective-permute-start(bf16[8,64,128]{2,1,0:T(8,128)(2,1)S(1)} %get-tuple-element.82), channel_id=1, source_target_pairs={{0,2},{1,3},{2,0},{3,1},{4,6},{5,7},{6,4},{7,5},{8,10},{9,11},{10,... | collective-permute-start | bytes 393224 | tf_op jit(solution)/shard_map/ppermute | solution.py:31
  52.8 8.9 %collective-permute-start.24 = (bf16[8,64,128]{2,1,0:T(8,128)(2,1)S(1)}, bf16[8,64,128]{2,1,0:T(8,128)(2,1)S(1)}, u32[]{:S(2)}, u32[]{:S(2)}) collective-permute-start(bf16[8,64,128]{2,1,0:T(8,128)(2,1)S(1)} %get-tuple-element.83), channel_id=1, source_target_pairs={{0,3},{1,2},{2,1},{3,0},{4,7},{5,6},{6,5},{7,4},{8,11},{9,10},{10,... | collective-permute-start | bytes 393224 | tf_op jit(solution)/shard_map/ppermute | solution.py:31
  54.7 10.3 %collective-permute-start.16 = (bf16[32,64,128]{2,1,0:T(8,128)(2,1)S(1)}, bf16[32,64,128]{2,1,0:T(8,128)(2,1)S(1)}, u32[]{:S(2)}, u32[]{:S(2)}) collective-permute-start(bf16[32,64,128]{2,1,0:T(8,128)(2,1)S(1)} %get-tuple-element.76.own_ref), channel_id=1, source_target_pairs={{4,8},{8,4},{12,16},{16,12},{20,24},{24,20},{28,32},{32,28},{36,40... | collective-permute-start | bytes 1572872 | tf_op jit(solution)/shard_map/ppermute | solution.py:47
  55.4 9.7 %collective-permute-start.15 = (bf16[32,64,128]{2,1,0:T(8,128)(2,1)S(1)}, bf16[32,64,128]{2,1,0:T(8,128)(2,1)S(1)}, u32[]{:S(2)}, u32[]{:S(2)}) collective-permute-start(bf16[32,64,128]{2,1,0:T(8,128)(2,1)S(1)} %get-tuple-element.76.own_ref), channel_id=1, source_target_pairs={{0,4},{4,0},{8,12},{12,8},{16,20},{20,16},{24,28},{28,24},{32,36},... | collective-permute-start | bytes 1572872 | tf_op jit(solution)/shard_map/ppermute | solution.py:31
  64.1 13.9 %collective-permute-start.25 = (bf16[32,64,128]{2,1,0:T(8,128)(2,1)S(1)}, bf16[32,64,128]{2,1,0:T(8,128)(2,1)S(1)}, u32[]{:S(2)}, u32[]{:S(2)}) collective-permute-start(bf16[32,64,128]{2,1,0:T(8,128)(2,1)S(1)} %get-tuple-element.85), channel_id=1, source_target_pairs={{0,4},{4,0},{8,12},{12,8},{16,20},{20,16},{24,28},{28,24},{32,36},... | collective-permute-start | bytes 1572872 | tf_op jit(solution)/shard_map/ppermute | solution.py:31
  64.2 13.8 %collective-permute-start.26 = (bf16[32,64,128]{2,1,0:T(8,128)(2,1)S(1)}, bf16[32,64,128]{2,1,0:T(8,128)(2,1)S(1)}, u32[]{:S(2)}, u32[]{:S(2)}) collective-permute-start(bf16[32,64,128]{2,1,0:T(8,128)(2,1)S(1)} %get-tuple-element.86), channel_id=1, source_target_pairs={{4,8},{8,4},{12,16},{16,12},{20,24},{24,20},{28,32},{32,28},{36,40... | collective-permute-start | bytes 1572872 | tf_op jit(solution)/shard_map/ppermute | solution.py:47
  78.2 9.8 %collective-permute-start.27 = (bf16[8,64,128]{2,1,0:T(8,128)(2,1)S(1)}, bf16[8,64,128]{2,1,0:T(8,128)(2,1)S(1)}, u32[]{:S(2)}, u32[]{:S(2)}) collective-permute-start(bf16[8,64,128]{2,1,0:T(8,128)(2,1)S(1)} %get-tuple-element.91), channel_id=1, source_target_pairs={{0,1},{1,0},{2,3},{3,2},{4,5},{5,4},{6,7},{7,6},{8,9},{9,8},{10,11... | collective-permute-start | bytes 393224 | tf_op jit(solution)/shard_map/ppermute | solution.py:31
  78.3 15.3 %collective-permute-start.21 = (bf16[16,64,128]{2,1,0:T(8,128)(2,1)S(1)}, bf16[16,64,128]{2,1,0:T(8,128)(2,1)S(1)}, u32[]{:S(2)}, u32[]{:S(2)}) collective-permute-start(bf16[16,64,128]{2,1,0:T(8,128)(2,1)S(1)} %shard_map.107), channel_id=1, source_target_pairs={{4,8},{8,4},{12,16},{16,12},{20,24},{24,20},{28,32},{32,28},{36,40... | collective-permute-start | bytes 786440 | tf_op jit(solution)/shard_map/ppermute | solution.py:47
  79.0 14.6 %collective-permute-start.20 = (bf16[16,64,128]{2,1,0:T(8,128)(2,1)S(1)}, bf16[16,64,128]{2,1,0:T(8,128)(2,1)S(1)}, u32[]{:S(2)}, u32[]{:S(2)}) collective-permute-start(bf16[16,64,128]{2,1,0:T(8,128)(2,1)S(1)} %shard_map.107), channel_id=1, source_target_pairs={{0,4},{4,0},{8,12},{12,8},{16,20},{20,16},{24,28},{28,24},{32,36},... | collective-permute-start | bytes 786440 | tf_op jit(solution)/shard_map/ppermute | solution.py:31
  129.3 11.7 %collective-permute-start.43 = (bf16[16,64,128]{2,1,0:T(8,128)(2,1)S(1)}, bf16[16,64,128]{2,1,0:T(8,128)(2,1)S(1)}, u32[]{:S(2)}, u32[]{:S(2)}) collective-permute-start(bf16[16,64,128]{2,1,0:T(8,128)(2,1)S(1)} %get-tuple-element.102), channel_id=1, source_target_pairs={{0,4},{4,0},{8,12},{12,8},{16,20},{20,16},{24,28},{28,24},{32,36},... | collective-permute-start | bytes 786440 | tf_op jit(solution)/shard_map/ppermute | solution.py:31
  129.4 11.6 %collective-permute-start.44 = (bf16[16,64,128]{2,1,0:T(8,128)(2,1)S(1)}, bf16[16,64,128]{2,1,0:T(8,128)(2,1)S(1)}, u32[]{:S(2)}, u32[]{:S(2)}) collective-permute-start(bf16[16,64,128]{2,1,0:T(8,128)(2,1)S(1)} %get-tuple-element.103), channel_id=1, source_target_pairs={{4,8},{8,4},{12,16},{16,12},{20,24},{24,20},{28,32},{32,28},{36,40... | collective-permute-start | bytes 786440 | tf_op jit(solution)/shard_map/ppermute | solution.py:47
  130.1 9.5 %collective-permute-start.42 = (bf16[8,64,128]{2,1,0:T(8,128)(2,1)S(1)}, bf16[8,64,128]{2,1,0:T(8,128)(2,1)S(1)}, u32[]{:S(2)}, u32[]{:S(2)}) collective-permute-start(bf16[8,64,128]{2,1,0:T(8,128)(2,1)S(1)} %get-tuple-element.99.low_ref), channel_id=1, source_target_pairs={{0,3},{1,2},{2,1},{3,0},{4,7},{5,6},{6,5},{7,4},{8,11},{9,10},{10,... | collective-permute-start | bytes 393224 | tf_op jit(solution)/shard_map/ppermute | solution.py:31
  131.7 7.9 %collective-permute-start.41 = (bf16[8,64,128]{2,1,0:T(8,128)(2,1)S(1)}, bf16[8,64,128]{2,1,0:T(8,128)(2,1)S(1)}, u32[]{:S(2)}, u32[]{:S(2)}) collective-permute-start(bf16[8,64,128]{2,1,0:T(8,128)(2,1)S(1)} %get-tuple-element.99.low_ref), channel_id=1, source_target_pairs={{0,2},{1,3},{2,0},{3,1},{4,6},{5,7},{6,4},{7,5},{8,10},{9,11},{10,... | collective-permute-start | bytes 393224 | tf_op jit(solution)/shard_map/ppermute | solution.py:31
  132.8 8.2 %collective-permute-start.40 = (bf16[8,64,128]{2,1,0:T(8,128)(2,1)S(1)}, bf16[8,64,128]{2,1,0:T(8,128)(2,1)S(1)}, u32[]{:S(2)}, u32[]{:S(2)}) collective-permute-start(bf16[8,64,128]{2,1,0:T(8,128)(2,1)S(1)} %get-tuple-element.99.low_ref), channel_id=1, source_target_pairs={{0,1},{1,0},{2,3},{3,2},{4,5},{5,4},{6,7},{7,6},{8,9},{9,8},{10,11... | collective-permute-start | bytes 393224 | tf_op jit(solution)/shard_map/ppermute | solution.py:31
  141.1 19.4 %collective-permute-start.46 = (bf16[32,64,128]{2,1,0:T(8,128)(2,1)S(1)}, bf16[32,64,128]{2,1,0:T(8,128)(2,1)S(1)}, u32[]{:S(2)}, u32[]{:S(2)}) collective-permute-start(bf16[32,64,128]{2,1,0:T(8,128)(2,1)S(1)} %get-tuple-element.104.own_ref), channel_id=1, source_target_pairs={{4,8},{8,4},{12,16},{16,12},{20,24},{24,20},{28,32},{32,28},{36,40... | collective-permute-start | bytes 1572872 | tf_op jit(solution)/shard_map/ppermute | solution.py:47
  141.8 18.7 %collective-permute-start.45 = (bf16[32,64,128]{2,1,0:T(8,128)(2,1)S(1)}, bf16[32,64,128]{2,1,0:T(8,128)(2,1)S(1)}, u32[]{:S(2)}, u32[]{:S(2)}) collective-permute-start(bf16[32,64,128]{2,1,0:T(8,128)(2,1)S(1)} %get-tuple-element.104.own_ref), channel_id=1, source_target_pairs={{0,4},{4,0},{8,12},{12,8},{16,20},{20,16},{24,28},{28,24},{32,36},... | collective-permute-start | bytes 1572872 | tf_op jit(solution)/shard_map/ppermute | solution.py:31
  146.3 8.8 %collective-permute-start.53 = (bf16[8,64,128]{2,1,0:T(8,128)(2,1)S(1)}, bf16[8,64,128]{2,1,0:T(8,128)(2,1)S(1)}, u32[]{:S(2)}, u32[]{:S(2)}) collective-permute-start(bf16[8,64,128]{2,1,0:T(8,128)(2,1)S(1)} %get-tuple-element.112), channel_id=1, source_target_pairs={{0,2},{1,3},{2,0},{3,1},{4,6},{5,7},{6,4},{7,5},{8,10},{9,11},{10,... | collective-permute-start | bytes 393224 | tf_op jit(solution)/shard_map/ppermute | solution.py:31
  148.8 8.6 %collective-permute-start.54 = (bf16[8,64,128]{2,1,0:T(8,128)(2,1)S(1)}, bf16[8,64,128]{2,1,0:T(8,128)(2,1)S(1)}, u32[]{:S(2)}, u32[]{:S(2)}) collective-permute-start(bf16[8,64,128]{2,1,0:T(8,128)(2,1)S(1)} %get-tuple-element.113), channel_id=1, source_target_pairs={{0,3},{1,2},{2,1},{3,0},{4,7},{5,6},{6,5},{7,4},{8,11},{9,10},{10,... | collective-permute-start | bytes 393224 | tf_op jit(solution)/shard_map/ppermute | solution.py:31
  159.8 20.4 %collective-permute-start.55 = (bf16[32,64,128]{2,1,0:T(8,128)(2,1)S(1)}, bf16[32,64,128]{2,1,0:T(8,128)(2,1)S(1)}, u32[]{:S(2)}, u32[]{:S(2)}) collective-permute-start(bf16[32,64,128]{2,1,0:T(8,128)(2,1)S(1)} %get-tuple-element.115), channel_id=1, source_target_pairs={{0,4},{4,0},{8,12},{12,8},{16,20},{20,16},{24,28},{28,24},{32,36},... | collective-permute-start | bytes 1572872 | tf_op jit(solution)/shard_map/ppermute | solution.py:31
  159.9 20.3 %collective-permute-start.56 = (bf16[32,64,128]{2,1,0:T(8,128)(2,1)S(1)}, bf16[32,64,128]{2,1,0:T(8,128)(2,1)S(1)}, u32[]{:S(2)}, u32[]{:S(2)}) collective-permute-start(bf16[32,64,128]{2,1,0:T(8,128)(2,1)S(1)} %get-tuple-element.116), channel_id=1, source_target_pairs={{4,8},{8,4},{12,16},{16,12},{20,24},{24,20},{28,32},{32,28},{36,40... | collective-permute-start | bytes 1572872 | tf_op jit(solution)/shard_map/ppermute | solution.py:47
  173.3 14.9 %collective-permute-start.51 = (bf16[16,64,128]{2,1,0:T(8,128)(2,1)S(1)}, bf16[16,64,128]{2,1,0:T(8,128)(2,1)S(1)}, u32[]{:S(2)}, u32[]{:S(2)}) collective-permute-start(bf16[16,64,128]{2,1,0:T(8,128)(2,1)S(1)} %shard_map.116), channel_id=1, source_target_pairs={{4,8},{8,4},{12,16},{16,12},{20,24},{24,20},{28,32},{32,28},{36,40... | collective-permute-start | bytes 786440 | tf_op jit(solution)/shard_map/ppermute | solution.py:47
  174.0 14.3 %collective-permute-start.50 = (bf16[16,64,128]{2,1,0:T(8,128)(2,1)S(1)}, bf16[16,64,128]{2,1,0:T(8,128)(2,1)S(1)}, u32[]{:S(2)}, u32[]{:S(2)}) collective-permute-start(bf16[16,64,128]{2,1,0:T(8,128)(2,1)S(1)} %shard_map.116), channel_id=1, source_target_pairs={{0,4},{4,0},{8,12},{12,8},{16,20},{20,16},{24,28},{28,24},{32,36},... | collective-permute-start | bytes 786440 | tf_op jit(solution)/shard_map/ppermute | solution.py:31
  180.3 9.6 %collective-permute-start.57 = (bf16[8,64,128]{2,1,0:T(8,128)(2,1)S(1)}, bf16[8,64,128]{2,1,0:T(8,128)(2,1)S(1)}, u32[]{:S(2)}, u32[]{:S(2)}) collective-permute-start(bf16[8,64,128]{2,1,0:T(8,128)(2,1)S(1)} %get-tuple-element.121), channel_id=1, source_target_pairs={{0,1},{1,0},{2,3},{3,2},{4,5},{5,4},{6,7},{7,6},{8,9},{9,8},{10,11... | collective-permute-start | bytes 393224 | tf_op jit(solution)/shard_map/ppermute | solution.py:31
  182.4 10.1 %collective-permute-start.58 = (bf16[8,64,128]{2,1,0:T(8,128)(2,1)S(1)}, bf16[8,64,128]{2,1,0:T(8,128)(2,1)S(1)}, u32[]{:S(2)}, u32[]{:S(2)}) collective-permute-start(bf16[8,64,128]{2,1,0:T(8,128)(2,1)S(1)} %get-tuple-element.122), channel_id=1, source_target_pairs={{0,2},{1,3},{2,0},{3,1},{4,6},{5,7},{6,4},{7,5},{8,10},{9,11},{10,... | collective-permute-start | bytes 393224 | tf_op jit(solution)/shard_map/ppermute | solution.py:31
  186.5 7.8 %collective-permute-start.59 = (bf16[8,64,128]{2,1,0:T(8,128)(2,1)S(1)}, bf16[8,64,128]{2,1,0:T(8,128)(2,1)S(1)}, u32[]{:S(2)}, u32[]{:S(2)}) collective-permute-start(bf16[8,64,128]{2,1,0:T(8,128)(2,1)S(1)} %get-tuple-element.123), channel_id=1, source_target_pairs={{0,3},{1,2},{2,1},{3,0},{4,7},{5,6},{6,5},{7,4},{8,11},{9,10},{10,... | collective-permute-start | bytes 393224 | tf_op jit(solution)/shard_map/ppermute | solution.py:31
  196.0 7.6 %collective-permute-start.63 = (f32[192,128]{1,0:T(8,128)S(1)}, f32[192,128]{1,0:T(8,128)S(1)}, u32[]{:S(2)}, u32[]{:S(2)}) collective-permute-start(f32[192,128]{1,0:T(8,128)S(1)} %add.169), channel_id=1, source_target_pairs={{0,3},{1,2},{2,1},{3,0},{4,7},{5,6},{6,5},{7,4},{8,11},{9,10},{10,... | collective-permute-start | bytes 294920 | tf_op jit(solution)/shard_map/ppermute | solution.py:31
  (43 other events, 349.5 us)

commit v5 on v3

--- a/solution.py
+++ b/solution.py
@@ -49,10 +49,13 @@
 
 def reduce_yzx(value):
     size = lax.axis_size(DOM)
-    parts = [swap_y(value, k) for k in (1, 2, 3)]
-    value = (value + parts[0]) + (parts[1] + parts[2])
-    for unit in (2, 8):
-        parts = [swap(value, DOM, size, k * unit) for k in (1, 2, 3)]
+    for unit in (None, 2, 8):
+        parts = []
+        for k in (1, 2, 3):
+            if unit is None:
+                parts.append(swap_y(value, k))
+            else:
+                parts.append(swap(value, DOM, size, k * unit))
         value = (value + parts[0]) + (parts[1] + parts[2])
     return value
 

time: 228 us -> 228 us (level)
  no operation moved by 1% of the time
where the time goes in v5:
time: 228 us; the launch traced here: 227 us
  starting transfers between devices  94.4 us (41%)
  waiting for transfers between devices  92.8 us (41%)
  Pallas kernels  33.5 us (15%)
  local copies, waits for them, and re-layouts  2.36 us (1%)
    ppermute x64, waiting for transfers between devices, swap(): return lax.ppermute(value, axis, [(i, i ^ distance) for i in range(size)])  92.8 us
    ppermute x64, starting transfers between devices, swap(): return lax.ppermute(value, axis, [(i, i ^ distance) for i in range(size)])  88.6 us
    pallas_call x20, Pallas kernels, call(): pl.pallas_call(body, in_specs=specs, out_specs=tuple((VM for _ in outs)),...  33.5 us
    ppermute x8, starting transfers between devices, swap_next(): return lax.ppermute(value, DOM, route)  5.81 us
  transfers between devices with their start and end apart: 72, of which 42 were waited for; matrix products, arithmetic and copies ran while one was open for 0% of the time, Pallas kernels for 6%

profile of v5, /device:TPU:0, one launch (start us, length us, event | category | flops | bytes accessed | tf_op | source)
XLA Modules:
  0.0 226.8 jit_solution(5514633437056362240)
XLA Ops:
  5.9 3.1 %collective-permute-start.3 = (f32[64,64]{1,0:T(8,128)S(1)}, f32[64,64]{1,0:T(8,128)S(1)}, u32[]{:S(2)}, u32[]{:S(2)}) collective-permute-start(f32[64,64]{1,0:T(8,128)S(1)} %add.154), channel_id=1, source_target_pairs={{0,3},{1,2},{2,1},{3,0},{4,7},{5,6},{6,5},{7,4},{8,11},{9,10},{10,... | collective-permute-start | bytes 49160 | tf_op jit(solution)/shard_map/ppermute | solution.py:31
  11.0 3.4 %collective-permute-done.2 = f32[64,64]{1,0:T(8,128)S(1)} collective-permute-done((f32[64,64]{1,0:T(8,128)S(1)}, f32[64,64]{1,0:T(8,128)S(1)}, u32[]{:S(2)}, u32[]{:S(2)}) %collective-permute-start.2) | collective-permute-done | bytes 16416 | tf_op jit(solution)/shard_map/ppermute | solution.py:31
  14.5 4.1 %collective-permute-start.6 = (f32[64,64]{1,0:T(8,128)S(1)}, f32[64,64]{1,0:T(8,128)S(1)}, u32[]{:S(2)}, u32[]{:S(2)}) collective-permute-start(f32[64,64]{1,0:T(8,128)S(1)} %add_add_fusion.8), channel_id=1, source_target_pairs={{0,24},{4,28},{8,16},{12,20},{16,8},{20,12},{24,0},{28,4},{32,56},... | collective-permute-start | bytes 49160 | tf_op jit(solution)/shard_map/ppermute | solution.py:31
  20.5 3.5 %collective-permute-done.5 = f32[64,64]{1,0:T(8,128)S(1)} collective-permute-done((f32[64,64]{1,0:T(8,128)S(1)}, f32[64,64]{1,0:T(8,128)S(1)}, u32[]{:S(2)}, u32[]{:S(2)}) %collective-permute-start.5) | collective-permute-done | bytes 16416 | tf_op jit(solution)/shard_map/ppermute | solution.py:31
  24.0 2.8 %collective-permute-start.9 = (f32[64,64]{1,0:T(8,128)S(1)}, f32[64,64]{1,0:T(8,128)S(1)}, u32[]{:S(2)}, u32[]{:S(2)}) collective-permute-start(f32[64,64]{1,0:T(8,128)S(1)} %add_add_fusion.7), channel_id=1, source_target_pairs={{0,96},{4,100},{8,104},{12,108},{16,112},{20,116},{24,120},{28,124... | collective-permute-start | bytes 49160 | tf_op jit(solution)/shard_map/ppermute | solution.py:31
  29.2 3.1 %collective-permute-done.8 = f32[64,64]{1,0:T(8,128)S(1)} collective-permute-done((f32[64,64]{1,0:T(8,128)S(1)}, f32[64,64]{1,0:T(8,128)S(1)}, u32[]{:S(2)}, u32[]{:S(2)}) %collective-permute-start.8) | collective-permute-done | bytes 16416 | tf_op jit(solution)/shard_map/ppermute | solution.py:31
  32.3 3.3 %shard_map.103 = (f32[8,64,128]{2,1,0:T(8,128)S(1)}, bf16[8,64,128]{2,1,0:T(8,128)(2,1)S(1)}, f32[64,64]{1,0:T(8,128)S(1)}) custom-call(f32[64,64]{1,0:T(8,128)S(1)} %add_add_fusion.6.g_ref, f32[8,64,128]{2,1,0:T(8,128)S(1)} %copy-done.3, f32[1]{0:T(128)} %constant.108.clone.1.n_ref.refs_2_), custom_call_target="tpu_custom_call" | custom-call | tf_op jit(solution)/shard_map/pallas_call | solution.py:80
  43.1 5.5 %collective-permute-done.12.q3_ref = bf16[8,64,128]{2,1,0:T(8,128)(2,1)S(1)} collective-permute-done((bf16[8,64,128]{2,1,0:T(8,128)(2,1)S(1)}, bf16[8,64,128]{2,1,0:T(8,128)(2,1)S(1)}, u32[]{:S(2)}, u32[]{:S(2)}) %collective-permute-start.12) | collective-permute-done | bytes 131104 | tf_op jit(solution)/shard_map/ppermute | solution.py:31
  55.4 4.0 %collective-permute-start.15 = (bf16[32,64,128]{2,1,0:T(8,128)(2,1)S(1)}, bf16[32,64,128]{2,1,0:T(8,128)(2,1)S(1)}, u32[]{:S(2)}, u32[]{:S(2)}) collective-permute-start(bf16[32,64,128]{2,1,0:T(8,128)(2,1)S(1)} %get-tuple-element.78.own_ref), channel_id=1, source_target_pairs={{0,4},{4,0},{8,12},{12,8},{16,20},{20,16},{24,28},{28,24},{32,36},... | collective-permute-start | bytes 1572872 | tf_op jit(solution)/shard_map/ppermute | solution.py:31
  65.1 3.4 %shard_map.106 = (f32[8,64,128]{2,1,0:T(8,128)S(1)}, bf16[8,64,128]{2,1,0:T(8,128)(2,1)S(1)}) custom-call(s32[104]{0:T(128)S(1)} %get-tuple-element.70.col_ref, s32[104]{0:T(128)S(1)} %get-tuple-element.71.row_ref, bf16[32,64,128]{2,1,0:T(8,128)(2,1)S(1)} %get-tuple-element.78.own_ref, bf16[32,64,128]{2,1,0:T(8,128)(2,1)S(1)} %collective-permute-done.15.cp_ref, ...), custom_call_target="tpu_custom_call" | custom-call | flops 218000000 | bytes 5000000 | tf_op jit(solution)/shard_map/pallas_call | solution.py:80
  70.6 4.9 %collective-permute-done.19.b_ref.refs_4_ = bf16[8,64,128]{2,1,0:T(8,128)(2,1)S(1)} collective-permute-done((bf16[8,64,128]{2,1,0:T(8,128)(2,1)S(1)}, bf16[8,64,128]{2,1,0:T(8,128)(2,1)S(1)}, u32[]{:S(2)}, u32[]{:S(2)}) %collective-permute-start.19) | collective-permute-done | bytes 131104 | tf_op jit(solution)/shard_map/ppermute | solution.py:31
  75.4 2.6 %collective-permute-done.18.a_ref.refs_3_ = bf16[8,64,128]{2,1,0:T(8,128)(2,1)S(1)} collective-permute-done((bf16[8,64,128]{2,1,0:T(8,128)(2,1)S(1)}, bf16[8,64,128]{2,1,0:T(8,128)(2,1)S(1)}, u32[]{:S(2)}, u32[]{:S(2)}) %collective-permute-start.18) | collective-permute-done | bytes 131104 | tf_op jit(solution)/shard_map/ppermute | solution.py:31
  79.0 4.4 %collective-permute-start.20 = (bf16[16,64,128]{2,1,0:T(8,128)(2,1)S(1)}, bf16[16,64,128]{2,1,0:T(8,128)(2,1)S(1)}, u32[]{:S(2)}, u32[]{:S(2)}) collective-permute-start(bf16[16,64,128]{2,1,0:T(8,128)(2,1)S(1)} %shard_map.107), channel_id=1, source_target_pairs={{0,4},{4,0},{8,12},{12,8},{16,20},{20,16},{24,28},{28,24},{32,36},... | collective-permute-start | bytes 786440 | tf_op jit(solution)/shard_map/ppermute | solution.py:31
  83.4 3.4 %collective-permute-start.28 = (bf16[8,64,128]{2,1,0:T(8,128)(2,1)S(1)}, bf16[8,64,128]{2,1,0:T(8,128)(2,1)S(1)}, u32[]{:S(2)}, u32[]{:S(2)}) collective-permute-start(bf16[8,64,128]{2,1,0:T(8,128)(2,1)S(1)} %get-tuple-element.94), channel_id=1, source_target_pairs={{0,2},{1,3},{2,0},{3,1},{4,6},{5,7},{6,4},{7,5},{8,10},{9,11},{10,... | collective-permute-start | bytes 393224 | tf_op jit(solution)/shard_map/ppermute | solution.py:31
  88.0 2.6 %collective-permute-done.28.refs_2_ = bf16[8,64,128]{2,1,0:T(8,128)(2,1)S(1)} collective-permute-done((bf16[8,64,128]{2,1,0:T(8,128)(2,1)S(1)}, bf16[8,64,128]{2,1,0:T(8,128)(2,1)S(1)}, u32[]{:S(2)}, u32[]{:S(2)}) %collective-permute-start.28) | collective-permute-done | bytes 131104 | tf_op jit(solution)/shard_map/ppermute | solution.py:31
  90.6 2.6 %collective-permute-done.29.refs_3_ = bf16[8,64,128]{2,1,0:T(8,128)(2,1)S(1)} collective-permute-done((bf16[8,64,128]{2,1,0:T(8,128)(2,1)S(1)}, bf16[8,64,128]{2,1,0:T(8,128)(2,1)S(1)}, u32[]{:S(2)}, u32[]{:S(2)}) %collective-permute-start.29) | collective-permute-done | bytes 131104 | tf_op jit(solution)/shard_map/ppermute | solution.py:31
  104.0 3.3 %collective-permute-start.36 = (f32[64,128]{1,0:T(8,128)S(1)}, f32[64,128]{1,0:T(8,128)S(1)}, u32[]{:S(2)}, u32[]{:S(2)}) collective-permute-start(f32[64,128]{1,0:T(8,128)S(1)} %add_add_fusion.5), channel_id=1, source_target_pairs={{0,24},{4,28},{8,16},{12,20},{16,8},{20,12},{24,0},{28,4},{32,56},... | collective-permute-start | bytes 98312 | tf_op jit(solution)/shard_map/ppermute | solution.py:31
  109.2 3.5 %collective-permute-done.35 = f32[64,128]{1,0:T(8,128)S(1)} collective-permute-done((f32[64,128]{1,0:T(8,128)S(1)}, f32[64,128]{1,0:T(8,128)S(1)}, u32[]{:S(2)}, u32[]{:S(2)}) %collective-permute-start.35) | collective-permute-done | bytes 32800 | tf_op jit(solution)/shard_map/ppermute | solution.py:31
  114.2 3.5 %collective-permute-start.38 = (f32[64,128]{1,0:T(8,128)S(1)}, f32[64,128]{1,0:T(8,128)S(1)}, u32[]{:S(2)}, u32[]{:S(2)}) collective-permute-start(f32[64,128]{1,0:T(8,128)S(1)} %add_add_fusion.4), channel_id=1, source_target_pairs={{0,64},{4,68},{8,72},{12,76},{16,80},{20,84},{24,88},{28,92},{32,9... | collective-permute-start | bytes 98312 | tf_op jit(solution)/shard_map/ppermute | solution.py:31
  122.9 5.0 %shard_map.112 = (f32[8,64,128]{2,1,0:T(8,128)S(1)}, f32[8,64,128]{2,1,0:T(8,128)S(1)}, f32[8,64,128]{2,1,0:T(8,128)S(1)}, f32[8,64,128]{2,1,0:T(8,128)S(1)}, bf...) custom-call(f32[64,128]{1,0:T(8,128)S(1)} %get-tuple-element.135.refs_0_, ...), custom_call_target="tpu_custom_call" | custom-call | tf_op jit(solution)/shard_map/pallas_call | solution.py:80
  134.2 5.4 %collective-permute-done.43.q3_ref = bf16[8,64,128]{2,1,0:T(8,128)(2,1)S(1)} collective-permute-done((bf16[8,64,128]{2,1,0:T(8,128)(2,1)S(1)}, bf16[8,64,128]{2,1,0:T(8,128)(2,1)S(1)}, u32[]{:S(2)}, u32[]{:S(2)}) %collective-permute-start.43) | collective-permute-done | bytes 131104 | tf_op jit(solution)/shard_map/ppermute | solution.py:31
  141.9 3.9 %collective-permute-start.46 = (bf16[32,64,128]{2,1,0:T(8,128)(2,1)S(1)}, bf16[32,64,128]{2,1,0:T(8,128)(2,1)S(1)}, u32[]{:S(2)}, u32[]{:S(2)}) collective-permute-start(bf16[32,64,128]{2,1,0:T(8,128)(2,1)S(1)} %get-tuple-element.106.own_ref), channel_id=1, source_target_pairs={{0,4},{4,0},{8,12},{12,8},{16,20},{20,16},{24,28},{28,24},{32,36},... | collective-permute-start | bytes 1572872 | tf_op jit(solution)/shard_map/ppermute | solution.py:31
  152.1 3.2 %collective-permute-done.54.b2_ref = bf16[8,64,128]{2,1,0:T(8,128)(2,1)S(1)} collective-permute-done((bf16[8,64,128]{2,1,0:T(8,128)(2,1)S(1)}, bf16[8,64,128]{2,1,0:T(8,128)(2,1)S(1)}, u32[]{:S(2)}, u32[]{:S(2)}) %collective-permute-start.54) | collective-permute-done | bytes 131104 | tf_op jit(solution)/shard_map/ppermute | solution.py:31
  161.0 3.4 %shard_map.115 = (f32[8,64,128]{2,1,0:T(8,128)S(1)}, bf16[8,64,128]{2,1,0:T(8,128)(2,1)S(1)}) custom-call(s32[104]{0:T(128)S(1)} %get-tuple-element.70.col_ref, s32[104]{0:T(128)S(1)} %get-tuple-element.71.row_ref, bf16[32,64,128]{2,1,0:T(8,128)(2,1)S(1)} %get-tuple-element.106.own_ref, bf16[32,64,128]{2,1,0:T(8,128)(2,1)S(1)} %collective-permute-done.46.cp_ref, ...), custom_call_target="tpu_custom_call" | custom-call | flops 218000000 | bytes 5000000 | tf_op jit(solution)/shard_map/pallas_call | solution.py:80
  166.0 8.1 %collective-permute-done.50.b_ref.refs_4_ = bf16[8,64,128]{2,1,0:T(8,128)(2,1)S(1)} collective-permute-done((bf16[8,64,128]{2,1,0:T(8,128)(2,1)S(1)}, bf16[8,64,128]{2,1,0:T(8,128)(2,1)S(1)}, u32[]{:S(2)}, u32[]{:S(2)}) %collective-permute-start.50) | collective-permute-done | bytes 131104 | tf_op jit(solution)/shard_map/ppermute | solution.py:31
  174.8 5.4 %collective-permute-start.51 = (bf16[16,64,128]{2,1,0:T(8,128)(2,1)S(1)}, bf16[16,64,128]{2,1,0:T(8,128)(2,1)S(1)}, u32[]{:S(2)}, u32[]{:S(2)}) collective-permute-start(bf16[16,64,128]{2,1,0:T(8,128)(2,1)S(1)} %shard_map.116), channel_id=1, source_target_pairs={{0,4},{4,0},{8,12},{12,8},{16,20},{20,16},{24,28},{28,24},{32,36},... | collective-permute-start | bytes 786440 | tf_op jit(solution)/shard_map/ppermute | solution.py:31
  183.6 3.0 %collective-permute-done.48.refs_2_ = bf16[8,64,128]{2,1,0:T(8,128)(2,1)S(1)} collective-permute-done((bf16[8,64,128]{2,1,0:T(8,128)(2,1)S(1)}, bf16[8,64,128]{2,1,0:T(8,128)(2,1)S(1)}, u32[]{:S(2)}, u32[]{:S(2)}) %collective-permute-start.48) | collective-permute-done | bytes 131104 | tf_op jit(solution)/shard_map/ppermute | solution.py:31
  189.8 2.6 %collective-permute-done.59.refs_2_ = bf16[8,64,128]{2,1,0:T(8,128)(2,1)S(1)} collective-permute-done((bf16[8,64,128]{2,1,0:T(8,128)(2,1)S(1)}, bf16[8,64,128]{2,1,0:T(8,128)(2,1)S(1)}, u32[]{:S(2)}, u32[]{:S(2)}) %collective-permute-start.59) | collective-permute-done | bytes 131104 | tf_op jit(solution)/shard_map/ppermute | solution.py:31
  197.6 2.5 %collective-permute-start.62 = (f32[96,128]{1,0:T(8,128)S(1)}, f32[96,128]{1,0:T(8,128)S(1)}, u32[]{:S(2)}, u32[]{:S(2)}) collective-permute-start(f32[96,128]{1,0:T(8,128)S(1)} %select_add_fusion), channel_id=1, source_target_pairs={{0,1},{1,0},{2,3},{3,2},{4,5},{5,4},{6,7},{7,6},{8,9},{9,8},{10,11... | collective-permute-start | bytes 147464 | tf_op jit(solution)/shard_map/ppermute | solution.py:31
  203.2 3.1 %collective-permute-start.67 = (f32[96,128]{1,0:T(8,128)S(1)}, f32[96,128]{1,0:T(8,128)S(1)}, u32[]{:S(2)}, u32[]{:S(2)}) collective-permute-start(f32[96,128]{1,0:T(8,128)S(1)} %add_add_fusion.2), channel_id=1, source_target_pairs={{0,24},{4,28},{8,16},{12,20},{16,8},{20,12},{24,0},{28,4},{32,56},... | collective-permute-start | bytes 147464 | tf_op jit(solution)/shard_map/ppermute | solution.py:31
  208.6 3.3 %collective-permute-done.66 = f32[96,128]{1,0:T(8,128)S(1)} collective-permute-done((f32[96,128]{1,0:T(8,128)S(1)}, f32[96,128]{1,0:T(8,128)S(1)}, u32[]{:S(2)}, u32[]{:S(2)}) %collective-permute-start.66) | collective-permute-done | bytes 49184 | tf_op jit(solution)/shard_map/ppermute | solution.py:31
  220.7 6.1 %shard_map.121 = (f32[8,64,128]{2,1,0:T(8,128)}, f32[8,64,128]{2,1,0:T(8,128)}, f32[8,64,128]{2,1,0:T(8,128)}, f32[8,64,128]{2,1,0:T(8,128)}) custom-call(f32[96,128]{1,0:T(8,128)S(1)} %get-tuple-element.133.refs_0_, f32[96,128]{1,0:T(8,128)S(1)} %get-tuple-element.132.refs_1_, f32[1]{0:T(128)} %constant.108.clone.1.n_ref.refs_2_, ...), custom_call_target="tpu_custom_call" | custom-call | tf_op jit(solution)/shard_map/pallas_call | solution.py:80
  (162 shorter events, 102.7 us)
Async XLA Ops:
  38.1 11.7 %collective-permute-start.13 = (bf16[16,64,128]{2,1,0:T(8,128)(2,1)S(1)}, bf16[16,64,128]{2,1,0:T(8,128)(2,1)S(1)}, u32[]{:S(2)}, u32[]{:S(2)}) collective-permute-start(bf16[16,64,128]{2,1,0:T(8,128)(2,1)S(1)} %get-tuple-element.76), channel_id=1, source_target_pairs={{0,4},{4,0},{8,12},{12,8},{16,20},{20,16},{24,28},{28,24},{32,36},... | collective-permute-start | bytes 786440 | tf_op jit(solution)/shard_map/ppermute | solution.py:31
  38.2 11.6 %collective-permute-start.14 = (bf16[16,64,128]{2,1,0:T(8,128)(2,1)S(1)}, bf16[16,64,128]{2,1,0:T(8,128)(2,1)S(1)}, u32[]{:S(2)}, u32[]{:S(2)}) collective-permute-start(bf16[16,64,128]{2,1,0:T(8,128)(2,1)S(1)} %get-tuple-element.77), channel_id=1, source_target_pairs={{4,8},{8,4},{12,16},{16,12},{20,24},{24,20},{28,32},{32,28},{36,40... | collective-permute-start | bytes 786440 | tf_op jit(solution)/shard_map/ppermute | solution.py:47
  38.9 9.6 %collective-permute-start.12 = (bf16[8,64,128]{2,1,0:T(8,128)(2,1)S(1)}, bf16[8,64,128]{2,1,0:T(8,128)(2,1)S(1)}, u32[]{:S(2)}, u32[]{:S(2)}) collective-permute-start(bf16[8,64,128]{2,1,0:T(8,128)(2,1)S(1)} %get-tuple-element.74.low_ref), channel_id=1, source_target_pairs={{0,3},{1,2},{2,1},{3,0},{4,7},{5,6},{6,5},{7,4},{8,11},{9,10},{10,... | collective-permute-start | bytes 393224 | tf_op jit(solution)/shard_map/ppermute | solution.py:31
  40.3 8.2 %collective-permute-start.11 = (bf16[8,64,128]{2,1,0:T(8,128)(2,1)S(1)}, bf16[8,64,128]{2,1,0:T(8,128)(2,1)S(1)}, u32[]{:S(2)}, u32[]{:S(2)}) collective-permute-start(bf16[8,64,128]{2,1,0:T(8,128)(2,1)S(1)} %get-tuple-element.74.low_ref), channel_id=1, source_target_pairs={{0,2},{1,3},{2,0},{3,1},{4,6},{5,7},{6,4},{7,5},{8,10},{9,11},{10,... | collective-permute-start | bytes 393224 | tf_op jit(solution)/shard_map/ppermute | solution.py:31
  41.5 8.3 %collective-permute-start.10 = (bf16[8,64,128]{2,1,0:T(8,128)(2,1)S(1)}, bf16[8,64,128]{2,1,0:T(8,128)(2,1)S(1)}, u32[]{:S(2)}, u32[]{:S(2)}) collective-permute-start(bf16[8,64,128]{2,1,0:T(8,128)(2,1)S(1)} %get-tuple-element.74.low_ref), channel_id=1, source_target_pairs={{0,1},{1,0},{2,3},{3,2},{4,5},{5,4},{6,7},{7,6},{8,9},{9,8},{10,11... | collective-permute-start | bytes 393224 | tf_op jit(solution)/shard_map/ppermute | solution.py:31
  50.0 9.4 %collective-permute-start.22 = (bf16[8,64,128]{2,1,0:T(8,128)(2,1)S(1)}, bf16[8,64,128]{2,1,0:T(8,128)(2,1)S(1)}, u32[]{:S(2)}, u32[]{:S(2)}) collective-permute-start(bf16[8,64,128]{2,1,0:T(8,128)(2,1)S(1)} %get-tuple-element.83), channel_id=1, source_target_pairs={{0,1},{1,0},{2,3},{3,2},{4,5},{5,4},{6,7},{7,6},{8,9},{9,8},{10,11... | collective-permute-start | bytes 393224 | tf_op jit(solution)/shard_map/ppermute | solution.py:31
  50.4 9.0 %collective-permute-start.23 = (bf16[8,64,128]{2,1,0:T(8,128)(2,1)S(1)}, bf16[8,64,128]{2,1,0:T(8,128)(2,1)S(1)}, u32[]{:S(2)}, u32[]{:S(2)}) collective-permute-start(bf16[8,64,128]{2,1,0:T(8,128)(2,1)S(1)} %get-tuple-element.84), channel_id=1, source_target_pairs={{0,2},{1,3},{2,0},{3,1},{4,6},{5,7},{6,4},{7,5},{8,10},{9,11},{10,... | collective-permute-start | bytes 393224 | tf_op jit(solution)/shard_map/ppermute | solution.py:31
  52.8 8.9 %collective-permute-start.24 = (bf16[8,64,128]{2,1,0:T(8,128)(2,1)S(1)}, bf16[8,64,128]{2,1,0:T(8,128)(2,1)S(1)}, u32[]{:S(2)}, u32[]{:S(2)}) collective-permute-start(bf16[8,64,128]{2,1,0:T(8,128)(2,1)S(1)} %get-tuple-element.85), channel_id=1, source_target_pairs={{0,3},{1,2},{2,1},{3,0},{4,7},{5,6},{6,5},{7,4},{8,11},{9,10},{10,... | collective-permute-start | bytes 393224 | tf_op jit(solution)/shard_map/ppermute | solution.py:31
  54.7 10.3 %collective-permute-start.16 = (bf16[32,64,128]{2,1,0:T(8,128)(2,1)S(1)}, bf16[32,64,128]{2,1,0:T(8,128)(2,1)S(1)}, u32[]{:S(2)}, u32[]{:S(2)}) collective-permute-start(bf16[32,64,128]{2,1,0:T(8,128)(2,1)S(1)} %get-tuple-element.78.own_ref), channel_id=1, source_target_pairs={{4,8},{8,4},{12,16},{16,12},{20,24},{24,20},{28,32},{32,28},{36,40... | collective-permute-start | bytes 1572872 | tf_op jit(solution)/shard_map/ppermute | solution.py:47
  55.4 9.6 %collective-permute-start.15 = (bf16[32,64,128]{2,1,0:T(8,128)(2,1)S(1)}, bf16[32,64,128]{2,1,0:T(8,128)(2,1)S(1)}, u32[]{:S(2)}, u32[]{:S(2)}) collective-permute-start(bf16[32,64,128]{2,1,0:T(8,128)(2,1)S(1)} %get-tuple-element.78.own_ref), channel_id=1, source_target_pairs={{0,4},{4,0},{8,12},{12,8},{16,20},{20,16},{24,28},{28,24},{32,36},... | collective-permute-start | bytes 1572872 | tf_op jit(solution)/shard_map/ppermute | solution.py:31
  64.1 13.9 %collective-permute-start.25 = (bf16[32,64,128]{2,1,0:T(8,128)(2,1)S(1)}, bf16[32,64,128]{2,1,0:T(8,128)(2,1)S(1)}, u32[]{:S(2)}, u32[]{:S(2)}) collective-permute-start(bf16[32,64,128]{2,1,0:T(8,128)(2,1)S(1)} %get-tuple-element.87), channel_id=1, source_target_pairs={{0,4},{4,0},{8,12},{12,8},{16,20},{20,16},{24,28},{28,24},{32,36},... | collective-permute-start | bytes 1572872 | tf_op jit(solution)/shard_map/ppermute | solution.py:31
  64.2 13.8 %collective-permute-start.26 = (bf16[32,64,128]{2,1,0:T(8,128)(2,1)S(1)}, bf16[32,64,128]{2,1,0:T(8,128)(2,1)S(1)}, u32[]{:S(2)}, u32[]{:S(2)}) collective-permute-start(bf16[32,64,128]{2,1,0:T(8,128)(2,1)S(1)} %get-tuple-element.88), channel_id=1, source_target_pairs={{4,8},{8,4},{12,16},{16,12},{20,24},{24,20},{28,32},{32,28},{36,40... | collective-permute-start | bytes 1572872 | tf_op jit(solution)/shard_map/ppermute | solution.py:47
  78.2 9.8 %collective-permute-start.27 = (bf16[8,64,128]{2,1,0:T(8,128)(2,1)S(1)}, bf16[8,64,128]{2,1,0:T(8,128)(2,1)S(1)}, u32[]{:S(2)}, u32[]{:S(2)}) collective-permute-start(bf16[8,64,128]{2,1,0:T(8,128)(2,1)S(1)} %get-tuple-element.93), channel_id=1, source_target_pairs={{0,1},{1,0},{2,3},{3,2},{4,5},{5,4},{6,7},{7,6},{8,9},{9,8},{10,11... | collective-permute-start | bytes 393224 | tf_op jit(solution)/shard_map/ppermute | solution.py:31
  78.3 15.3 %collective-permute-start.21 = (bf16[16,64,128]{2,1,0:T(8,128)(2,1)S(1)}, bf16[16,64,128]{2,1,0:T(8,128)(2,1)S(1)}, u32[]{:S(2)}, u32[]{:S(2)}) collective-permute-start(bf16[16,64,128]{2,1,0:T(8,128)(2,1)S(1)} %shard_map.107), channel_id=1, source_target_pairs={{4,8},{8,4},{12,16},{16,12},{20,24},{24,20},{28,32},{32,28},{36,40... | collective-permute-start | bytes 786440 | tf_op jit(solution)/shard_map/ppermute | solution.py:47
  79.0 14.6 %collective-permute-start.20 = (bf16[16,64,128]{2,1,0:T(8,128)(2,1)S(1)}, bf16[16,64,128]{2,1,0:T(8,128)(2,1)S(1)}, u32[]{:S(2)}, u32[]{:S(2)}) collective-permute-start(bf16[16,64,128]{2,1,0:T(8,128)(2,1)S(1)} %shard_map.107), channel_id=1, source_target_pairs={{0,4},{4,0},{8,12},{12,8},{16,20},{20,16},{24,28},{28,24},{32,36},... | collective-permute-start | bytes 786440 | tf_op jit(solution)/shard_map/ppermute | solution.py:31
  129.1 11.9 %collective-permute-start.44 = (bf16[16,64,128]{2,1,0:T(8,128)(2,1)S(1)}, bf16[16,64,128]{2,1,0:T(8,128)(2,1)S(1)}, u32[]{:S(2)}, u32[]{:S(2)}) collective-permute-start(bf16[16,64,128]{2,1,0:T(8,128)(2,1)S(1)} %get-tuple-element.104), channel_id=1, source_target_pairs={{0,4},{4,0},{8,12},{12,8},{16,20},{20,16},{24,28},{28,24},{32,36},... | collective-permute-start | bytes 786440 | tf_op jit(solution)/shard_map/ppermute | solution.py:31
  129.3 11.7 %collective-permute-start.45 = (bf16[16,64,128]{2,1,0:T(8,128)(2,1)S(1)}, bf16[16,64,128]{2,1,0:T(8,128)(2,1)S(1)}, u32[]{:S(2)}, u32[]{:S(2)}) collective-permute-start(bf16[16,64,128]{2,1,0:T(8,128)(2,1)S(1)} %get-tuple-element.105), channel_id=1, source_target_pairs={{4,8},{8,4},{12,16},{16,12},{20,24},{24,20},{28,32},{32,28},{36,40... | collective-permute-start | bytes 786440 | tf_op jit(solution)/shard_map/ppermute | solution.py:47
  130.0 9.6 %collective-permute-start.43 = (bf16[8,64,128]{2,1,0:T(8,128)(2,1)S(1)}, bf16[8,64,128]{2,1,0:T(8,128)(2,1)S(1)}, u32[]{:S(2)}, u32[]{:S(2)}) collective-permute-start(bf16[8,64,128]{2,1,0:T(8,128)(2,1)S(1)} %get-tuple-element.101.low_ref), channel_id=1, source_target_pairs={{0,3},{1,2},{2,1},{3,0},{4,7},{5,6},{6,5},{7,4},{8,11},{9,10},{10,... | collective-permute-start | bytes 393224 | tf_op jit(solution)/shard_map/ppermute | solution.py:31
  131.8 7.8 %collective-permute-start.42 = (bf16[8,64,128]{2,1,0:T(8,128)(2,1)S(1)}, bf16[8,64,128]{2,1,0:T(8,128)(2,1)S(1)}, u32[]{:S(2)}, u32[]{:S(2)}) collective-permute-start(bf16[8,64,128]{2,1,0:T(8,128)(2,1)S(1)} %get-tuple-element.101.low_ref), channel_id=1, source_target_pairs={{0,2},{1,3},{2,0},{3,1},{4,6},{5,7},{6,4},{7,5},{8,10},{9,11},{10,... | collective-permute-start | bytes 393224 | tf_op jit(solution)/shard_map/ppermute | solution.py:31
  133.0 8.0 %collective-permute-start.41 = (bf16[8,64,128]{2,1,0:T(8,128)(2,1)S(1)}, bf16[8,64,128]{2,1,0:T(8,128)(2,1)S(1)}, u32[]{:S(2)}, u32[]{:S(2)}) collective-permute-start(bf16[8,64,128]{2,1,0:T(8,128)(2,1)S(1)} %get-tuple-element.101.low_ref), channel_id=1, source_target_pairs={{0,1},{1,0},{2,3},{3,2},{4,5},{5,4},{6,7},{7,6},{8,9},{9,8},{10,11... | collective-permute-start | bytes 393224 | tf_op jit(solution)/shard_map/ppermute | solution.py:31
  141.2 19.8 %collective-permute-start.47 = (bf16[32,64,128]{2,1,0:T(8,128)(2,1)S(1)}, bf16[32,64,128]{2,1,0:T(8,128)(2,1)S(1)}, u32[]{:S(2)}, u32[]{:S(2)}) collective-permute-start(bf16[32,64,128]{2,1,0:T(8,128)(2,1)S(1)} %get-tuple-element.106.own_ref), channel_id=1, source_target_pairs={{4,8},{8,4},{12,16},{16,12},{20,24},{24,20},{28,32},{32,28},{36,40... | collective-permute-start | bytes 1572872 | tf_op jit(solution)/shard_map/ppermute | solution.py:47
  141.9 19.1 %collective-permute-start.46 = (bf16[32,64,128]{2,1,0:T(8,128)(2,1)S(1)}, bf16[32,64,128]{2,1,0:T(8,128)(2,1)S(1)}, u32[]{:S(2)}, u32[]{:S(2)}) collective-permute-start(bf16[32,64,128]{2,1,0:T(8,128)(2,1)S(1)} %get-tuple-element.106.own_ref), channel_id=1, source_target_pairs={{0,4},{4,0},{8,12},{12,8},{16,20},{20,16},{24,28},{28,24},{32,36},... | collective-permute-start | bytes 1572872 | tf_op jit(solution)/shard_map/ppermute | solution.py:31
  146.6 8.7 %collective-permute-start.54 = (bf16[8,64,128]{2,1,0:T(8,128)(2,1)S(1)}, bf16[8,64,128]{2,1,0:T(8,128)(2,1)S(1)}, u32[]{:S(2)}, u32[]{:S(2)}) collective-permute-start(bf16[8,64,128]{2,1,0:T(8,128)(2,1)S(1)} %get-tuple-element.114), channel_id=1, source_target_pairs={{0,2},{1,3},{2,0},{3,1},{4,6},{5,7},{6,4},{7,5},{8,10},{9,11},{10,... | collective-permute-start | bytes 393224 | tf_op jit(solution)/shard_map/ppermute | solution.py:31
  148.9 8.6 %collective-permute-start.55 = (bf16[8,64,128]{2,1,0:T(8,128)(2,1)S(1)}, bf16[8,64,128]{2,1,0:T(8,128)(2,1)S(1)}, u32[]{:S(2)}, u32[]{:S(2)}) collective-permute-start(bf16[8,64,128]{2,1,0:T(8,128)(2,1)S(1)} %get-tuple-element.115), channel_id=1, source_target_pairs={{0,3},{1,2},{2,1},{3,0},{4,7},{5,6},{6,5},{7,4},{8,11},{9,10},{10,... | collective-permute-start | bytes 393224 | tf_op jit(solution)/shard_map/ppermute | solution.py:31
  159.9 20.3 %collective-permute-start.56 = (bf16[32,64,128]{2,1,0:T(8,128)(2,1)S(1)}, bf16[32,64,128]{2,1,0:T(8,128)(2,1)S(1)}, u32[]{:S(2)}, u32[]{:S(2)}) collective-permute-start(bf16[32,64,128]{2,1,0:T(8,128)(2,1)S(1)} %get-tuple-element.117), channel_id=1, source_target_pairs={{0,4},{4,0},{8,12},{12,8},{16,20},{20,16},{24,28},{28,24},{32,36},... | collective-permute-start | bytes 1572872 | tf_op jit(solution)/shard_map/ppermute | solution.py:31
  160.0 20.2 %collective-permute-start.57 = (bf16[32,64,128]{2,1,0:T(8,128)(2,1)S(1)}, bf16[32,64,128]{2,1,0:T(8,128)(2,1)S(1)}, u32[]{:S(2)}, u32[]{:S(2)}) collective-permute-start(bf16[32,64,128]{2,1,0:T(8,128)(2,1)S(1)} %get-tuple-element.118), channel_id=1, source_target_pairs={{4,8},{8,4},{12,16},{16,12},{20,24},{24,20},{28,32},{32,28},{36,40... | collective-permute-start | bytes 1572872 | tf_op jit(solution)/shard_map/ppermute | solution.py:47
  164.4 9.7 %collective-permute-start.50 = (bf16[8,64,128]{2,1,0:T(8,128)(2,1)S(1)}, bf16[8,64,128]{2,1,0:T(8,128)(2,1)S(1)}, u32[]{:S(2)}, u32[]{:S(2)}) collective-permute-start(bf16[8,64,128]{2,1,0:T(8,128)(2,1)S(1)} %get-tuple-element.107.refs_1_), channel_id=1, source_target_pairs={{0,3},{1,2},{2,1},{3,0},{4,7},{5,6},{6,5},{7,4},{8,11},{9,10},{10,... | collective-permute-start | bytes 393224 | tf_op jit(solution)/shard_map/ppermute | solution.py:31
  166.0 8.1 %collective-permute-start.49 = (bf16[8,64,128]{2,1,0:T(8,128)(2,1)S(1)}, bf16[8,64,128]{2,1,0:T(8,128)(2,1)S(1)}, u32[]{:S(2)}, u32[]{:S(2)}) collective-permute-start(bf16[8,64,128]{2,1,0:T(8,128)(2,1)S(1)} %get-tuple-element.107.refs_1_), channel_id=1, source_target_pairs={{0,2},{1,3},{2,0},{3,1},{4,6},{5,7},{6,4},{7,5},{8,10},{9,11},{10,... | collective-permute-start | bytes 393224 | tf_op jit(solution)/shard_map/ppermute | solution.py:31
  174.1 14.0 %collective-permute-start.52 = (bf16[16,64,128]{2,1,0:T(8,128)(2,1)S(1)}, bf16[16,64,128]{2,1,0:T(8,128)(2,1)S(1)}, u32[]{:S(2)}, u32[]{:S(2)}) collective-permute-start(bf16[16,64,128]{2,1,0:T(8,128)(2,1)S(1)} %shard_map.116), channel_id=1, source_target_pairs={{4,8},{8,4},{12,16},{16,12},{20,24},{24,20},{28,32},{32,28},{36,40... | collective-permute-start | bytes 786440 | tf_op jit(solution)/shard_map/ppermute | solution.py:47
  174.8 13.3 %collective-permute-start.51 = (bf16[16,64,128]{2,1,0:T(8,128)(2,1)S(1)}, bf16[16,64,128]{2,1,0:T(8,128)(2,1)S(1)}, u32[]{:S(2)}, u32[]{:S(2)}) collective-permute-start(bf16[16,64,128]{2,1,0:T(8,128)(2,1)S(1)} %shard_map.116), channel_id=1, source_target_pairs={{0,4},{4,0},{8,12},{12,8},{16,20},{20,16},{24,28},{28,24},{32,36},... | collective-permute-start | bytes 786440 | tf_op jit(solution)/shard_map/ppermute | solution.py:31
  180.4 9.3 %collective-permute-start.58 = (bf16[8,64,128]{2,1,0:T(8,128)(2,1)S(1)}, bf16[8,64,128]{2,1,0:T(8,128)(2,1)S(1)}, u32[]{:S(2)}, u32[]{:S(2)}) collective-permute-start(bf16[8,64,128]{2,1,0:T(8,128)(2,1)S(1)} %get-tuple-element.123), channel_id=1, source_target_pairs={{0,1},{1,0},{2,3},{3,2},{4,5},{5,4},{6,7},{7,6},{8,9},{9,8},{10,11... | collective-permute-start | bytes 393224 | tf_op jit(solution)/shard_map/ppermute | solution.py:31
  182.5 9.8 %collective-permute-start.59 = (bf16[8,64,128]{2,1,0:T(8,128)(2,1)S(1)}, bf16[8,64,128]{2,1,0:T(8,128)(2,1)S(1)}, u32[]{:S(2)}, u32[]{:S(2)}) collective-permute-start(bf16[8,64,128]{2,1,0:T(8,128)(2,1)S(1)} %get-tuple-element.124), channel_id=1, source_target_pairs={{0,2},{1,3},{2,0},{3,1},{4,6},{5,7},{6,4},{7,5},{8,10},{9,11},{10,... | collective-permute-start | bytes 393224 | tf_op jit(solution)/shard_map/ppermute | solution.py:31
  (45 other events, 348.0 us)

commit v6 on v5

--- a/solution.py
+++ b/solution.py
@@ -168,9 +168,12 @@
         low_ref[b] = v.astype(BF16)
 
 
-def mid_kernel(low_ref, q1_ref, q2_ref, q3_ref, pa_ref, cp_ref, zp_ref, own4_ref, o0_ref, o1_ref, o2_ref, o3_ref):
+def pack_kernel(low_ref, q1_ref, q2_ref, q3_ref, own4_ref):
     for k, src in enumerate((low_ref, q1_ref, q2_ref, q3_ref)):
         own4_ref[8 * k : 8 * k + 8] = src[...]
+
+
+def mid_kernel(pa_ref, cp_ref, zp_ref, o0_ref, o1_ref, o2_ref, o3_ref):
     o0_ref[...] = pa_ref[0:8]
     o1_ref[...] = pa_ref[8:16].astype(BF16)
     for k, out in ((0, o2_ref), (8, o3_ref)):
@@ -403,14 +406,11 @@
             nbytes=3_000_000,
         )
         ra_zp, ra_cp = swap_next(pa_zp), swap_core(pa_cp)
-        own4, o0, o1, o2, o3 = call(
-            mid_kernel,
-            [VM] * 7,
-            [((32, K, TILE), BF16), (blk, F32)] + [(blk, BF16)] * 3,
-            [],
-            (blow, *q, pa_own, ra_cp, ra_zp),
-        )
+        (own4,) = call(pack_kernel, [VM] * 4, [((32, K, TILE), BF16)], [], (blow, *q))
         m_zp = swap_next(own4)
+        o0, o1, o2, o3 = call(
+            mid_kernel, [VM] * 3, [(blk, F32)] + [(blk, BF16)] * 3, [], (pa_own, ra_cp, ra_zp)
+        )
         b1, b2, b3 = (swap_y(o, k) for k, o in ((1, o1), (2, o2), (3, o3)))
         m_cp = swap_core(own4)
         pm_own, pm_cp, pm_zp = call(

time: 228 us -> 225 us (0.987)
  waiting for transfers between devices: 92.8 us -> 85.8 us
  starting transfers between devices: 94.4 us -> 98 us
    ppermute x64, waiting for transfers between devices: 92.8 us -> 85.8 us  [swap(): return lax.ppermute(value, axis, [(i, i ^ distance) for i in range(size)])]
    ppermute x64, starting transfers between devices: 88.6 us -> 92.1 us  [swap(): return lax.ppermute(value, axis, [(i, i ^ distance) for i in range(size)])]
    pallas_call x20 -> x22, Pallas kernels: 33.5 us -> 33.5 us  [call(): pl.pallas_call(body, in_specs=specs, out_specs=tuple((VM for _ in outs)),...]
  transfers between devices with their start and end apart: 72 -> 72, of which waited for: 42 -> 46; matrix products, arithmetic and copies ran while one was open for 0% -> 0% of each run, Pallas kernels for 6% -> 8%
where the time goes in v6:
time: 225 us; the launch traced here: 223 us
  starting transfers between devices  98 us (44%)
  waiting for transfers between devices  85.8 us (38%)
  Pallas kernels  33.5 us (15%)
  local copies, waits for them, and re-layouts  2.36 us (1%)
    ppermute x64, starting transfers between devices, swap(): return lax.ppermute(value, axis, [(i, i ^ distance) for i in range(size)])  92.1 us
    ppermute x64, waiting for transfers between devices, swap(): return lax.ppermute(value, axis, [(i, i ^ distance) for i in range(size)])  85.8 us
    pallas_call x22, Pallas kernels, call(): pl.pallas_call(body, in_specs=specs, out_specs=tuple((VM for _ in outs)),...  33.5 us
    ppermute x8, starting transfers between devices, swap_next(): return lax.ppermute(value, DOM, route)  5.83 us
  transfers between devices with their start and end apart: 72, of which 46 were waited for; matrix products, arithmetic and copies ran while one was open for 0% of the time, Pallas kernels for 8%

profile of v6, /device:TPU:0, one launch (start us, length us, event | category | flops | bytes accessed | tf_op | source)
XLA Modules:
  0.0 223.3 jit_solution(542707876553298916)
XLA Ops:
  5.9 3.1 %collective-permute-start.3 = (f32[64,64]{1,0:T(8,128)S(1)}, f32[64,64]{1,0:T(8,128)S(1)}, u32[]{:S(2)}, u32[]{:S(2)}) collective-permute-start(f32[64,64]{1,0:T(8,128)S(1)} %add.154), channel_id=1, source_target_pairs={{0,3},{1,2},{2,1},{3,0},{4,7},{5,6},{6,5},{7,4},{8,11},{9,10},{10,... | collective-permute-start | bytes 49160 | tf_op jit(solution)/shard_map/ppermute | solution.py:31
  11.0 3.4 %collective-permute-done.2 = f32[64,64]{1,0:T(8,128)S(1)} collective-permute-done((f32[64,64]{1,0:T(8,128)S(1)}, f32[64,64]{1,0:T(8,128)S(1)}, u32[]{:S(2)}, u32[]{:S(2)}) %collective-permute-start.2) | collective-permute-done | bytes 16416 | tf_op jit(solution)/shard_map/ppermute | solution.py:31
  14.5 4.1 %collective-permute-start.6 = (f32[64,64]{1,0:T(8,128)S(1)}, f32[64,64]{1,0:T(8,128)S(1)}, u32[]{:S(2)}, u32[]{:S(2)}) collective-permute-start(f32[64,64]{1,0:T(8,128)S(1)} %add_add_fusion.8), channel_id=1, source_target_pairs={{0,24},{4,28},{8,16},{12,20},{16,8},{20,12},{24,0},{28,4},{32,56},... | collective-permute-start | bytes 49160 | tf_op jit(solution)/shard_map/ppermute | solution.py:31
  20.5 3.5 %collective-permute-done.5 = f32[64,64]{1,0:T(8,128)S(1)} collective-permute-done((f32[64,64]{1,0:T(8,128)S(1)}, f32[64,64]{1,0:T(8,128)S(1)}, u32[]{:S(2)}, u32[]{:S(2)}) %collective-permute-start.5) | collective-permute-done | bytes 16416 | tf_op jit(solution)/shard_map/ppermute | solution.py:31
  24.0 2.8 %collective-permute-start.9 = (f32[64,64]{1,0:T(8,128)S(1)}, f32[64,64]{1,0:T(8,128)S(1)}, u32[]{:S(2)}, u32[]{:S(2)}) collective-permute-start(f32[64,64]{1,0:T(8,128)S(1)} %add_add_fusion.7), channel_id=1, source_target_pairs={{0,96},{4,100},{8,104},{12,108},{16,112},{20,116},{24,120},{28,124... | collective-permute-start | bytes 49160 | tf_op jit(solution)/shard_map/ppermute | solution.py:31
  29.2 3.1 %collective-permute-done.8 = f32[64,64]{1,0:T(8,128)S(1)} collective-permute-done((f32[64,64]{1,0:T(8,128)S(1)}, f32[64,64]{1,0:T(8,128)S(1)}, u32[]{:S(2)}, u32[]{:S(2)}) %collective-permute-start.8) | collective-permute-done | bytes 16416 | tf_op jit(solution)/shard_map/ppermute | solution.py:31
  32.3 3.3 %shard_map.103 = (f32[8,64,128]{2,1,0:T(8,128)S(1)}, bf16[8,64,128]{2,1,0:T(8,128)(2,1)S(1)}, f32[64,64]{1,0:T(8,128)S(1)}) custom-call(f32[64,64]{1,0:T(8,128)S(1)} %add_add_fusion.6.g_ref, f32[8,64,128]{2,1,0:T(8,128)S(1)} %copy-done.3, f32[1]{0:T(128)} %constant.108.clone.1.n_ref.refs_2_), custom_call_target="tpu_custom_call" | custom-call | tf_op jit(solution)/shard_map/pallas_call | solution.py:80
  44.9 3.7 %collective-permute-start.13 = (bf16[32,64,128]{2,1,0:T(8,128)(2,1)S(1)}, bf16[32,64,128]{2,1,0:T(8,128)(2,1)S(1)}, u32[]{:S(2)}, u32[]{:S(2)}) collective-permute-start(bf16[32,64,128]{2,1,0:T(8,128)(2,1)S(1)} %shard_map.104.own_ref), channel_id=1, source_target_pairs={{0,4},{4,0},{8,12},{12,8},{16,20},{20,16},{24,28},{28,24},{32,36},... | collective-permute-start | bytes 1572872 | tf_op jit(solution)/shard_map/ppermute | solution.py:31
  54.2 3.7 %collective-permute-done.23.b2_ref = bf16[8,64,128]{2,1,0:T(8,128)(2,1)S(1)} collective-permute-done((bf16[8,64,128]{2,1,0:T(8,128)(2,1)S(1)}, bf16[8,64,128]{2,1,0:T(8,128)(2,1)S(1)}, u32[]{:S(2)}, u32[]{:S(2)}) %collective-permute-start.23) | collective-permute-done | bytes 131104 | tf_op jit(solution)/shard_map/ppermute | solution.py:31
  57.9 3.2 %collective-permute-done.24.b3_ref = bf16[8,64,128]{2,1,0:T(8,128)(2,1)S(1)} collective-permute-done((bf16[8,64,128]{2,1,0:T(8,128)(2,1)S(1)}, bf16[8,64,128]{2,1,0:T(8,128)(2,1)S(1)}, u32[]{:S(2)}, u32[]{:S(2)}) %collective-permute-start.24) | collective-permute-done | bytes 131104 | tf_op jit(solution)/shard_map/ppermute | solution.py:31
  61.1 2.4 %shard_map.110 = (f32[32,64,128]{2,1,0:T(8,128)S(1)}, bf16[32,64,128]{2,1,0:T(8,128)(2,1)S(1)}, bf16[32,64,128]{2,1,0:T(8,128)(2,1)S(1)}) custom-call(s32[104]{0:T(128)S(1)} %get-tuple-element.68.col_ref, s32[104]{0:T(128)S(1)} %get-tuple-element.69.row_ref, f32[8,64,128]{2,1,0:T(8,128)S(1)} %get-tuple-element.79.back0_ref, ...), custom_call_target="tpu_custom_call" | custom-call | flops 218000000 | bytes 5000000 | tf_op jit(solution)/shard_map/pallas_call | solution.py:80
  64.5 3.4 %shard_map.105 = (f32[8,64,128]{2,1,0:T(8,128)S(1)}, bf16[8,64,128]{2,1,0:T(8,128)(2,1)S(1)}) custom-call(s32[104]{0:T(128)S(1)} %get-tuple-element.68.col_ref, s32[104]{0:T(128)S(1)} %get-tuple-element.69.row_ref, bf16[32,64,128]{2,1,0:T(8,128)(2,1)S(1)} %shard_map.104.own_ref, bf16[32,64,128]{2,1,0:T(8,128)(2,1)S(1)} %collective-permute-done.13.cp_ref, ...), custom_call_target="tpu_custom_call" | custom-call | flops 218000000 | bytes 5000000 | tf_op jit(solution)/shard_map/pallas_call | solution.py:80
  70.3 4.1 %collective-permute-done.17.b_ref.refs_4_ = bf16[8,64,128]{2,1,0:T(8,128)(2,1)S(1)} collective-permute-done((bf16[8,64,128]{2,1,0:T(8,128)(2,1)S(1)}, bf16[8,64,128]{2,1,0:T(8,128)(2,1)S(1)}, u32[]{:S(2)}, u32[]{:S(2)}) %collective-permute-start.17) | collective-permute-done | bytes 131104 | tf_op jit(solution)/shard_map/ppermute | solution.py:31
  74.4 2.6 %collective-permute-done.16.a_ref.refs_3_ = bf16[8,64,128]{2,1,0:T(8,128)(2,1)S(1)} collective-permute-done((bf16[8,64,128]{2,1,0:T(8,128)(2,1)S(1)}, bf16[8,64,128]{2,1,0:T(8,128)(2,1)S(1)}, u32[]{:S(2)}, u32[]{:S(2)}) %collective-permute-start.16) | collective-permute-done | bytes 131104 | tf_op jit(solution)/shard_map/ppermute | solution.py:31
  77.7 5.3 %collective-permute-start.18 = (bf16[16,64,128]{2,1,0:T(8,128)(2,1)S(1)}, bf16[16,64,128]{2,1,0:T(8,128)(2,1)S(1)}, u32[]{:S(2)}, u32[]{:S(2)}) collective-permute-start(bf16[16,64,128]{2,1,0:T(8,128)(2,1)S(1)} %shard_map.106), channel_id=1, source_target_pairs={{0,4},{4,0},{8,12},{12,8},{16,20},{20,16},{24,28},{28,24},{32,36},... | collective-permute-start | bytes 786440 | tf_op jit(solution)/shard_map/ppermute | solution.py:31
  93.1 2.7 %collective-permute-done.28.refs_2_ = bf16[8,64,128]{2,1,0:T(8,128)(2,1)S(1)} collective-permute-done((bf16[8,64,128]{2,1,0:T(8,128)(2,1)S(1)}, bf16[8,64,128]{2,1,0:T(8,128)(2,1)S(1)}, u32[]{:S(2)}, u32[]{:S(2)}) %collective-permute-start.28) | collective-permute-done | bytes 131104 | tf_op jit(solution)/shard_map/ppermute | solution.py:31
  106.1 3.5 %collective-permute-start.36 = (f32[64,128]{1,0:T(8,128)S(1)}, f32[64,128]{1,0:T(8,128)S(1)}, u32[]{:S(2)}, u32[]{:S(2)}) collective-permute-start(f32[64,128]{1,0:T(8,128)S(1)} %add_add_fusion.5), channel_id=1, source_target_pairs={{0,24},{4,28},{8,16},{12,20},{16,8},{20,12},{24,0},{28,4},{32,56},... | collective-permute-start | bytes 98312 | tf_op jit(solution)/shard_map/ppermute | solution.py:31
  111.5 3.5 %collective-permute-done.35 = f32[64,128]{1,0:T(8,128)S(1)} collective-permute-done((f32[64,128]{1,0:T(8,128)S(1)}, f32[64,128]{1,0:T(8,128)S(1)}, u32[]{:S(2)}, u32[]{:S(2)}) %collective-permute-start.35) | collective-permute-done | bytes 32800 | tf_op jit(solution)/shard_map/ppermute | solution.py:31
  122.8 5.0 %shard_map.113 = (f32[8,64,128]{2,1,0:T(8,128)S(1)}, f32[8,64,128]{2,1,0:T(8,128)S(1)}, f32[8,64,128]{2,1,0:T(8,128)S(1)}, f32[8,64,128]{2,1,0:T(8,128)S(1)}, bf...) custom-call(f32[64,128]{1,0:T(8,128)S(1)} %get-tuple-element.131.refs_0_, ...), custom_call_target="tpu_custom_call" | custom-call | tf_op jit(solution)/shard_map/pallas_call | solution.py:80
  133.9 3.5 %collective-permute-done.43.q3_ref = bf16[8,64,128]{2,1,0:T(8,128)(2,1)S(1)} collective-permute-done((bf16[8,64,128]{2,1,0:T(8,128)(2,1)S(1)}, bf16[8,64,128]{2,1,0:T(8,128)(2,1)S(1)}, u32[]{:S(2)}, u32[]{:S(2)}) %collective-permute-start.43) | collective-permute-done | bytes 131104 | tf_op jit(solution)/shard_map/ppermute | solution.py:31
  138.8 2.9 %collective-permute-start.44 = (bf16[32,64,128]{2,1,0:T(8,128)(2,1)S(1)}, bf16[32,64,128]{2,1,0:T(8,128)(2,1)S(1)}, u32[]{:S(2)}, u32[]{:S(2)}) collective-permute-start(bf16[32,64,128]{2,1,0:T(8,128)(2,1)S(1)} %shard_map.114.own_ref), channel_id=1, source_target_pairs={{0,4},{4,0},{8,12},{12,8},{16,20},{20,16},{24,28},{28,24},{32,36},... | collective-permute-start | bytes 1572872 | tf_op jit(solution)/shard_map/ppermute | solution.py:31
  148.3 2.9 %collective-permute-done.54.b2_ref = bf16[8,64,128]{2,1,0:T(8,128)(2,1)S(1)} collective-permute-done((bf16[8,64,128]{2,1,0:T(8,128)(2,1)S(1)}, bf16[8,64,128]{2,1,0:T(8,128)(2,1)S(1)}, u32[]{:S(2)}, u32[]{:S(2)}) %collective-permute-start.54) | collective-permute-done | bytes 131104 | tf_op jit(solution)/shard_map/ppermute | solution.py:31
  153.3 2.4 %shard_map.120 = (f32[32,64,128]{2,1,0:T(8,128)S(1)}, bf16[32,64,128]{2,1,0:T(8,128)(2,1)S(1)}, bf16[32,64,128]{2,1,0:T(8,128)(2,1)S(1)}) custom-call(s32[104]{0:T(128)S(1)} %get-tuple-element.68.col_ref, s32[104]{0:T(128)S(1)} %get-tuple-element.69.row_ref, f32[8,64,128]{2,1,0:T(8,128)S(1)} %get-tuple-element.108.back0_ref, ...), custom_call_target="tpu_custom_call" | custom-call | flops 218000000 | bytes 5000000 | tf_op jit(solution)/shard_map/pallas_call | solution.py:80
  156.8 3.4 %shard_map.115 = (f32[8,64,128]{2,1,0:T(8,128)S(1)}, bf16[8,64,128]{2,1,0:T(8,128)(2,1)S(1)}) custom-call(s32[104]{0:T(128)S(1)} %get-tuple-element.68.col_ref, s32[104]{0:T(128)S(1)} %get-tuple-element.69.row_ref, bf16[32,64,128]{2,1,0:T(8,128)(2,1)S(1)} %shard_map.114.own_ref, bf16[32,64,128]{2,1,0:T(8,128)(2,1)S(1)} %collective-permute-done.44.cp_ref, ...), custom_call_target="tpu_custom_call" | custom-call | flops 218000000 | bytes 5000000 | tf_op jit(solution)/shard_map/pallas_call | solution.py:80
  162.1 4.4 %collective-permute-done.48.b_ref.refs_4_ = bf16[8,64,128]{2,1,0:T(8,128)(2,1)S(1)} collective-permute-done((bf16[8,64,128]{2,1,0:T(8,128)(2,1)S(1)}, bf16[8,64,128]{2,1,0:T(8,128)(2,1)S(1)}, u32[]{:S(2)}, u32[]{:S(2)}) %collective-permute-start.48) | collective-permute-done | bytes 131104 | tf_op jit(solution)/shard_map/ppermute | solution.py:31
  169.3 5.9 %collective-permute-start.49 = (bf16[16,64,128]{2,1,0:T(8,128)(2,1)S(1)}, bf16[16,64,128]{2,1,0:T(8,128)(2,1)S(1)}, u32[]{:S(2)}, u32[]{:S(2)}) collective-permute-start(bf16[16,64,128]{2,1,0:T(8,128)(2,1)S(1)} %shard_map.116), channel_id=1, source_target_pairs={{0,4},{4,0},{8,12},{12,8},{16,20},{20,16},{24,28},{28,24},{32,36},... | collective-permute-start | bytes 786440 | tf_op jit(solution)/shard_map/ppermute | solution.py:31
  178.8 2.8 %collective-permute-done.46.refs_2_ = bf16[8,64,128]{2,1,0:T(8,128)(2,1)S(1)} collective-permute-done((bf16[8,64,128]{2,1,0:T(8,128)(2,1)S(1)}, bf16[8,64,128]{2,1,0:T(8,128)(2,1)S(1)}, u32[]{:S(2)}, u32[]{:S(2)}) %collective-permute-start.46) | collective-permute-done | bytes 131104 | tf_op jit(solution)/shard_map/ppermute | solution.py:31
  185.0 2.6 %collective-permute-done.59.refs_2_ = bf16[8,64,128]{2,1,0:T(8,128)(2,1)S(1)} collective-permute-done((bf16[8,64,128]{2,1,0:T(8,128)(2,1)S(1)}, bf16[8,64,128]{2,1,0:T(8,128)(2,1)S(1)}, u32[]{:S(2)}, u32[]{:S(2)}) %collective-permute-start.59) | collective-permute-done | bytes 131104 | tf_op jit(solution)/shard_map/ppermute | solution.py:31
  192.8 2.4 %collective-permute-start.62 = (f32[96,128]{1,0:T(8,128)S(1)}, f32[96,128]{1,0:T(8,128)S(1)}, u32[]{:S(2)}, u32[]{:S(2)}) collective-permute-start(f32[96,128]{1,0:T(8,128)S(1)} %select_add_fusion), channel_id=1, source_target_pairs={{0,1},{1,0},{2,3},{3,2},{4,5},{5,4},{6,7},{7,6},{8,9},{9,8},{10,11... | collective-permute-start | bytes 147464 | tf_op jit(solution)/shard_map/ppermute | solution.py:31
  198.4 5.0 %collective-permute-start.67 = (f32[96,128]{1,0:T(8,128)S(1)}, f32[96,128]{1,0:T(8,128)S(1)}, u32[]{:S(2)}, u32[]{:S(2)}) collective-permute-start(f32[96,128]{1,0:T(8,128)S(1)} %add_add_fusion.2), channel_id=1, source_target_pairs={{0,24},{4,28},{8,16},{12,20},{16,8},{20,12},{24,0},{28,4},{32,56},... | collective-permute-start | bytes 147464 | tf_op jit(solution)/shard_map/ppermute | solution.py:31
  205.5 3.5 %collective-permute-done.66 = f32[96,128]{1,0:T(8,128)S(1)} collective-permute-done((f32[96,128]{1,0:T(8,128)S(1)}, f32[96,128]{1,0:T(8,128)S(1)}, u32[]{:S(2)}, u32[]{:S(2)}) %collective-permute-start.66) | collective-permute-done | bytes 49184 | tf_op jit(solution)/shard_map/ppermute | solution.py:31
  217.2 6.1 %shard_map.123 = (f32[8,64,128]{2,1,0:T(8,128)}, f32[8,64,128]{2,1,0:T(8,128)}, f32[8,64,128]{2,1,0:T(8,128)}, f32[8,64,128]{2,1,0:T(8,128)}) custom-call(f32[96,128]{1,0:T(8,128)S(1)} %get-tuple-element.129.refs_0_, f32[96,128]{1,0:T(8,128)S(1)} %get-tuple-element.128.refs_1_, f32[1]{0:T(128)} %constant.108.clone.1.n_ref.refs_2_, ...), custom_call_target="tpu_custom_call" | custom-call | tf_op jit(solution)/shard_map/pallas_call | solution.py:80
  (164 shorter events, 106.8 us)
Async XLA Ops:
  35.6 7.4 %collective-permute-start.12 = (bf16[8,64,128]{2,1,0:T(8,128)(2,1)S(1)}, bf16[8,64,128]{2,1,0:T(8,128)(2,1)S(1)}, u32[]{:S(2)}, u32[]{:S(2)}) collective-permute-start(bf16[8,64,128]{2,1,0:T(8,128)(2,1)S(1)} %get-tuple-element.72.low_ref), channel_id=1, source_target_pairs={{0,3},{1,2},{2,1},{3,0},{4,7},{5,6},{6,5},{7,4},{8,11},{9,10},{10,... | collective-permute-start | bytes 393224 | tf_op jit(solution)/shard_map/ppermute | solution.py:31
  37.0 6.5 %collective-permute-start.11 = (bf16[8,64,128]{2,1,0:T(8,128)(2,1)S(1)}, bf16[8,64,128]{2,1,0:T(8,128)(2,1)S(1)}, u32[]{:S(2)}, u32[]{:S(2)}) collective-permute-start(bf16[8,64,128]{2,1,0:T(8,128)(2,1)S(1)} %get-tuple-element.72.low_ref), channel_id=1, source_target_pairs={{0,2},{1,3},{2,0},{3,1},{4,6},{5,7},{6,4},{7,5},{8,10},{9,11},{10,... | collective-permute-start | bytes 393224 | tf_op jit(solution)/shard_map/ppermute | solution.py:31
  44.2 20.3 %collective-permute-start.14 = (bf16[32,64,128]{2,1,0:T(8,128)(2,1)S(1)}, bf16[32,64,128]{2,1,0:T(8,128)(2,1)S(1)}, u32[]{:S(2)}, u32[]{:S(2)}) collective-permute-start(bf16[32,64,128]{2,1,0:T(8,128)(2,1)S(1)} %shard_map.104.own_ref), channel_id=1, source_target_pairs={{4,8},{8,4},{12,16},{16,12},{20,24},{24,20},{28,32},{32,28},{36,40... | collective-permute-start | bytes 1572872 | tf_op jit(solution)/shard_map/ppermute | solution.py:47
  44.9 19.6 %collective-permute-start.13 = (bf16[32,64,128]{2,1,0:T(8,128)(2,1)S(1)}, bf16[32,64,128]{2,1,0:T(8,128)(2,1)S(1)}, u32[]{:S(2)}, u32[]{:S(2)}) collective-permute-start(bf16[32,64,128]{2,1,0:T(8,128)(2,1)S(1)} %shard_map.104.own_ref), channel_id=1, source_target_pairs={{0,4},{4,0},{8,12},{12,8},{16,20},{20,16},{24,28},{28,24},{32,36},... | collective-permute-start | bytes 1572872 | tf_op jit(solution)/shard_map/ppermute | solution.py:31
  49.2 8.6 %collective-permute-start.23 = (bf16[8,64,128]{2,1,0:T(8,128)(2,1)S(1)}, bf16[8,64,128]{2,1,0:T(8,128)(2,1)S(1)}, u32[]{:S(2)}, u32[]{:S(2)}) collective-permute-start(bf16[8,64,128]{2,1,0:T(8,128)(2,1)S(1)} %get-tuple-element.81), channel_id=1, source_target_pairs={{0,2},{1,3},{2,0},{3,1},{4,6},{5,7},{6,4},{7,5},{8,10},{9,11},{10,... | collective-permute-start | bytes 393224 | tf_op jit(solution)/shard_map/ppermute | solution.py:31
  51.6 9.5 %collective-permute-start.24 = (bf16[8,64,128]{2,1,0:T(8,128)(2,1)S(1)}, bf16[8,64,128]{2,1,0:T(8,128)(2,1)S(1)}, u32[]{:S(2)}, u32[]{:S(2)}) collective-permute-start(bf16[8,64,128]{2,1,0:T(8,128)(2,1)S(1)} %get-tuple-element.82), channel_id=1, source_target_pairs={{0,3},{1,2},{2,1},{3,0},{4,7},{5,6},{6,5},{7,4},{8,11},{9,10},{10,... | collective-permute-start | bytes 393224 | tf_op jit(solution)/shard_map/ppermute | solution.py:31
  63.5 19.5 %collective-permute-start.25 = (bf16[32,64,128]{2,1,0:T(8,128)(2,1)S(1)}, bf16[32,64,128]{2,1,0:T(8,128)(2,1)S(1)}, u32[]{:S(2)}, u32[]{:S(2)}) collective-permute-start(bf16[32,64,128]{2,1,0:T(8,128)(2,1)S(1)} %get-tuple-element.84), channel_id=1, source_target_pairs={{0,4},{4,0},{8,12},{12,8},{16,20},{20,16},{24,28},{28,24},{32,36},... | collective-permute-start | bytes 1572872 | tf_op jit(solution)/shard_map/ppermute | solution.py:31
  63.7 19.3 %collective-permute-start.26 = (bf16[32,64,128]{2,1,0:T(8,128)(2,1)S(1)}, bf16[32,64,128]{2,1,0:T(8,128)(2,1)S(1)}, u32[]{:S(2)}, u32[]{:S(2)}) collective-permute-start(bf16[32,64,128]{2,1,0:T(8,128)(2,1)S(1)} %get-tuple-element.85), channel_id=1, source_target_pairs={{4,8},{8,4},{12,16},{16,12},{20,24},{24,20},{28,32},{32,28},{36,40... | collective-permute-start | bytes 1572872 | tf_op jit(solution)/shard_map/ppermute | solution.py:47
  70.0 7.0 %collective-permute-start.16 = (bf16[8,64,128]{2,1,0:T(8,128)(2,1)S(1)}, bf16[8,64,128]{2,1,0:T(8,128)(2,1)S(1)}, u32[]{:S(2)}, u32[]{:S(2)}) collective-permute-start(bf16[8,64,128]{2,1,0:T(8,128)(2,1)S(1)} %get-tuple-element.73.refs_1_), channel_id=1, source_target_pairs={{0,2},{1,3},{2,0},{3,1},{4,6},{5,7},{6,4},{7,5},{8,10},{9,11},{10,... | collective-permute-start | bytes 393224 | tf_op jit(solution)/shard_map/ppermute | solution.py:31
  77.0 14.5 %collective-permute-start.19 = (bf16[16,64,128]{2,1,0:T(8,128)(2,1)S(1)}, bf16[16,64,128]{2,1,0:T(8,128)(2,1)S(1)}, u32[]{:S(2)}, u32[]{:S(2)}) collective-permute-start(bf16[16,64,128]{2,1,0:T(8,128)(2,1)S(1)} %shard_map.106), channel_id=1, source_target_pairs={{4,8},{8,4},{12,16},{16,12},{20,24},{24,20},{28,32},{32,28},{36,40... | collective-permute-start | bytes 786440 | tf_op jit(solution)/shard_map/ppermute | solution.py:47
  77.7 13.8 %collective-permute-start.18 = (bf16[16,64,128]{2,1,0:T(8,128)(2,1)S(1)}, bf16[16,64,128]{2,1,0:T(8,128)(2,1)S(1)}, u32[]{:S(2)}, u32[]{:S(2)}) collective-permute-start(bf16[16,64,128]{2,1,0:T(8,128)(2,1)S(1)} %shard_map.106), channel_id=1, source_target_pairs={{0,4},{4,0},{8,12},{12,8},{16,20},{20,16},{24,28},{28,24},{32,36},... | collective-permute-start | bytes 786440 | tf_op jit(solution)/shard_map/ppermute | solution.py:31
  83.2 9.9 %collective-permute-start.27 = (bf16[8,64,128]{2,1,0:T(8,128)(2,1)S(1)}, bf16[8,64,128]{2,1,0:T(8,128)(2,1)S(1)}, u32[]{:S(2)}, u32[]{:S(2)}) collective-permute-start(bf16[8,64,128]{2,1,0:T(8,128)(2,1)S(1)} %get-tuple-element.90), channel_id=1, source_target_pairs={{0,1},{1,0},{2,3},{3,2},{4,5},{5,4},{6,7},{7,6},{8,9},{9,8},{10,11... | collective-permute-start | bytes 393224 | tf_op jit(solution)/shard_map/ppermute | solution.py:31
  85.3 10.5 %collective-permute-start.28 = (bf16[8,64,128]{2,1,0:T(8,128)(2,1)S(1)}, bf16[8,64,128]{2,1,0:T(8,128)(2,1)S(1)}, u32[]{:S(2)}, u32[]{:S(2)}) collective-permute-start(bf16[8,64,128]{2,1,0:T(8,128)(2,1)S(1)} %get-tuple-element.91), channel_id=1, source_target_pairs={{0,2},{1,3},{2,0},{3,1},{4,6},{5,7},{6,4},{7,5},{8,10},{9,11},{10,... | collective-permute-start | bytes 393224 | tf_op jit(solution)/shard_map/ppermute | solution.py:31
  89.4 7.8 %collective-permute-start.29 = (bf16[8,64,128]{2,1,0:T(8,128)(2,1)S(1)}, bf16[8,64,128]{2,1,0:T(8,128)(2,1)S(1)}, u32[]{:S(2)}, u32[]{:S(2)}) collective-permute-start(bf16[8,64,128]{2,1,0:T(8,128)(2,1)S(1)} %get-tuple-element.92), channel_id=1, source_target_pairs={{0,3},{1,2},{2,1},{3,0},{4,7},{5,6},{6,5},{7,4},{8,11},{9,10},{10,... | collective-permute-start | bytes 393224 | tf_op jit(solution)/shard_map/ppermute | solution.py:31
  127.8 9.6 %collective-permute-start.43 = (bf16[8,64,128]{2,1,0:T(8,128)(2,1)S(1)}, bf16[8,64,128]{2,1,0:T(8,128)(2,1)S(1)}, u32[]{:S(2)}, u32[]{:S(2)}) collective-permute-start(bf16[8,64,128]{2,1,0:T(8,128)(2,1)S(1)} %get-tuple-element.98.low_ref), channel_id=1, source_target_pairs={{0,3},{1,2},{2,1},{3,0},{4,7},{5,6},{6,5},{7,4},{8,11},{9,10},{10,... | collective-permute-start | bytes 393224 | tf_op jit(solution)/shard_map/ppermute | solution.py:31
  129.6 7.9 %collective-permute-start.42 = (bf16[8,64,128]{2,1,0:T(8,128)(2,1)S(1)}, bf16[8,64,128]{2,1,0:T(8,128)(2,1)S(1)}, u32[]{:S(2)}, u32[]{:S(2)}) collective-permute-start(bf16[8,64,128]{2,1,0:T(8,128)(2,1)S(1)} %get-tuple-element.98.low_ref), channel_id=1, source_target_pairs={{0,2},{1,3},{2,0},{3,1},{4,6},{5,7},{6,4},{7,5},{8,10},{9,11},{10,... | collective-permute-start | bytes 393224 | tf_op jit(solution)/shard_map/ppermute | solution.py:31
  131.0 7.0 %collective-permute-start.41 = (bf16[8,64,128]{2,1,0:T(8,128)(2,1)S(1)}, bf16[8,64,128]{2,1,0:T(8,128)(2,1)S(1)}, u32[]{:S(2)}, u32[]{:S(2)}) collective-permute-start(bf16[8,64,128]{2,1,0:T(8,128)(2,1)S(1)} %get-tuple-element.98.low_ref), channel_id=1, source_target_pairs={{0,1},{1,0},{2,3},{3,2},{4,5},{5,4},{6,7},{7,6},{8,9},{9,8},{10,11... | collective-permute-start | bytes 393224 | tf_op jit(solution)/shard_map/ppermute | solution.py:31
  133.1 8.5 %collective-permute-start.51 = (bf16[16,64,128]{2,1,0:T(8,128)(2,1)S(1)}, bf16[16,64,128]{2,1,0:T(8,128)(2,1)S(1)}, u32[]{:S(2)}, u32[]{:S(2)}) collective-permute-start(bf16[16,64,128]{2,1,0:T(8,128)(2,1)S(1)} %get-tuple-element.106), channel_id=1, source_target_pairs={{0,4},{4,0},{8,12},{12,8},{16,20},{20,16},{24,28},{28,24},{32,36},... | collective-permute-start | bytes 786440 | tf_op jit(solution)/shard_map/ppermute | solution.py:31
  133.2 8.4 %collective-permute-start.52 = (bf16[16,64,128]{2,1,0:T(8,128)(2,1)S(1)}, bf16[16,64,128]{2,1,0:T(8,128)(2,1)S(1)}, u32[]{:S(2)}, u32[]{:S(2)}) collective-permute-start(bf16[16,64,128]{2,1,0:T(8,128)(2,1)S(1)} %get-tuple-element.107), channel_id=1, source_target_pairs={{4,8},{8,4},{12,16},{16,12},{20,24},{24,20},{28,32},{32,28},{36,40... | collective-permute-start | bytes 786440 | tf_op jit(solution)/shard_map/ppermute | solution.py:47
  138.1 18.6 %collective-permute-start.45 = (bf16[32,64,128]{2,1,0:T(8,128)(2,1)S(1)}, bf16[32,64,128]{2,1,0:T(8,128)(2,1)S(1)}, u32[]{:S(2)}, u32[]{:S(2)}) collective-permute-start(bf16[32,64,128]{2,1,0:T(8,128)(2,1)S(1)} %shard_map.114.own_ref), channel_id=1, source_target_pairs={{4,8},{8,4},{12,16},{16,12},{20,24},{24,20},{28,32},{32,28},{36,40... | collective-permute-start | bytes 1572872 | tf_op jit(solution)/shard_map/ppermute | solution.py:47
  138.8 18.0 %collective-permute-start.44 = (bf16[32,64,128]{2,1,0:T(8,128)(2,1)S(1)}, bf16[32,64,128]{2,1,0:T(8,128)(2,1)S(1)}, u32[]{:S(2)}, u32[]{:S(2)}) collective-permute-start(bf16[32,64,128]{2,1,0:T(8,128)(2,1)S(1)} %shard_map.114.own_ref), channel_id=1, source_target_pairs={{0,4},{4,0},{8,12},{12,8},{16,20},{20,16},{24,28},{28,24},{32,36},... | collective-permute-start | bytes 1572872 | tf_op jit(solution)/shard_map/ppermute | solution.py:31
  142.7 8.4 %collective-permute-start.54 = (bf16[8,64,128]{2,1,0:T(8,128)(2,1)S(1)}, bf16[8,64,128]{2,1,0:T(8,128)(2,1)S(1)}, u32[]{:S(2)}, u32[]{:S(2)}) collective-permute-start(bf16[8,64,128]{2,1,0:T(8,128)(2,1)S(1)} %get-tuple-element.110), channel_id=1, source_target_pairs={{0,2},{1,3},{2,0},{3,1},{4,6},{5,7},{6,4},{7,5},{8,10},{9,11},{10,... | collective-permute-start | bytes 393224 | tf_op jit(solution)/shard_map/ppermute | solution.py:31
  144.8 8.5 %collective-permute-start.55 = (bf16[8,64,128]{2,1,0:T(8,128)(2,1)S(1)}, bf16[8,64,128]{2,1,0:T(8,128)(2,1)S(1)}, u32[]{:S(2)}, u32[]{:S(2)}) collective-permute-start(bf16[8,64,128]{2,1,0:T(8,128)(2,1)S(1)} %get-tuple-element.111), channel_id=1, source_target_pairs={{0,3},{1,2},{2,1},{3,0},{4,7},{5,6},{6,5},{7,4},{8,11},{9,10},{10,... | collective-permute-start | bytes 393224 | tf_op jit(solution)/shard_map/ppermute | solution.py:31
  155.7 19.5 %collective-permute-start.56 = (bf16[32,64,128]{2,1,0:T(8,128)(2,1)S(1)}, bf16[32,64,128]{2,1,0:T(8,128)(2,1)S(1)}, u32[]{:S(2)}, u32[]{:S(2)}) collective-permute-start(bf16[32,64,128]{2,1,0:T(8,128)(2,1)S(1)} %get-tuple-element.113), channel_id=1, source_target_pairs={{0,4},{4,0},{8,12},{12,8},{16,20},{20,16},{24,28},{28,24},{32,36},... | collective-permute-start | bytes 1572872 | tf_op jit(solution)/shard_map/ppermute | solution.py:31
  155.8 19.4 %collective-permute-start.57 = (bf16[32,64,128]{2,1,0:T(8,128)(2,1)S(1)}, bf16[32,64,128]{2,1,0:T(8,128)(2,1)S(1)}, u32[]{:S(2)}, u32[]{:S(2)}) collective-permute-start(bf16[32,64,128]{2,1,0:T(8,128)(2,1)S(1)} %get-tuple-element.114), channel_id=1, source_target_pairs={{4,8},{8,4},{12,16},{16,12},{20,24},{24,20},{28,32},{32,28},{36,40... | collective-permute-start | bytes 1572872 | tf_op jit(solution)/shard_map/ppermute | solution.py:47
  162.1 6.6 %collective-permute-start.47 = (bf16[8,64,128]{2,1,0:T(8,128)(2,1)S(1)}, bf16[8,64,128]{2,1,0:T(8,128)(2,1)S(1)}, u32[]{:S(2)}, u32[]{:S(2)}) collective-permute-start(bf16[8,64,128]{2,1,0:T(8,128)(2,1)S(1)} %get-tuple-element.99.refs_1_), channel_id=1, source_target_pairs={{0,2},{1,3},{2,0},{3,1},{4,6},{5,7},{6,4},{7,5},{8,10},{9,11},{10,... | collective-permute-start | bytes 393224 | tf_op jit(solution)/shard_map/ppermute | solution.py:31
  168.7 14.7 %collective-permute-start.50 = (bf16[16,64,128]{2,1,0:T(8,128)(2,1)S(1)}, bf16[16,64,128]{2,1,0:T(8,128)(2,1)S(1)}, u32[]{:S(2)}, u32[]{:S(2)}) collective-permute-start(bf16[16,64,128]{2,1,0:T(8,128)(2,1)S(1)} %shard_map.116), channel_id=1, source_target_pairs={{4,8},{8,4},{12,16},{16,12},{20,24},{24,20},{28,32},{32,28},{36,40... | collective-permute-start | bytes 786440 | tf_op jit(solution)/shard_map/ppermute | solution.py:47
  169.3 14.0 %collective-permute-start.49 = (bf16[16,64,128]{2,1,0:T(8,128)(2,1)S(1)}, bf16[16,64,128]{2,1,0:T(8,128)(2,1)S(1)}, u32[]{:S(2)}, u32[]{:S(2)}) collective-permute-start(bf16[16,64,128]{2,1,0:T(8,128)(2,1)S(1)} %shard_map.116), channel_id=1, source_target_pairs={{0,4},{4,0},{8,12},{12,8},{16,20},{20,16},{24,28},{28,24},{32,36},... | collective-permute-start | bytes 786440 | tf_op jit(solution)/shard_map/ppermute | solution.py:31
  175.5 9.5 %collective-permute-start.58 = (bf16[8,64,128]{2,1,0:T(8,128)(2,1)S(1)}, bf16[8,64,128]{2,1,0:T(8,128)(2,1)S(1)}, u32[]{:S(2)}, u32[]{:S(2)}) collective-permute-start(bf16[8,64,128]{2,1,0:T(8,128)(2,1)S(1)} %get-tuple-element.119), channel_id=1, source_target_pairs={{0,1},{1,0},{2,3},{3,2},{4,5},{5,4},{6,7},{7,6},{8,9},{9,8},{10,11... | collective-permute-start | bytes 393224 | tf_op jit(solution)/shard_map/ppermute | solution.py:31
  177.6 10.1 %collective-permute-start.59 = (bf16[8,64,128]{2,1,0:T(8,128)(2,1)S(1)}, bf16[8,64,128]{2,1,0:T(8,128)(2,1)S(1)}, u32[]{:S(2)}, u32[]{:S(2)}) collective-permute-start(bf16[8,64,128]{2,1,0:T(8,128)(2,1)S(1)} %get-tuple-element.120), channel_id=1, source_target_pairs={{0,2},{1,3},{2,0},{3,1},{4,6},{5,7},{6,4},{7,5},{8,10},{9,11},{10,... | collective-permute-start | bytes 393224 | tf_op jit(solution)/shard_map/ppermute | solution.py:31
  181.6 7.8 %collective-permute-start.60 = (bf16[8,64,128]{2,1,0:T(8,128)(2,1)S(1)}, bf16[8,64,128]{2,1,0:T(8,128)(2,1)S(1)}, u32[]{:S(2)}, u32[]{:S(2)}) collective-permute-start(bf16[8,64,128]{2,1,0:T(8,128)(2,1)S(1)} %get-tuple-element.121), channel_id=1, source_target_pairs={{0,3},{1,2},{2,1},{3,0},{4,7},{5,6},{6,5},{7,4},{8,11},{9,10},{10,... | collective-permute-start | bytes 393224 | tf_op jit(solution)/shard_map/ppermute | solution.py:31
  198.4 7.1 %collective-permute-start.67 = (f32[96,128]{1,0:T(8,128)S(1)}, f32[96,128]{1,0:T(8,128)S(1)}, u32[]{:S(2)}, u32[]{:S(2)}) collective-permute-start(f32[96,128]{1,0:T(8,128)S(1)} %add_add_fusion.2), channel_id=1, source_target_pairs={{0,24},{4,28},{8,16},{12,20},{16,8},{20,12},{24,0},{28,4},{32,56},... | collective-permute-start | bytes 147464 | tf_op jit(solution)/shard_map/ppermute | solution.py:31
  (45 other events, 344.4 us)
